TPU v7x, 256 devices: a whole 4x4x8 slice. The times are simulated.
256 devices in a mesh: seg: 32 (over x, z), tok: 8 (over y, core).
Axes of the slice: x: 4, y: 4, z: 8, core: 2. Of those that a mesh axis runs over, the one named last changes fastest.
Arguments:
- queries: bfloat16 [65536, 2048], P(('seg', 'tok')), may hold values from -40 to 40
- keys: bfloat16 [65536, 512], P(('seg', 'tok')), may hold values from -40 to 40
- values: bfloat16 [65536, 512], P(('seg', 'tok')), may hold values from -6 to 6
- gain_mem: float32 [2048], replicated, may hold values from 0.25 to 1.75
- gain_dot: float32 [2048], replicated, may hold values from 0.25 to 1.75
- out_weight: bfloat16 [2048, 2048], replicated, may hold values from -0.125 to 0.125
Outputs:
- layer_out: bfloat16 [65536, 2048], P(('seg', 'tok'))
All inputs are finite; a program needn't handle non-finite values.
Results may differ from a plain program's by a relative error of at most 0.008.
Values may be sent and summed in bfloat16 or wider, within the bound.
No kernel may reach another device: no remote copies, remote signals or barrier semaphores. Data moves between devices by JAX's collectives and lax.ppermute only.
A program may use at most 128 MiB of HBM per device.

v0:
```python
import jax
import jax.numpy as jnp
from jax import lax
from jax.sharding import Mesh
from jax.sharding import PartitionSpec as P

HEAD_DIMENSION = 128
SEG = ("seg_0", "seg_1")
SEG_TOK = ("seg_0", "seg_1", "tok")


def split_up(shard, dim, devices):
    before, after = (shard.shape[:dim], shard.shape[dim + 1 :])
    return jnp.moveaxis(shard.reshape(*before, devices, -1, *after), dim, 0)


def sum_at_owner(shard, axis, dim):
    devices = lax.axis_size(axis)
    blocks = lax.all_to_all(split_up(shard, dim, devices), axis, 0, 0, tiled=True)
    return jnp.sum(blocks.astype(jnp.float32), axis=0)


def filled_with(shard, identity):
    return jnp.zeros_like(shard) + jnp.asarray(identity, shard.dtype)


def prefix_by_axis(shard, axes, combine, identity):
    before = start = filled_with(shard, identity)
    running = shard
    for axis in reversed(axes):
        devices, mine = (lax.axis_size(axis), lax.axis_index(axis))
        pieces = lax.all_gather(running.astype(jnp.bfloat16), axis)
        inside, running = (start, start)
        for k in range(devices):
            passed = k < mine
            running = combine(running, pieces[k].astype(shard.dtype))
            inside = jnp.where(passed, running, inside)
        before = combine(inside, before)
    return before


def joined_along(blocks, dim):
    blocks = jnp.moveaxis(blocks, 0, dim)
    shape = blocks.shape
    return blocks.reshape(*shape[:dim], shape[dim] * shape[dim + 1], *shape[dim + 2 :])


def sent_to_all(shard, axis):
    copies = jnp.broadcast_to(shard, (lax.axis_size(axis), *shard.shape))
    return lax.all_to_all(copies, axis, split_axis=0, concat_axis=0, tiled=True)


def gathered_copies(shard, axis, dim):
    return joined_along(sent_to_all(shard, axis), dim)


def side_by_side(arrays, axis, dim, along):
    widths = [a.shape[along] for a in arrays]
    both = jnp.concatenate(arrays, axis=along)
    out = lax.all_gather(both, axis, axis=dim, tiled=True)
    return tuple(jnp.split(out, [sum(widths[:k]) for k in range(1, len(widths))], axis=along))


def feature_map(inputs):
    return jax.nn.elu(inputs) + 1.0


def head_norm(inputs, gain):
    return inputs * lax.rsqrt(jnp.mean(inputs * inputs, axis=-1, keepdims=True) + 1e-06) * gain


def add_terms(earlier_terms, later_terms):
    return earlier_terms + later_terms


def local(queries, keys, values, gain_mem, gain_dot, out_weight):
    row_count = queries.shape[0]
    head_size = HEAD_DIMENSION
    heads_query = queries.shape[1] // head_size
    heads_value = keys.shape[1] // head_size
    query_group_width = heads_query // heads_value
    scale = float(head_size) ** (-0.5)
    first_row = lax.axis_index("tok") * row_count
    query_block = queries.reshape(row_count, heads_value, query_group_width, head_size)
    query_positions = first_row + jnp.arange(row_count, dtype=jnp.int32)
    sig_keys = (
        feature_map(keys.astype(jnp.float32))
        .astype(jnp.bfloat16)
        .reshape(row_count, heads_value, head_size)
    )
    value_heads_own = values.reshape(row_count, heads_value, head_size)
    partial_value = jnp.einsum(
        "rgd,rge->gde", sig_keys, value_heads_own, preferred_element_type=jnp.float32
    )
    owned = sum_at_owner(partial_value.astype(jnp.bfloat16), "tok", 1)
    earlier = prefix_by_axis(owned, SEG, add_terms, jnp.zeros_like(owned))
    earlier = gathered_copies(earlier.astype(jnp.bfloat16), "tok", 1).astype(earlier.dtype)
    key_piece, value_piece = side_by_side((keys, values), "tok", 0, 1)
    piece_rows = key_piece.shape[0]
    key_heads = key_piece.reshape(piece_rows, heads_value, head_size)
    value_heads = value_piece.reshape(piece_rows, heads_value, head_size)
    key_positions = jnp.arange(piece_rows, dtype=jnp.int32)
    visible = query_positions[:, None] >= key_positions[None, :]
    scores = (
        jnp.einsum("rgjd,cgd->gjrc", query_block, key_heads, preferred_element_type=jnp.float32)
        * scale
    )
    scores = jnp.where(visible, scores, -1e30)
    running_max = jnp.full((heads_value, query_group_width, row_count, 1), -1e30, jnp.float32)
    new_max = jnp.maximum(running_max, jnp.max(scores, axis=-1, keepdims=True))
    weights = jnp.where(visible, jnp.exp(scores - new_max), 0.0)
    product = jnp.einsum(
        "gjrc,cgd->gjrd",
        weights.astype(jnp.bfloat16),
        value_heads,
        preferred_element_type=jnp.float32,
    )
    final_sum = jnp.sum(weights, axis=-1, keepdims=True)
    dot_part = jnp.transpose(product / final_sum, (2, 0, 1, 3)).reshape(
        row_count, heads_query, head_size
    )
    sig_queries = feature_map(query_block.astype(jnp.float32))
    memory_part = jnp.einsum(
        "rgjd,gde->rgje", sig_queries, earlier, precision=lax.Precision.HIGHEST
    )
    memory_part = memory_part.reshape(row_count, heads_query, head_size)
    gain_memory = gain_mem.reshape(heads_query, head_size)
    gain_attend = gain_dot.reshape(heads_query, head_size)
    mixed = (0.5 * (head_norm(memory_part, gain_memory) + head_norm(dot_part, gain_attend))).astype(
        jnp.bfloat16
    )
    mixed = mixed.reshape(row_count, heads_query * head_size)
    return jnp.dot(mixed, out_weight, preferred_element_type=jnp.float32).astype(jnp.bfloat16)


def solution(mesh):
    finer = Mesh(mesh.devices.reshape(4, 8, mesh.shape["tok"]), ("seg_0", "seg_1", "tok"))
    in_specs = (P(SEG_TOK, None), P(SEG_TOK, None), P(SEG_TOK, None), P(), P(), P())
    out_specs = P(SEG_TOK, None)
    return jax.shard_map(local, mesh=finer, in_specs=in_specs, out_specs=out_specs, check_vma=False)
```

profile of v0, /device:TPU:1, one launch (start us, length us, event | category | flops | bytes accessed | tf_op | source)
XLA Modules:
  0.0 139.0 jit_solution(16360745656923667339)
XLA Ops:
  6.5 0.0 copy-start.2
  6.5 0.0 copy-start.3
  6.5 0.0 all-gather.3.cloned.1.call-start
  6.5 1.1 copy.28
  7.7 1.1 copy.29
  8.8 0.8 pad_maximum_fusion
  9.6 0.0 all-gather.3.cloned.1.call-update
  9.6 0.0 copy-done.2
  9.7 0.0 copy-start.1
  9.7 0.2 fusion.25
  9.9 0.1 copy.37
  10.0 0.0 copy-done.3
  10.1 0.2 convolution_convert_fusion.1
  10.3 0.7 copy.58
  10.9 6.5 %all-to-all-start = ((bf16[8,4,16,128]{3,2,1,0:T(8,128)(2,1)}), bf16[8,4,16,128]{3,2,1,0:T(8,128)(2,1)S(1)}, u32[]{:S(2)}, u32[]{:S(2)}) async-start(bf16[8,4,16,128]{3,2,1,0:T(8,128)(2,1)} %bitcast.105), calls=%async_computation | async-start | bytes 262144 | tf_op jit(solution)/shard_map/all_to_all | solution.py:19
  17.4 5.3 %all-to-all-done = bf16[8,4,16,128]{3,2,1,0:T(8,128)(2,1)S(1)} async-done(((bf16[8,4,16,128]{3,2,1,0:T(8,128)(2,1)}), bf16[8,4,16,128]{3,2,1,0:T(8,128)(2,1)S(1)}, u32[]{:S(2)}, u32[]{:S(2)}) %all-to-all-start) | async-done | bytes 131104 | tf_op jit(solution)/shard_map/all_to_all | solution.py:19
  22.7 22.9 %all-gather = bf16[32,16,128]{2,1,0:T(8,128)(2,1)S(1)} all-gather(bf16[4,16,128]{2,1,0:T(8,128)(2,1)S(1)} %reduce_sum.39), channel_id=2, replica_groups=mesh['seg_0'=4,'seg_1'=8,'tok'=8] {'seg_1'}, dimensions={0}, use_global_device_ids=true | all-gather | bytes 147456 | tf_op jit(solution)/shard_map/all_gather | solution.py:32
  45.6 9.9 %all_gather.15 = bf16[4,4,16,128]{3,2,1,0:T(8,128)(2,1)S(1)} all-gather(bf16[1,4,16,128]{3,2,1,0:T(8,128)(2,1)S(1)} %fusion.41), channel_id=1, replica_groups=mesh['seg_0'=4,'seg_1'=8,'tok'=8] {'seg_0'}, dimensions={0}, use_global_device_ids=true | all-gather | bytes 81920 | tf_op jit(solution)/shard_map/all_gather | solution.py:32
  55.6 0.7 broadcast_in_dim.34
  56.2 11.2 %all-to-all-start.1 = ((bf16[8,4,16,128]{3,2,1,0:T(8,128)(2,1)}), bf16[8,4,16,128]{3,2,1,0:T(8,128)(2,1)S(1)}, u32[]{:S(2)}, u32[]{:S(2)}) async-start(bf16[8,4,16,128]{3,2,1,0:T(8,128)(2,1)} %broadcast_in_dim.34), calls=%async_computation.1 | async-start | bytes 262144 | tf_op jit(solution)/shard_map/all_to_all | solution.py:50
  67.4 0.3 iota_compare_fusion
  67.8 0.0 copy-done.1
  67.8 0.8 reshape.121
  68.6 4.1 %all-to-all-done.1 = bf16[8,4,16,128]{3,2,1,0:T(8,128)(2,1)S(1)} async-done(((bf16[8,4,16,128]{3,2,1,0:T(8,128)(2,1)}), bf16[8,4,16,128]{3,2,1,0:T(8,128)(2,1)S(1)}, u32[]{:S(2)}, u32[]{:S(2)}) %all-to-all-start.1) | async-done | bytes 131104 | tf_op jit(solution)/shard_map/all_to_all | solution.py:50
  72.7 3.4 %fusion.15 = (f32[256,4,4]{0,2,1:T(4,128)S(1)}, f32[4,128,256,4]{2,1,3,0:T(8,128)}) fusion(bf16[4,128,128,1]{2,1,3,0:T(8,128)(2,1)S(1)} %bitcast.110, bf16[256,4,4,128]{3,2,1,0:T(4,128)(2,1)S(1)} %reshape.121), kind=kOutput, calls=%fused_computation.22 | convolution fusion | flops 808972288 | bytes 3293184 | tf_op jit(solution)/shard_map/rgjd,gde->rgje/dot_general | solution.py:123
  76.2 0.0 all-gather.3.cloned.1.call-done
  76.2 2.5 %fusion.48 = (bf16[2048,512]{0,1:T(8,128)(2,1)S(1)}, bf16[2048,512]{0,1:T(8,128)(2,1)S(1)}) fusion(bf16[2048,1024]{0,1:T(8,128)(2,1)} %all-gather.3.cloned.1.call-done), kind=kLoop, calls=%fused_computation.75 | loop fusion | bytes 8388608 | tf_op jit(solution)/shard_map/split | solution.py:61
  78.8 13.9 %fusion = (f32[4,4,256]{2,1,0:T(4,128)S(1)}, f32[4,2048,256,4]{2,1,3,0:T(8,128)}) fusion(pred[256,2048]{0,1:T(8,128)(4,1)S(1)} %iota_compare_fusion, bf16[2048,4,128,1]{0,2,3,1:T(8,128)(2,1)S(1)} %bitcast.106, bf16[256,4,4,128]{3,2,1,0:T(4,128)(2,1)S(1)} %reshape.121), kind=kOutput, calls=%fused_computation.2 | convolution fusion | flops 2172645376 | bytes 37240832 | tf_op jit(solution)/shard_map/rgjd,cgd->gjrc/dot_general | solution.py:105
  92.7 14.9 %fusion.1 = f32[4,4,256]{2,1,0:T(4,128)S(1)} fusion(f32[4,2048,256,4]{2,1,3,0:T(8,128)} %get-tuple-element.8, f32[4,4,256]{2,1,0:T(4,128)S(1)} %broadcast_maximum_fusion, pred[256,2048]{0,1:T(8,128)(4,1)S(1)} %iota_compare_fusion), kind=kLoop, calls=%fused_computation.3 | loop fusion | flops 41938944 | bytes 34111488 | tf_op jit(solution)/shard_map/reduce_sum | solution.py:118
  107.6 0.0 copy-start
  107.6 0.0 copy-start.4
  107.6 0.0 copy-start.5
  107.6 15.7 %multiply_reduce_fusion = (f32[256,4,4]{0,2,1:T(4,128)S(1)}, f32[256,4,4,128]{0,3,2,1:T(8,128)}) fusion(f32[256,4,4]{0,2,1:T(4,128)S(1)} %bitcast.111, bf16[2048,4,128,1]{0,2,3,1:T(8,128)(2,1)S(1)} %bitcast.107, f32[4,2048,256,4]{2,1,3,0:T(8,128)} %get-tuple-element.8, f32[4,4,256]{2,1,0:T(4,128)S(1)} %broadcast_maximum_fusion, ...), kind=kOutput, calls=%fused_computation.23 | convolution fusion | flops 2190995456 | bytes 38322176 | tf_op jit(solution)/shard_map/gjrc,cgd->gjrd/dot_general | solution.py:112
  123.3 0.0 copy-done
  123.4 0.0 copy-done.4
  123.4 0.0 copy-done.5
  123.4 2.0 %fusion.13 = bf16[256,2048]{0,1:T(8,128)(2,1)S(1)} fusion(f32[4,128,256,4]{2,1,3,0:T(8,128)S(1)} %copy-done, f32[256,4,4,128]{0,3,2,1:T(8,128)} %get-tuple-element.10, f32[2048]{0:T(1024)S(1)} %copy-done.4, f32[256,16]{0,1:T(8,128)S(1)} %rsqrt.25, f32[2048]{0:T(1024)S(1)} %copy-done.5, f32[256,16]{0,1:T(8,128)S(1)} %rsqrt.23), kind=kLoop, calls=%fused_computation.17 | loop fusion | flops 3670016 | bytes 5292032 | tf_op jit(solution)/shard_map/convert_element_type | solution.py:129
  125.4 6.7 %convolution_convert_fusion = bf16[256,2048]{1,0:T(8,128)(2,1)} fusion(bf16[256,2048]{0,1:T(8,128)(2,1)S(1)} %fusion.13, bf16[2048,2048]{1,0:T(8,128)(2,1)} %param.11), kind=kOutput, calls=%fused_computation.9 | convolution fusion | flops 2148007936 | bytes 10485760 | tf_op jit(solution)/shard_map/dot_general | solution.py:133
  (10 shorter events, 0.2 us)
Async XLA Ops:
  6.5 3.1 %copy-start.2 = (bf16[256,512]{1,0:T(8,128)(2,1)S(1)}, bf16[256,512]{1,0:T(8,128)(2,1)}, u32[]{:S(2)}) copy-start(bf16[256,512]{1,0:T(8,128)(2,1)} %param.7) | copy-start | bytes 786436
  6.5 3.5 %copy-start.3 = (bf16[256,512]{1,0:T(8,128)(2,1)S(1)}, bf16[256,512]{1,0:T(8,128)(2,1)}, u32[]{:S(2)}) copy-start(bf16[256,512]{1,0:T(8,128)(2,1)} %param.8) | copy-start | bytes 786436
  6.5 69.7 %all-gather.3.cloned.1.call-start = ((), (), s32[]{:S(2)}) async-start(), calls=%async_computation.2 | async-start | bytes 4718592 | tf_op jit(solution)/shard_map/all_gather | solution.py:60
  9.7 58.1 %copy-start.1 = (bf16[256,2048]{1,0:T(8,128)(2,1)S(1)}, bf16[256,2048]{1,0:T(8,128)(2,1)}, u32[]{:S(2)}) copy-start(bf16[256,2048]{1,0:T(8,128)(2,1)} %param.6) | copy-start | bytes 3145732
  10.9 11.7 %all-to-all-start = ((bf16[8,4,16,128]{3,2,1,0:T(8,128)(2,1)}), bf16[8,4,16,128]{3,2,1,0:T(8,128)(2,1)S(1)}, u32[]{:S(2)}, u32[]{:S(2)}) async-start(bf16[8,4,16,128]{3,2,1,0:T(8,128)(2,1)} %bitcast.105), calls=%async_computation | async-start | bytes 262144 | tf_op jit(solution)/shard_map/all_to_all | solution.py:19
  56.2 16.5 %all-to-all-start.1 = ((bf16[8,4,16,128]{3,2,1,0:T(8,128)(2,1)}), bf16[8,4,16,128]{3,2,1,0:T(8,128)(2,1)S(1)}, u32[]{:S(2)}, u32[]{:S(2)}) async-start(bf16[8,4,16,128]{3,2,1,0:T(8,128)(2,1)} %broadcast_in_dim.34), calls=%async_computation.1 | async-start | bytes 262144 | tf_op jit(solution)/shard_map/all_to_all | solution.py:50
  107.6 15.8 %copy-start = (f32[4,128,256,4]{2,1,3,0:T(8,128)S(1)}, f32[4,128,256,4]{2,1,3,0:T(8,128)}, u32[]{:S(2)}) copy-start(f32[4,128,256,4]{2,1,3,0:T(8,128)} %get-tuple-element.12) | copy-start | bytes 6291460
  107.6 15.8 %copy-start.4 = (f32[2048]{0:T(1024)S(1)}, f32[2048]{0:T(1024)}, u32[]{:S(2)}) copy-start(f32[2048]{0:T(1024)} %param.10) | copy-start | bytes 24580
  107.6 15.8 %copy-start.5 = (f32[2048]{0:T(1024)S(1)}, f32[2048]{0:T(1024)}, u32[]{:S(2)}) copy-start(f32[2048]{0:T(1024)} %param.9) | copy-start | bytes 24580
Sparse Core Ops, SparseCore 0:
  9.8 42.2 all-gather.2
where the time goes:
time: 140 us; the launch traced here: 139 us
  matrix products  40 us (29%)
  blocking collectives  32.8 us (23%)
  other arithmetic  18.5 us (13%)
  starting transfers between devices  17.7 us (13%)
  between operations  13.6 us (10%)
  waiting for transfers between devices  9.44 us (7%)
  local copies, waits for them, and re-layouts  7.03 us (5%)
    all_gather x2, blocking collectives, prefix_by_axis(): pieces = lax.all_gather(running.astype(jnp.bfloat16), axis)  32.8 us
    dot_general x1, matrix products, local(): jnp.einsum('gjrc,cgd->gjrd', weights.astype(jnp.bfloat16), value_heads, p...  15.7 us
    reduce_sum x1, other arithmetic, local(): final_sum = jnp.sum(weights, axis=-1, keepdims=True)  14.9 us
    dot_general x1, matrix products, local(): jnp.einsum('rgjd,cgd->gjrc', query_block, key_heads, preferred_element_ty...  13.9 us
    all_to_all x1, starting transfers between devices, sent_to_all(): return lax.all_to_all(copies, axis, split_axis=0, concat_axis=0, tiled=True)  11.2 us
    dot_general x1, matrix products, local(): jnp.dot(mixed, out_weight, preferred_element_type=jnp.float32)  6.72 us
    all_to_all x1, starting transfers between devices, sum_at_owner(): lax.all_to_all(split_up(shard, dim, devices), axis, 0, 0, tiled=True)  6.47 us
    all_to_all x1, waiting for transfers between devices, sum_at_owner(): lax.all_to_all(split_up(shard, dim, devices), axis, 0, 0, tiled=True)  5.26 us
  transfers between devices with their start and end apart: 3, of which 2 were waited for; matrix products, arithmetic and copies ran while one was open for 5% of the time, Pallas kernels for 0%

commit v1 on v0

v1 whole, which is shorter than its diff:
```python
import functools

import jax
import jax.numpy as jnp
from jax import lax
from jax.experimental import pallas as pl
from jax.experimental.pallas import tpu as pltpu
from jax.sharding import Mesh
from jax.sharding import PartitionSpec as P


HEAD = 128
GROUP = 4
HEADS = 8
AXES = ("sx", "sz", "y", "c")
EXP_SCALE = float(HEAD) ** (-0.5) * 1.4426950408889634
NT = (((1,), (1,)), ((), ()))
TN = (((0,), (0,)), ((), ()))
BF16 = jnp.bfloat16
F32 = jnp.float32
VM = pl.BlockSpec(memory_space=pltpu.VMEM)
HBM = pl.BlockSpec(memory_space=pltpu.HBM)


def placed(x, space=pltpu.VMEM):
    return pltpu.with_memory_space_constraint(x, space)


def kernel_call(body, outs, args, limit, flops=0, nbytes=0, trans=0, specs=None, **more):
    specs = specs or [VM] * len(args)
    args = [placed(a, s.memory_space) for a, s in zip(args, specs)]
    return pl.pallas_call(
        body,
        out_shape=[pltpu.VMEM(shape, dtype) for shape, dtype in outs],
        in_specs=specs,
        out_specs=[VM] * len(outs),
        compiler_params=pltpu.CompilerParams(vmem_limit_bytes=limit * 2**20),
        cost_estimate=pl.CostEstimate(flops=flops, bytes_accessed=nbytes, transcendentals=trans),
        **more,
    )(*args)


def feature_map(x):
    return jnp.where(x > 0, x + 1.0, jnp.exp(jnp.minimum(x, 0.0)))


def prep_kv_kernel(k, v, keep, send, sems):
    half = k.shape[1] // 2
    c = lax.axis_index("c")
    copies = []
    for n, (out, who) in enumerate(((send, 1 - c), (keep, c))):
        cols = pl.ds(pl.multiple_of(who * half, half), half)
        for i, src in enumerate((k, v)):
            dst = out.at[:, i * half : (i + 1) * half]
            copies.append(pltpu.make_async_copy(src.at[:, cols], dst, sems.at[2 * n + i]))
    for copy in copies:
        copy.start()
    for copy in copies:
        copy.wait()


def prep_kv(k, v):
    outs = [(k.shape, BF16)] * 2
    return kernel_call(
        prep_kv_kernel, outs, (k, v), 8, nbytes=2**20, specs=[HBM, HBM],
        scratch_shapes=[pltpu.SemaphoreType.DMA((4,))],
    )


def prep_q_kernel(q, keep, send, sems):
    half = q.shape[1] // 2
    c = lax.axis_index("c")
    copies = []
    for n, (out, who) in enumerate(((send, 1 - c), (keep, c))):
        cols = pl.ds(pl.multiple_of(who * half, half), half)
        copies.append(pltpu.make_async_copy(q.at[:, cols], out, sems.at[n]))
    for copy in copies:
        copy.start()
    for copy in copies:
        copy.wait()


def prep_q(q):
    outs = [((q.shape[0], q.shape[1] // 2), BF16)] * 2
    return kernel_call(
        prep_q_kernel, outs, (q,), 8, nbytes=2**21, specs=[HBM],
        scratch_shapes=[pltpu.SemaphoreType.DMA((2,))],
    )


def part_kernel(keep, recv, both, total, sent):
    rows, cols = keep.shape
    mine = lax.axis_index("c") * rows
    other = rows - mine
    both[pl.ds(pl.multiple_of(mine, rows), rows), :] = keep[...]
    both[pl.ds(pl.multiple_of(other, rows), rows), :] = recv[...]
    for g in range(2):
        kk = slice(g * HEAD, (g + 1) * HEAD)
        vv = slice(cols // 2 + g * HEAD, cols // 2 + (g + 1) * HEAD)
        acc = None
        for ref in (keep, recv):
            sig = feature_map(ref[:, kk].astype(F32)).astype(BF16)
            term = lax.dot_general(sig, ref[:, vv], TN, preferred_element_type=F32)
            acc = term if acc is None else acc + term
        total[kk, :] = acc
        sent[kk, :] = acc.astype(BF16)


def part(keep, recv):
    rows, cols = keep.shape
    outs = [((2 * rows, cols), BF16), ((cols // 2, HEAD), F32), ((cols // 2, HEAD), BF16)]
    return kernel_call(part_kernel, outs, (keep, recv), 8, 2**26, 2**21)


def tiles():
    for g in range(2):
        for b in range(2):
            for j in range(GROUP):
                h = g * GROUP + j
                yield g, b, h, slice(h * HEAD, (h + 1) * HEAD), slice(2 * h * HEAD, 2 * (h + 1) * HEAD)


def fill_ones(kv, v_ones):
    for g in range(2):
        v = kv[:, (2 + g) * HEAD : (3 + g) * HEAD]
        v_ones[g] = jnp.concatenate([v, jnp.ones_like(v)], axis=1)


def weigh(s, m, v_ones):
    w = jnp.exp2(s * EXP_SCALE - m * EXP_SCALE).astype(BF16)
    return jnp.dot(w, v_ones, preferred_element_type=F32)


def first_kernel(q_keep, q_recv, kv, ext, top, v_ones):
    rows, keys = q_keep.shape[0], kv.shape[0]
    fill_ones(kv, v_ones)
    c = lax.axis_index("c")
    for g, b, h, cols, wide in tiles():
        q = (q_keep, q_recv)[b]
        first = (c if b == 0 else 1 - c) * rows
        row = lax.broadcasted_iota(jnp.int32, (rows, keys), 0) + first
        mask = row >= lax.broadcasted_iota(jnp.int32, (rows, keys), 1)
        s = lax.dot_general(
            q[:, cols], kv[:, g * HEAD : (g + 1) * HEAD], NT, preferred_element_type=F32
        )
        s = jnp.where(mask, s, -1e30)
        m = jnp.max(s, axis=-1, keepdims=True)
        ext[b, :, wide] = weigh(s, m, v_ones[g])
        top[b, :, cols] = jnp.broadcast_to(m, (rows, HEAD))


def state(rows):
    return [((2, rows, 2 * HEADS * HEAD), F32), ((2, rows, HEADS * HEAD), F32)]


def attend_first(q_keep, q_recv, kv):
    rows, keys = q_keep.shape[0], kv.shape[0]
    scores = 2 * HEADS * rows * keys
    return kernel_call(
        first_kernel, state(rows), (q_keep, q_recv, kv), 20,
        4 * scores * HEAD, 2**22, scores,
        scratch_shapes=[pltpu.VMEM((2, keys, 2 * HEAD), BF16)],
    )


def fold_chunk(q_refs, kv, v_ones, ext, top):
    keys = kv.shape[0]
    fill_ones(kv, v_ones)
    for g, b, h, cols, wide in tiles():
        s = lax.dot_general(
            q_refs[b][:, cols], kv[:, g * HEAD : (g + 1) * HEAD], NT, preferred_element_type=F32
        )
        old = top[b, :, cols]
        new = jnp.maximum(old, jnp.max(s, axis=-1, keepdims=True))
        floor = new * EXP_SCALE
        w = [
            jnp.exp2(s[:, n : n + HEAD] * EXP_SCALE - floor).astype(BF16)
            for n in range(0, keys, HEAD)
        ]
        out = jnp.dot(jnp.concatenate(w, axis=1), v_ones[g], preferred_element_type=F32)
        alpha = jnp.exp2(old * EXP_SCALE - floor)
        yield b, h, cols, wide, new, ext[b, :, wide] * jnp.concatenate([alpha, alpha], axis=1) + out


def next_kernel(q_keep, q_recv, left, right, ext_in, top_in, ext, top, v_ones):
    y = lax.axis_index("y")

    def fold(kv, source):
        for b, h, cols, wide, new, total in fold_chunk((q_keep, q_recv), kv, v_ones, *source):
            ext[b, :, wide] = total
            top[b, :, cols] = new

    pl.when(y >= 1)(lambda: fold(left, (ext, top)))
    pl.when(y == 3)(lambda: fold(right, (ext, top)))


def attend_next(q_keep, q_recv, left, right, ext, top):
    rows, keys = q_keep.shape[0], left.shape[0]
    scores = 2 * HEADS * rows * keys * 2
    return kernel_call(
        next_kernel, state(rows), (q_keep, q_recv, left, right, ext, top), 20,
        4 * scores * HEAD, 2**22, scores,
        scratch_shapes=[pltpu.VMEM((2, keys, 2 * HEAD), BF16)],
        input_output_aliases={4: 0, 5: 1},
    )


def head_norm(x, gain):
    return x * (0.5 * lax.rsqrt(jnp.mean(x * x, axis=-1, keepdims=True) + 1e-06)) * gain


def last_kernel(q_keep, q_recv, kv, ext, top, gain, out, v_ones):
    y, c = lax.axis_index("y"), lax.axis_index("c")
    own = pl.multiple_of(c * HEADS, HEADS)

    def put(b, h, cols, total):
        acc, den = total[:, :HEAD], total[:, HEAD:]
        square = jnp.mean(acc * acc + 1e-06 * (den * den), axis=-1, keepdims=True)
        out[b, :, cols] = acc * (0.5 * lax.rsqrt(square)) * gain[pl.ds(own + h, 1), :]

    @pl.when(y >= 2)
    def _():
        for b, h, cols, wide, new, total in fold_chunk((q_keep, q_recv), kv, v_ones, ext, top):
            put(b, h, cols, total)

    @pl.when(y < 2)
    def _():
        for g, b, h, cols, wide in tiles():
            put(b, h, cols, ext[b, :, wide])


def attend_last(q_keep, q_recv, far, ext, top, gain):
    rows, keys = q_keep.shape[0], far.shape[0]
    scores = 2 * HEADS * rows * keys
    outs = [((2, rows, HEADS * HEAD), F32)]
    return kernel_call(
        last_kernel, outs, (q_keep, q_recv, far, ext, top, gain), 20,
        4 * scores * HEAD, 2**22, scores,
        scratch_shapes=[pltpu.VMEM((2, keys, 2 * HEAD), BF16)],
    )[0]


def mix_kernel(q_keep, q_recv, dot, m0, m1, m2, m3, gain, keep, send):
    own = pl.multiple_of(lax.axis_index("c") * HEADS, HEADS)
    memory = (m0[...].astype(F32) + m1[...].astype(F32)) + (m2[...].astype(F32) + m3[...].astype(F32))
    memory = memory.astype(BF16)
    for g, b, h, cols, wide in tiles():
        q, out = ((q_keep, keep), (q_recv, send))[b]
        sig = feature_map(q[:, cols].astype(F32)).astype(BF16)
        read = jnp.dot(sig, memory[g * HEAD : (g + 1) * HEAD], preferred_element_type=F32)
        mixed = head_norm(read, gain[pl.ds(own + h, 1), :]) + dot[b, :, cols]
        out[:, cols] = mixed.astype(BF16)


def mix(q_keep, q_recv, dot, memory, gain):
    outs = [(q_keep.shape, BF16)] * 2
    args = (q_keep, q_recv, dot, *memory, gain)
    return kernel_call(mix_kernel, outs, args, 16, 2**27, 2**22)


def project_first_kernel(x, weight, out):
    half = x.shape[1]
    own = pl.multiple_of(lax.axis_index("c") * half, half)
    for n in range(0, weight.shape[1], 512):
        out[:, n : n + 512] = jnp.dot(
            x[...], weight[pl.ds(own, half), n : n + 512], preferred_element_type=F32
        )


def project_first(x, weight):
    outs = [((x.shape[0], weight.shape[1]), F32)]
    return kernel_call(project_first_kernel, outs, (x, weight), 16, 2**30, 2**23)[0]


def project_last_kernel(x, begun, weight, out):
    half = x.shape[1]
    other = pl.multiple_of(half - lax.axis_index("c") * half, half)
    n = pl.ds(pl.multiple_of(pl.program_id(0) * 512, 512), 512)
    total = begun[:, n] + jnp.dot(x[...], weight[pl.ds(other, half), n], preferred_element_type=F32)
    out[...] = total.astype(BF16)


def project_last(x, begun, weight):
    rows, width = begun.shape
    args = [placed(a) for a in (x, begun, weight)]
    return pl.pallas_call(
        project_last_kernel,
        grid=(width // 512,),
        out_shape=jax.ShapeDtypeStruct((rows, width), BF16),
        in_specs=[VM] * 3,
        out_specs=pl.BlockSpec((rows, 512), lambda n: (0, n)),
        name="project_last",
        compiler_params=pltpu.CompilerParams(vmem_limit_bytes=16 * 2**20),
        cost_estimate=pl.CostEstimate(flops=2**30, bytes_accessed=2**23, transcendentals=0),
    )(*args)


def permute(x, axis, partner):
    return lax.ppermute(x, axis, list(enumerate(partner)))


def shift(x, axis, step, size):
    return permute(x, axis, [(i + step) % size for i in range(size)])


def add_z_kernel(level, total, before, got, total_out, before_out, sent):
    upper = ((lax.axis_index("sz") >> level) & 1).astype(F32)
    term = got[...].astype(F32)
    before_out[...] = before[...] + term * upper
    total_out[...] = total[...] + term
    sent[...] = total_out[...].astype(BF16)


def add_x_kernel(before, x1, x2, x3, mine):
    x = lax.axis_index("sx")
    total = before[...]
    for step, ref in ((1, x1), (2, x2), (3, x3)):
        total = total + ref[...].astype(F32) * (x >= step).astype(F32)
    mine[...] = total.astype(BF16)


def earlier_memory(total, sent):
    before = jnp.zeros_like(total)
    pairs = ([i ^ 1 for i in range(8)], [i ^ 2 for i in range(8)], [7 - i for i in range(8)])
    outs = [(total.shape, F32), (total.shape, F32), (total.shape, BF16)]
    for level, partner in enumerate(pairs):
        got = permute(sent, "sz", partner)
        total, before, sent = kernel_call(
            functools.partial(add_z_kernel, level), outs, (total, before, got),
            4, 2**17, 2**18,
        )
    got = [shift(sent, "sx", step, 4) for step in (1, 2, 3)]
    return kernel_call(add_x_kernel, outs[2:], (before, *got), 4, 2**17, 2**18)[0]


def layer(queries, keys, values, gain_mem, gain_dot, out_weight):
    kv_keep, kv_send = prep_kv(keys, values)
    kv_recv = permute(kv_send, "c", (1, 0))
    q_keep, q_send = prep_q(queries)
    q_recv = permute(q_send, "c", (1, 0))
    kv, total, sent = part(kv_keep, kv_recv)
    left = shift(kv, "y", 1, 4)
    right = shift(kv, "y", 3, 4)
    far = shift(kv, "y", 2, 4)
    mine = earlier_memory(total, sent)
    memory = [mine] + [shift(mine, "y", step, 4) for step in (1, 2, 3)]
    ext, top = attend_first(q_keep, q_recv, kv)
    ext, top = attend_next(q_keep, q_recv, left, right, ext, top)
    gain_dot = gain_dot.reshape(2 * HEADS, HEAD)
    gain_mem = gain_mem.reshape(2 * HEADS, HEAD)
    dot = attend_last(q_keep, q_recv, far, ext, top, gain_dot)
    mixed_keep, mixed_send = mix(q_keep, q_recv, dot, memory, gain_mem)
    begun = project_first(mixed_keep, out_weight)
    mixed_recv = permute(mixed_send, "c", (1, 0))
    return project_last(mixed_recv, begun, out_weight)


def solution(mesh):
    finer = Mesh(mesh.devices.reshape(4, 8, 4, 2), AXES)
    in_specs = (P(AXES, None), P(AXES, None), P(AXES, None), P(), P(), P())
    return jax.shard_map(
        layer, mesh=finer, in_specs=in_specs, out_specs=P(AXES, None), check_vma=False
    )
```

time: 140 us -> 65.3 us (0.47)
  the two profiles are of different devices: /device:TPU:1 before, /device:TPU:25 now
where the time goes in v1:
time: 65.3 us; the launch traced here: 65.1 us
  starting transfers between devices  27.6 us (42%)
  Pallas kernels  22.7 us (35%)
  waiting for transfers between devices  14.6 us (22%)
    ppermute x15, starting transfers between devices, permute(): return lax.ppermute(x, axis, list(enumerate(partner)))  27.6 us
    pallas_call x12, Pallas kernels, kernel_call(): pl.pallas_call(body, out_shape=[pltpu.VMEM(shape, dtype) for shape, dtype...  20 us
    ppermute x15, waiting for transfers between devices, permute(): return lax.ppermute(x, axis, list(enumerate(partner)))  14.6 us
    pallas_call x1, Pallas kernels, project_last(): pl.pallas_call(project_last_kernel, grid=(width // 512,), out_shape=jax.S...  2.75 us
  transfers between devices with their start and end apart: 15, of which 7 were waited for; matrix products, arithmetic and copies ran while one was open for 0% of the time, Pallas kernels for 27%

profile of v1, /device:TPU:25, one launch (start us, length us, event | category | flops | bytes accessed | tf_op | source)
XLA Modules:
  0.0 65.1 jit_solution(2041002970778686664)
XLA Ops:
  0.0 1.1 %shard_map.65 = (bf16[256,512]{1,0:T(8,128)(2,1)S(1)}, bf16[256,512]{1,0:T(8,128)(2,1)S(1)}) custom-call(bf16[256,512]{1,0:T(8,128)(2,1)} %k.1, bf16[256,512]{1,0:T(8,128)(2,1)} %v.1), custom_call_target="tpu_custom_call" | custom-call | bytes 1048576 | tf_op jit(solution)/shard_map/pallas_call | solution.py:32
  1.1 0.8 %collective-permute-start.1 = (bf16[256,512]{1,0:T(8,128)(2,1)S(1)}, bf16[256,512]{1,0:T(8,128)(2,1)S(1)}, u32[]{:S(2)}, u32[]{:S(2)}) collective-permute-start(bf16[256,512]{1,0:T(8,128)(2,1)S(1)} %get-tuple-element.29), channel_id=1, source_target_pairs={{0,1},{1,0},{2,3},{3,2},{4,5},{5,4},{6,7},{7,6},{8,9},{9,8},{10,11... | collective-permute-start | bytes 786440 | tf_op jit(solution)/shard_map/ppermute | solution.py:299
  1.9 1.2 %shard_map.64 = (bf16[256,1024]{1,0:T(8,128)(2,1)S(1)}, bf16[256,1024]{1,0:T(8,128)(2,1)S(1)}) custom-call(bf16[256,2048]{1,0:T(8,128)(2,1)} %q.1), custom_call_target="tpu_custom_call" | custom-call | bytes 2097152 | tf_op jit(solution)/shard_map/pallas_call | solution.py:32
  3.1 0.1 collective-permute-start
  3.2 0.0 collective-permute-done.1.recv
  3.2 0.3 shard_map.66
  3.6 1.7 %collective-permute-start.3 = (bf16[512,512]{1,0:T(8,128)(2,1)S(1)}, bf16[512,512]{1,0:T(8,128)(2,1)S(1)}, u32[]{:S(2)}, u32[]{:S(2)}) collective-permute-start(bf16[512,512]{1,0:T(8,128)(2,1)S(1)} %get-tuple-element.30.kv), channel_id=1, source_target_pairs={{0,2},{2,4},{4,6},{6,0},{1,3},{3,5},{5,7},{7,1},{8,10},{10,12},{12... | collective-permute-start | bytes 1572872 | tf_op jit(solution)/shard_map/ppermute | solution.py:299
  5.3 0.0 collective-permute-start.4
  5.3 1.5 %collective-permute-start.5 = (bf16[256,128]{1,0:T(8,128)(2,1)S(1)}, bf16[256,128]{1,0:T(8,128)(2,1)S(1)}, u32[]{:S(2)}, u32[]{:S(2)}) collective-permute-start(bf16[256,128]{1,0:T(8,128)(2,1)S(1)} %get-tuple-element.36), channel_id=1, source_target_pairs={{0,8},{8,0},{16,24},{24,16},{32,40},{40,32},{48,56},{56,48},{1,9},... | collective-permute-start | bytes 196616 | tf_op jit(solution)/shard_map/ppermute | solution.py:299
  6.8 2.0 %collective-permute-done.5.got = bf16[256,128]{1,0:T(8,128)(2,1)S(1)} collective-permute-done((bf16[256,128]{1,0:T(8,128)(2,1)S(1)}, bf16[256,128]{1,0:T(8,128)(2,1)S(1)}, u32[]{:S(2)}, u32[]{:S(2)}) %collective-permute-start.5) | collective-permute-done | bytes 65568 | tf_op jit(solution)/shard_map/ppermute | solution.py:299
  8.8 3.1 %collective-permute-start.6 = (bf16[256,128]{1,0:T(8,128)(2,1)S(1)}, bf16[256,128]{1,0:T(8,128)(2,1)S(1)}, u32[]{:S(2)}, u32[]{:S(2)}) collective-permute-start(bf16[256,128]{1,0:T(8,128)(2,1)S(1)} %get-tuple-element.39), channel_id=1, source_target_pairs={{0,16},{8,24},{16,0},{24,8},{32,48},{40,56},{48,32},{56,40},{1,17}... | collective-permute-start | bytes 196616 | tf_op jit(solution)/shard_map/ppermute | solution.py:299
  11.9 2.0 %collective-permute-done.6.got = bf16[256,128]{1,0:T(8,128)(2,1)S(1)} collective-permute-done((bf16[256,128]{1,0:T(8,128)(2,1)S(1)}, bf16[256,128]{1,0:T(8,128)(2,1)S(1)}, u32[]{:S(2)}, u32[]{:S(2)}) %collective-permute-start.6) | collective-permute-done | bytes 65568 | tf_op jit(solution)/shard_map/ppermute | solution.py:299
  13.8 5.6 %collective-permute-start.7 = (bf16[256,128]{1,0:T(8,128)(2,1)S(1)}, bf16[256,128]{1,0:T(8,128)(2,1)S(1)}, u32[]{:S(2)}, u32[]{:S(2)}) collective-permute-start(bf16[256,128]{1,0:T(8,128)(2,1)S(1)} %get-tuple-element.42), channel_id=1, source_target_pairs={{0,56},{8,48},{16,40},{24,32},{32,24},{40,16},{48,8},{56,0},{1,57}... | collective-permute-start | bytes 196616 | tf_op jit(solution)/shard_map/ppermute | solution.py:299
  19.4 0.7 %collective-permute-start.2 = (bf16[512,512]{1,0:T(8,128)(2,1)S(1)}, bf16[512,512]{1,0:T(8,128)(2,1)S(1)}, u32[]{:S(2)}, u32[]{:S(2)}) collective-permute-start(bf16[512,512]{1,0:T(8,128)(2,1)S(1)} %get-tuple-element.30.kv), channel_id=1, source_target_pairs={{0,4},{2,6},{4,0},{6,2},{1,5},{3,7},{5,1},{7,3},{8,12},{10,14},{12... | collective-permute-start | bytes 1572872 | tf_op jit(solution)/shard_map/ppermute | solution.py:299
  20.1 1.5 %collective-permute-done.7.got = bf16[256,128]{1,0:T(8,128)(2,1)S(1)} collective-permute-done((bf16[256,128]{1,0:T(8,128)(2,1)S(1)}, bf16[256,128]{1,0:T(8,128)(2,1)S(1)}, u32[]{:S(2)}, u32[]{:S(2)}) %collective-permute-start.7) | collective-permute-done | bytes 65568 | tf_op jit(solution)/shard_map/ppermute | solution.py:299
  21.6 0.7 %shard_map.72 = (f32[256,128]{1,0:T(8,128)}, f32[256,128]{1,0:T(8,128)S(1)}, bf16[256,128]{1,0:T(8,128)(2,1)S(1)}) custom-call(f32[256,128]{1,0:T(8,128)S(1)} %get-tuple-element.40.total, f32[256,128]{1,0:T(8,128)S(1)} %get-tuple-element.41.before, bf16[256,128]{1,0:T(8,128)(2,1)S(1)} %collective-permute-done.7.got), custom_call_target="tpu_custom_call" | custom-call | flops 131072 | bytes 262144 | tf_op jit(solution)/shard_map/pallas_call | solution.py:32
  22.3 1.2 %collective-permute-start.8 = (bf16[256,128]{1,0:T(8,128)(2,1)S(1)}, bf16[256,128]{1,0:T(8,128)(2,1)S(1)}, u32[]{:S(2)}, u32[]{:S(2)}) collective-permute-start(bf16[256,128]{1,0:T(8,128)(2,1)S(1)} %get-tuple-element.44), channel_id=1, source_target_pairs={{0,64},{64,128},{128,192},{192,0},{1,65},{65,129},{129,193},{193,1... | collective-permute-start | bytes 196616 | tf_op jit(solution)/shard_map/ppermute | solution.py:299
  23.5 3.1 %collective-permute-done.8.x1 = bf16[256,128]{1,0:T(8,128)(2,1)S(1)} collective-permute-done((bf16[256,128]{1,0:T(8,128)(2,1)S(1)}, bf16[256,128]{1,0:T(8,128)(2,1)S(1)}, u32[]{:S(2)}, u32[]{:S(2)}) %collective-permute-start.8) | collective-permute-done | bytes 65568 | tf_op jit(solution)/shard_map/ppermute | solution.py:299
  26.6 1.5 %collective-permute-start.9 = (bf16[256,128]{1,0:T(8,128)(2,1)S(1)}, bf16[256,128]{1,0:T(8,128)(2,1)S(1)}, u32[]{:S(2)}, u32[]{:S(2)}) collective-permute-start(bf16[256,128]{1,0:T(8,128)(2,1)S(1)} %get-tuple-element.44), channel_id=1, source_target_pairs={{0,128},{64,192},{128,0},{192,64},{1,129},{65,193},{129,1},{193,65... | collective-permute-start | bytes 196616 | tf_op jit(solution)/shard_map/ppermute | solution.py:299
  28.2 3.6 %collective-permute-done.9.x2 = bf16[256,128]{1,0:T(8,128)(2,1)S(1)} collective-permute-done((bf16[256,128]{1,0:T(8,128)(2,1)S(1)}, bf16[256,128]{1,0:T(8,128)(2,1)S(1)}, u32[]{:S(2)}, u32[]{:S(2)}) %collective-permute-start.9) | collective-permute-done | bytes 65568 | tf_op jit(solution)/shard_map/ppermute | solution.py:299
  31.8 1.0 %collective-permute-start.10 = (bf16[256,128]{1,0:T(8,128)(2,1)S(1)}, bf16[256,128]{1,0:T(8,128)(2,1)S(1)}, u32[]{:S(2)}, u32[]{:S(2)}) collective-permute-start(bf16[256,128]{1,0:T(8,128)(2,1)S(1)} %get-tuple-element.44), channel_id=1, source_target_pairs={{0,192},{64,0},{128,64},{192,128},{1,193},{65,1},{129,65},{193,129... | collective-permute-start | bytes 196616 | tf_op jit(solution)/shard_map/ppermute | solution.py:299
  32.8 2.1 %collective-permute-done.10.x3 = bf16[256,128]{1,0:T(8,128)(2,1)S(1)} collective-permute-done((bf16[256,128]{1,0:T(8,128)(2,1)S(1)}, bf16[256,128]{1,0:T(8,128)(2,1)S(1)}, u32[]{:S(2)}, u32[]{:S(2)}) %collective-permute-start.10) | collective-permute-done | bytes 65568 | tf_op jit(solution)/shard_map/ppermute | solution.py:299
  34.9 0.1 shard_map.73.m0
  35.0 1.4 %collective-permute-start.11 = (bf16[256,128]{1,0:T(8,128)(2,1)S(1)}, bf16[256,128]{1,0:T(8,128)(2,1)S(1)}, u32[]{:S(2)}, u32[]{:S(2)}) collective-permute-start(bf16[256,128]{1,0:T(8,128)(2,1)S(1)} %shard_map.73.m0), channel_id=1, source_target_pairs={{0,2},{2,4},{4,6},{6,0},{1,3},{3,5},{5,7},{7,1},{8,10},{10,12},{12... | collective-permute-start | bytes 196616 | tf_op jit(solution)/shard_map/ppermute | solution.py:299
  36.3 0.0 collective-permute-done.q_recv
  36.3 0.6 collective-permute-start.12
  36.9 3.0 %shard_map.67 = (f32[2,256,2048]{2,1,0:T(8,128)S(1)}, f32[2,256,1024]{2,1,0:T(8,128)S(1)}) custom-call(bf16[256,1024]{1,0:T(8,128)(2,1)S(1)} %get-tuple-element.26.q_keep, bf16[256,1024]{1,0:T(8,128)(2,1)S(1)} %collective-permute-done.q_recv, bf16[512,512]{1,0:T(8,128)(2,1)S(1)} %get-tuple-element.30.kv), custom_call_target="tpu_custom_call" | custom-call | flops 1073741824 | bytes 4194304 | tf_op jit(solution)/shard_map/pallas_call | solution.py:32
  40.0 0.0 collective-permute-done.3.left
  40.0 0.3 collective-permute-start.13
  40.3 0.0 collective-permute-done.4.right
  40.3 0.0 copy-start.1
  40.3 0.0 slice-start
  40.3 6.9 %shard_map.68 = (f32[2,256,2048]{2,1,0:T(8,128)S(1)}, f32[2,256,1024]{2,1,0:T(8,128)S(1)}) custom-call(bf16[256,1024]{1,0:T(8,128)(2,1)S(1)} %get-tuple-element.26.q_keep, bf16[256,1024]{1,0:T(8,128)(2,1)S(1)} %collective-permute-done.q_recv, bf16[512,512]{1,0:T(8,128)(2,1)S(1)} %collective-permute-done.3.left, ...), custom_call_target="tpu_custom_call", output_to_operand_aliasing={{0}: (4, {}), {1}: (5, {})} | custom-call | flops 2147483648 | bytes 4194304 | tf_op jit(solution)/shard_map/pallas_call | solution.py:32
  47.3 0.0 collective-permute-done.2.kv
  47.3 0.0 copy-done.1
  47.3 0.0 copy-start
  47.3 0.0 slice-start.1
  47.3 4.0 %shard_map.69.dot = f32[2,256,1024]{2,1,0:T(8,128)S(1)} custom-call(bf16[256,1024]{1,0:T(8,128)(2,1)S(1)} %get-tuple-element.26.q_keep, bf16[256,1024]{1,0:T(8,128)(2,1)S(1)} %collective-permute-done.q_recv, bf16[512,512]{1,0:T(8,128)(2,1)S(1)} %collective-permute-done.2.kv, f32[2,256,2048]{2,1,0:T(8,128)S(1)} %get-tuple-element.33.ext, ...), custom_call_target="tpu_custom_call" | custom-call | flops 1073741824 | bytes 4194304 | tf_op jit(solution)/shard_map/pallas_call | solution.py:32
  51.4 0.0 collective-permute-done.11.m1
  51.4 0.0 collective-permute-done.12.m2
  51.4 0.0 collective-permute-done.13.m3
  51.4 0.0 copy-done
  51.4 1.2 %shard_map.74 = (bf16[256,1024]{1,0:T(8,128)(2,1)S(1)}, bf16[256,1024]{1,0:T(8,128)(2,1)S(1)}) custom-call(bf16[256,1024]{1,0:T(8,128)(2,1)S(1)} %get-tuple-element.26.q_keep, bf16[256,1024]{1,0:T(8,128)(2,1)S(1)} %collective-permute-done.q_recv, f32[2,256,1024]{2,1,0:T(8,128)S(1)} %shard_map.69.dot, bf16[256,128]{1,0:T(8,128)(2,1)S(1)} %shard_map.73.m0, ...), custom_call_target="tpu_custom_call" | custom-call | flops 134217728 | bytes 4194304 | tf_op jit(solution)/shard_map/pallas_call | solution.py:32
  52.6 8.2 %collective-permute-start.14 = (bf16[256,1024]{1,0:T(8,128)(2,1)S(1)}, bf16[256,1024]{1,0:T(8,128)(2,1)S(1)}, u32[]{:S(2)}, u32[]{:S(2)}) collective-permute-start(bf16[256,1024]{1,0:T(8,128)(2,1)S(1)} %get-tuple-element.45), channel_id=1, source_target_pairs={{0,1},{1,0},{2,3},{3,2},{4,5},{5,4},{6,7},{7,6},{8,9},{9,8},{10,11... | collective-permute-start | bytes 1572872 | tf_op jit(solution)/shard_map/ppermute | solution.py:299
  60.8 0.0 slice-done
  60.8 0.0 slice-done.1
  60.8 1.2 %shard_map.75.begun = f32[256,2048]{1,0:T(8,128)S(1)} custom-call(bf16[256,1024]{1,0:T(8,128)(2,1)S(1)} %get-tuple-element.46.x, bf16[2048,2048]{1,0:T(8,128)(2,1)S(1)} %bitcast.3), custom_call_target="tpu_custom_call" | custom-call | flops 1073741824 | bytes 8388608 | tf_op jit(solution)/shard_map/pallas_call | solution.py:32
  62.1 0.3 collective-permute-done.14.x
  62.4 2.8 %project_last.1 = bf16[256,2048]{1,0:T(8,128)(2,1)} custom-call(bf16[256,1024]{1,0:T(8,128)(2,1)S(1)} %collective-permute-done.14.x, f32[256,2048]{1,0:T(8,128)S(1)} %shard_map.75.begun, bf16[2048,2048]{1,0:T(8,128)(2,1)S(1)} %bitcast.3), custom_call_target="tpu_custom_call" | custom-call | flops 1073741824 | bytes 8388608 | tf_op jit(solution)/shard_map/project_last/pallas_call | solution.py:286
  (4 shorter events, 0.1 us)
Async XLA Ops:
  1.1 2.1 %collective-permute-start.1 = (bf16[256,512]{1,0:T(8,128)(2,1)S(1)}, bf16[256,512]{1,0:T(8,128)(2,1)S(1)}, u32[]{:S(2)}, u32[]{:S(2)}) collective-permute-start(bf16[256,512]{1,0:T(8,128)(2,1)S(1)} %get-tuple-element.29), channel_id=1, source_target_pairs={{0,1},{1,0},{2,3},{3,2},{4,5},{5,4},{6,7},{7,6},{8,9},{9,8},{10,11... | collective-permute-start | bytes 786440 | tf_op jit(solution)/shard_map/ppermute | solution.py:299
  3.1 33.2 %collective-permute-start = (bf16[256,1024]{1,0:T(8,128)(2,1)S(1)}, bf16[256,1024]{1,0:T(8,128)(2,1)S(1)}, u32[]{:S(2)}, u32[]{:S(2)}) collective-permute-start(bf16[256,1024]{1,0:T(8,128)(2,1)S(1)} %get-tuple-element.27), channel_id=1, source_target_pairs={{0,1},{1,0},{2,3},{3,2},{4,5},{5,4},{6,7},{7,6},{8,9},{9,8},{10,11... | collective-permute-start | bytes 1572872 | tf_op jit(solution)/shard_map/ppermute | solution.py:299
  3.6 36.4 %collective-permute-start.3 = (bf16[512,512]{1,0:T(8,128)(2,1)S(1)}, bf16[512,512]{1,0:T(8,128)(2,1)S(1)}, u32[]{:S(2)}, u32[]{:S(2)}) collective-permute-start(bf16[512,512]{1,0:T(8,128)(2,1)S(1)} %get-tuple-element.30.kv), channel_id=1, source_target_pairs={{0,2},{2,4},{4,6},{6,0},{1,3},{3,5},{5,7},{7,1},{8,10},{10,12},{12... | collective-permute-start | bytes 1572872 | tf_op jit(solution)/shard_map/ppermute | solution.py:299
  5.3 35.0 %collective-permute-start.4 = (bf16[512,512]{1,0:T(8,128)(2,1)S(1)}, bf16[512,512]{1,0:T(8,128)(2,1)S(1)}, u32[]{:S(2)}, u32[]{:S(2)}) collective-permute-start(bf16[512,512]{1,0:T(8,128)(2,1)S(1)} %get-tuple-element.30.kv), channel_id=1, source_target_pairs={{0,6},{2,0},{4,2},{6,4},{1,7},{3,1},{5,3},{7,5},{8,14},{10,8},{12,... | collective-permute-start | bytes 1572872 | tf_op jit(solution)/shard_map/ppermute | solution.py:299
  5.3 3.4 %collective-permute-start.5 = (bf16[256,128]{1,0:T(8,128)(2,1)S(1)}, bf16[256,128]{1,0:T(8,128)(2,1)S(1)}, u32[]{:S(2)}, u32[]{:S(2)}) collective-permute-start(bf16[256,128]{1,0:T(8,128)(2,1)S(1)} %get-tuple-element.36), channel_id=1, source_target_pairs={{0,8},{8,0},{16,24},{24,16},{32,40},{40,32},{48,56},{56,48},{1,9},... | collective-permute-start | bytes 196616 | tf_op jit(solution)/shard_map/ppermute | solution.py:299
  8.8 5.0 %collective-permute-start.6 = (bf16[256,128]{1,0:T(8,128)(2,1)S(1)}, bf16[256,128]{1,0:T(8,128)(2,1)S(1)}, u32[]{:S(2)}, u32[]{:S(2)}) collective-permute-start(bf16[256,128]{1,0:T(8,128)(2,1)S(1)} %get-tuple-element.39), channel_id=1, source_target_pairs={{0,16},{8,24},{16,0},{24,8},{32,48},{40,56},{48,32},{56,40},{1,17}... | collective-permute-start | bytes 196616 | tf_op jit(solution)/shard_map/ppermute | solution.py:299
  13.8 7.8 %collective-permute-start.7 = (bf16[256,128]{1,0:T(8,128)(2,1)S(1)}, bf16[256,128]{1,0:T(8,128)(2,1)S(1)}, u32[]{:S(2)}, u32[]{:S(2)}) collective-permute-start(bf16[256,128]{1,0:T(8,128)(2,1)S(1)} %get-tuple-element.42), channel_id=1, source_target_pairs={{0,56},{8,48},{16,40},{24,32},{32,24},{40,16},{48,8},{56,0},{1,57}... | collective-permute-start | bytes 196616 | tf_op jit(solution)/shard_map/ppermute | solution.py:299
  19.4 27.9 %collective-permute-start.2 = (bf16[512,512]{1,0:T(8,128)(2,1)S(1)}, bf16[512,512]{1,0:T(8,128)(2,1)S(1)}, u32[]{:S(2)}, u32[]{:S(2)}) collective-permute-start(bf16[512,512]{1,0:T(8,128)(2,1)S(1)} %get-tuple-element.30.kv), channel_id=1, source_target_pairs={{0,4},{2,6},{4,0},{6,2},{1,5},{3,7},{5,1},{7,3},{8,12},{10,14},{12... | collective-permute-start | bytes 1572872 | tf_op jit(solution)/shard_map/ppermute | solution.py:299
  22.3 4.3 %collective-permute-start.8 = (bf16[256,128]{1,0:T(8,128)(2,1)S(1)}, bf16[256,128]{1,0:T(8,128)(2,1)S(1)}, u32[]{:S(2)}, u32[]{:S(2)}) collective-permute-start(bf16[256,128]{1,0:T(8,128)(2,1)S(1)} %get-tuple-element.44), channel_id=1, source_target_pairs={{0,64},{64,128},{128,192},{192,0},{1,65},{65,129},{129,193},{193,1... | collective-permute-start | bytes 196616 | tf_op jit(solution)/shard_map/ppermute | solution.py:299
  26.6 5.2 %collective-permute-start.9 = (bf16[256,128]{1,0:T(8,128)(2,1)S(1)}, bf16[256,128]{1,0:T(8,128)(2,1)S(1)}, u32[]{:S(2)}, u32[]{:S(2)}) collective-permute-start(bf16[256,128]{1,0:T(8,128)(2,1)S(1)} %get-tuple-element.44), channel_id=1, source_target_pairs={{0,128},{64,192},{128,0},{192,64},{1,129},{65,193},{129,1},{193,65... | collective-permute-start | bytes 196616 | tf_op jit(solution)/shard_map/ppermute | solution.py:299
  31.8 3.1 %collective-permute-start.10 = (bf16[256,128]{1,0:T(8,128)(2,1)S(1)}, bf16[256,128]{1,0:T(8,128)(2,1)S(1)}, u32[]{:S(2)}, u32[]{:S(2)}) collective-permute-start(bf16[256,128]{1,0:T(8,128)(2,1)S(1)} %get-tuple-element.44), channel_id=1, source_target_pairs={{0,192},{64,0},{128,64},{192,128},{1,193},{65,1},{129,65},{193,129... | collective-permute-start | bytes 196616 | tf_op jit(solution)/shard_map/ppermute | solution.py:299
  35.0 16.4 %collective-permute-start.11 = (bf16[256,128]{1,0:T(8,128)(2,1)S(1)}, bf16[256,128]{1,0:T(8,128)(2,1)S(1)}, u32[]{:S(2)}, u32[]{:S(2)}) collective-permute-start(bf16[256,128]{1,0:T(8,128)(2,1)S(1)} %shard_map.73.m0), channel_id=1, source_target_pairs={{0,2},{2,4},{4,6},{6,0},{1,3},{3,5},{5,7},{7,1},{8,10},{10,12},{12... | collective-permute-start | bytes 196616 | tf_op jit(solution)/shard_map/ppermute | solution.py:299
  36.3 15.1 %collective-permute-start.12 = (bf16[256,128]{1,0:T(8,128)(2,1)S(1)}, bf16[256,128]{1,0:T(8,128)(2,1)S(1)}, u32[]{:S(2)}, u32[]{:S(2)}) collective-permute-start(bf16[256,128]{1,0:T(8,128)(2,1)S(1)} %shard_map.73.m0), channel_id=1, source_target_pairs={{0,4},{2,6},{4,0},{6,2},{1,5},{3,7},{5,1},{7,3},{8,12},{10,14},{12... | collective-permute-start | bytes 196616 | tf_op jit(solution)/shard_map/ppermute | solution.py:299
  40.0 11.4 %collective-permute-start.13 = (bf16[256,128]{1,0:T(8,128)(2,1)S(1)}, bf16[256,128]{1,0:T(8,128)(2,1)S(1)}, u32[]{:S(2)}, u32[]{:S(2)}) collective-permute-start(bf16[256,128]{1,0:T(8,128)(2,1)S(1)} %shard_map.73.m0), channel_id=1, source_target_pairs={{0,6},{2,0},{4,2},{6,4},{1,7},{3,1},{5,3},{7,5},{8,14},{10,8},{12,... | collective-permute-start | bytes 196616 | tf_op jit(solution)/shard_map/ppermute | solution.py:299
  40.3 7.0 %copy-start.1 = (f32[2048]{0:T(1024)S(1)}, f32[2048]{0:T(1024)}, u32[]{:S(2)}) copy-start(f32[2048]{0:T(1024)} %param.10) | copy-start | bytes 24580
  40.3 20.5 %slice-start = ((s8[8388608]{0:T(1024)(128)(4,1)}), s8[4194304]{0:T(1024)(128)(4,1)S(1)}, s32[]{:S(2)}) async-start(s8[8388608]{0:T(1024)(128)(4,1)} %bitcast.2), calls=%async_computation | async-start | bytes 8388608
  47.3 4.1 %copy-start = (f32[2048]{0:T(1024)S(1)}, f32[2048]{0:T(1024)}, u32[]{:S(2)}) copy-start(f32[2048]{0:T(1024)} %param.9) | copy-start | bytes 24580
  47.3 13.5 %slice-start.1 = ((s8[8388608]{0:T(1024)(128)(4,1)}), s8[4194304]{0:T(1024)(128)(4,1)S(1)}, s32[]{:S(2)}) async-start(s8[8388608]{0:T(1024)(128)(4,1)} %bitcast.2), calls=%async_computation.1 | async-start | bytes 8388608
  52.6 9.7 %collective-permute-start.14 = (bf16[256,1024]{1,0:T(8,128)(2,1)S(1)}, bf16[256,1024]{1,0:T(8,128)(2,1)S(1)}, u32[]{:S(2)}, u32[]{:S(2)}) collective-permute-start(bf16[256,1024]{1,0:T(8,128)(2,1)S(1)} %get-tuple-element.45), channel_id=1, source_target_pairs={{0,1},{1,0},{2,3},{3,2},{4,5},{5,4},{6,7},{7,6},{8,9},{9,8},{10,11... | collective-permute-start | bytes 1572872 | tf_op jit(solution)/shard_map/ppermute | solution.py:299

commit v2 on v1

v2 whole, which is shorter than its diff:
```python
import functools

import jax
import jax.numpy as jnp
from jax import lax
from jax.experimental import pallas as pl
from jax.experimental.pallas import tpu as pltpu
from jax.sharding import Mesh
from jax.sharding import PartitionSpec as P


HEAD = 128
GROUP = 4
HEADS = 8
AXES = ("sx", "sz", "y", "c")
EXP_SCALE = float(HEAD) ** (-0.5) * 1.4426950408889634
NT = (((1,), (1,)), ((), ()))
TN = (((0,), (0,)), ((), ()))
BF16 = jnp.bfloat16
F32 = jnp.float32
VM = pl.BlockSpec(memory_space=pltpu.VMEM)
HBM = pl.BlockSpec(memory_space=pltpu.HBM)


def placed(x, space=pltpu.VMEM):
    return pltpu.with_memory_space_constraint(x, space)


def kernel_call(body, outs, args, limit, flops=0, nbytes=0, trans=0, specs=None, **more):
    specs = specs or [VM] * len(args)
    args = [placed(a, s.memory_space) for a, s in zip(args, specs)]
    return pl.pallas_call(
        body,
        out_shape=[pltpu.VMEM(shape, dtype) for shape, dtype in outs],
        in_specs=specs,
        out_specs=[VM] * len(outs),
        compiler_params=pltpu.CompilerParams(vmem_limit_bytes=limit * 2**20),
        cost_estimate=pl.CostEstimate(flops=flops, bytes_accessed=nbytes, transcendentals=trans),
        **more,
    )(*args)


def feature_map(x):
    return jnp.where(x > 0, x + 1.0, jnp.exp(jnp.minimum(x, 0.0)))


def prep_kernel(k, v, q, kv_own, q_own, sems):
    half = k.shape[1] // 2
    c = lax.axis_index("c")
    moves = [(k, kv_own.at[:, :half], half), (v, kv_own.at[:, half:], half), (q, q_own, 4 * half)]
    copies = []
    for n, (src, dst, width) in enumerate(moves):
        cols = pl.ds(pl.multiple_of(c * width, width), width)
        copies.append(pltpu.make_async_copy(src.at[:, cols], dst, sems.at[n]))
        copies[-1].start()
    for copy in copies:
        copy.wait()


def prep(k, v, q):
    outs = [(k.shape, BF16), ((q.shape[0], q.shape[1] // 2), BF16)]
    return kernel_call(
        prep_kernel, outs, (k, v, q), 8, nbytes=2**21, specs=[HBM] * 3,
        scratch_shapes=[pltpu.SemaphoreType.DMA((3,))],
    )


def part_kernel(kv_own, k_recv, v_recv, both, total, sent):
    rows, half = k_recv.shape[0], k_recv.shape[1] // 2
    c = lax.axis_index("c")
    own = pl.ds(pl.multiple_of(c * half, half), half)
    both[pl.ds(pl.multiple_of(c * rows, rows), rows), :] = kv_own[...]
    for i, ref in enumerate((k_recv, v_recv)):
        at = pl.ds(pl.multiple_of(rows - c * rows, rows), rows)
        both[at, i * half : (i + 1) * half] = ref[:, own]
    for g in range(2):
        kk = slice(g * HEAD, (g + 1) * HEAD)
        vv = slice(half + g * HEAD, half + (g + 1) * HEAD)
        sig = feature_map(both[:, kk].astype(F32)).astype(BF16)
        acc = lax.dot_general(sig, both[:, vv], TN, preferred_element_type=F32)
        total[kk, :] = acc
        sent[kk, :] = acc.astype(BF16)


def part(kv_own, k_recv, v_recv):
    rows, cols = kv_own.shape
    outs = [((2 * rows, cols), BF16), ((cols // 2, HEAD), F32), ((cols // 2, HEAD), BF16)]
    return kernel_call(part_kernel, outs, (kv_own, k_recv, v_recv), 8, 2**26, 2**21)


def tiles(rows=256, size=128):
    for g in range(2):
        for b in range(2):
            for j in range(GROUP):
                h = g * GROUP + j
                cols, wide = slice(h * HEAD, (h + 1) * HEAD), slice(2 * h * HEAD, 2 * (h + 1) * HEAD)
                for r in range(0, rows, size):
                    yield g, b, h, slice(r, r + size), cols, wide


def head_of(q, h):
    if q.shape[1] == HEADS * HEAD:
        return slice(h * HEAD, (h + 1) * HEAD)
    first = lax.axis_index("c") * (HEADS * HEAD) + h * HEAD
    return pl.ds(pl.multiple_of(first, HEAD), HEAD)


def fill_ones(kv, v_ones):
    for g in range(2):
        v = kv[:, (2 + g) * HEAD : (3 + g) * HEAD]
        v_ones[g] = jnp.concatenate([v, jnp.ones_like(v)], axis=1)


def scores(q_refs, kv, g, b, h, r):
    q, k = q_refs[b][r, head_of(q_refs[b], h)], kv[:, g * HEAD : (g + 1) * HEAD]
    return lax.dot_general(q, k, NT, preferred_element_type=F32)


def weigh(s, new, v_ones):
    w = [
        jnp.exp2((s[:, n : n + HEAD] - new) * EXP_SCALE).astype(BF16)
        for n in range(0, s.shape[1], HEAD)
    ]
    return jnp.dot(jnp.concatenate(w, axis=1), v_ones, preferred_element_type=F32)


def first_kernel(q_keep, q_recv, kv, ext, top, v_ones):
    rows = q_keep.shape[0]
    fill_ones(kv, v_ones)
    c = lax.axis_index("c")
    for g, b, h, r, cols, wide in tiles():
        s = scores((q_keep, q_recv), kv, g, b, h, r)
        first = (c if b == 0 else 1 - c) * rows + r.start
        row = lax.broadcasted_iota(jnp.int32, s.shape, 0) + first
        s = jnp.where(row >= lax.broadcasted_iota(jnp.int32, s.shape, 1), s, -1e30)
        m = jnp.broadcast_to(jnp.max(s, axis=-1, keepdims=True), (s.shape[0], HEAD))
        ext[b, r, wide] = weigh(s, m, v_ones[g])
        top[b, r, cols] = m


def state(rows):
    return [((2, rows, 2 * HEADS * HEAD), F32), ((2, rows, HEADS * HEAD), F32)]


def attend_first(q_keep, q_recv, kv):
    rows, keys = q_keep.shape[0], kv.shape[0]
    count = 2 * HEADS * rows * keys
    return kernel_call(
        first_kernel, state(rows), (q_keep, q_recv, kv), 20,
        4 * count * HEAD, 2**22, count,
        scratch_shapes=[pltpu.VMEM((2, keys, 2 * HEAD), BF16)],
    )


def fold_chunk(q_refs, kv, v_ones, ext, top):
    fill_ones(kv, v_ones)
    for g, b, h, r, cols, wide in tiles():
        s = scores(q_refs, kv, g, b, h, r)
        old = top[b, r, cols]
        new = jnp.maximum(old, jnp.max(s, axis=-1, keepdims=True))
        alpha = jnp.exp2((old - new) * EXP_SCALE)
        total = ext[b, r, wide] * jnp.concatenate([alpha, alpha], axis=1) + weigh(s, new, v_ones[g])
        yield b, h, r, cols, wide, new, total


def next_kernel(first_y, q_keep, q_recv, kv, ext_in, top_in, ext, top, v_ones):
    @pl.when(lax.axis_index("y") >= first_y)
    def _():
        for b, h, r, cols, wide, new, total in fold_chunk((q_keep, q_recv), kv, v_ones, ext, top):
            ext[b, r, wide] = total
            top[b, r, cols] = new


def attend_next(first_y, q_keep, q_recv, kv, ext, top):
    rows, keys = q_keep.shape[0], kv.shape[0]
    count = 2 * HEADS * rows * keys
    return kernel_call(
        functools.partial(next_kernel, first_y), state(rows), (q_keep, q_recv, kv, ext, top),
        20, 4 * count * HEAD, 2**22, count,
        scratch_shapes=[pltpu.VMEM((2, keys, 2 * HEAD), BF16)],
        input_output_aliases={3: 0, 4: 1},
    )


def head_norm(x, gain):
    return x * (0.5 * lax.rsqrt(jnp.mean(x * x, axis=-1, keepdims=True) + 1e-06)) * gain


def last_kernel(q_keep, q_recv, kv_a, kv_b, ext, top, gain, out, kv, v_ones):
    y, c = lax.axis_index("y"), lax.axis_index("c")
    own = pl.multiple_of(c * HEADS, HEADS)

    def put(b, h, r, cols, total):
        acc, den = total[:, :HEAD], total[:, HEAD:]
        square = jnp.mean(acc * acc + 1e-06 * (den * den), axis=-1, keepdims=True)
        out[b, r, cols] = acc * (0.5 * lax.rsqrt(square)) * gain[pl.ds(own + h, 1), :]

    @pl.when(y >= 2)
    def _():
        half = kv_a.shape[0]
        kv[:half, :] = kv_a[...]
        kv[half:, :] = kv_b[...]
        for b, h, r, cols, wide, new, total in fold_chunk((q_keep, q_recv), kv, v_ones, ext, top):
            put(b, h, r, cols, total)

    @pl.when(y < 2)
    def _():
        for g, b, h, r, cols, wide in tiles():
            put(b, h, r, cols, ext[b, r, wide])


def attend_last(q_keep, q_recv, far, ext, top, gain):
    rows, keys, width = q_keep.shape[0], 2 * far[0].shape[0], far[0].shape[1]
    count = 2 * HEADS * rows * keys
    outs = [((2, rows, HEADS * HEAD), F32)]
    return kernel_call(
        last_kernel, outs, (q_keep, q_recv, *far, ext, top, gain), 20,
        4 * count * HEAD, 2**22, count,
        scratch_shapes=[pltpu.VMEM((keys, width), BF16), pltpu.VMEM((2, keys, 2 * HEAD), BF16)],
    )[0]


def sig_kernel(q_keep, q_recv, sig):
    for b, q in enumerate((q_keep, q_recv)):
        for h in range(HEADS):
            x = q[:, head_of(q, h)].astype(F32)
            sig[b, :, h * HEAD : (h + 1) * HEAD] = feature_map(x).astype(BF16)


def mix_kernel(b, sig, dot, m0, m1, m2, m3, gain, out):
    own = pl.multiple_of(lax.axis_index("c") * HEADS, HEADS)
    memory = (m0[...].astype(F32) + m1[...].astype(F32)) + (m2[...].astype(F32) + m3[...].astype(F32))
    memory = memory.astype(BF16)
    for h in range(HEADS):
        cols, g = slice(h * HEAD, (h + 1) * HEAD), h // GROUP
        read = jnp.dot(
            sig[b, :, cols], memory[g * HEAD : (g + 1) * HEAD], preferred_element_type=F32
        )
        mixed = head_norm(read, gain[pl.ds(own + h, 1), :]) + dot[b, :, cols]
        out[:, cols] = mixed.astype(BF16)


def mix(b, sig, dot, memory, gain):
    outs = [(sig.shape[1:], BF16)]
    body = functools.partial(mix_kernel, b)
    return kernel_call(body, outs, (sig, dot, *memory, gain), 12, 2**26, 2**21)[0]


def project_first_kernel(x, weight, out):
    half = x.shape[1]
    own = pl.multiple_of(lax.axis_index("c") * half, half)
    for n in range(0, weight.shape[1], 512):
        out[:, n : n + 512] = jnp.dot(
            x[...], weight[pl.ds(own, half), n : n + 512], preferred_element_type=F32
        )


def project_first(x, weight):
    outs = [((x.shape[0], weight.shape[1]), F32)]
    return kernel_call(project_first_kernel, outs, (x, weight), 16, 2**30, 2**23)[0]


def project_last_kernel(x, begun, weight, out, stage, sems):
    half, width = x.shape[1], 256
    other = pl.multiple_of(half - lax.axis_index("c") * half, half)
    copies = []
    for i in range(out.shape[1] // width):
        n = slice(i * width, (i + 1) * width)
        total = jnp.dot(x[...], weight[pl.ds(other, half), n], preferred_element_type=F32)
        stage[:, n] = (begun[:, n] + total).astype(BF16)
        copies.append(pltpu.make_async_copy(stage.at[:, n], out.at[:, n], sems.at[i]))
        copies[-1].start()
    for copy in copies:
        copy.wait()


def project_last(x, begun, weight):
    shape = begun.shape
    return pl.pallas_call(
        project_last_kernel,
        out_shape=pltpu.HBM(shape, BF16),
        in_specs=[VM] * 3,
        out_specs=HBM,
        scratch_shapes=[pltpu.VMEM(shape, BF16), pltpu.SemaphoreType.DMA((shape[1] // 256,))],
        name="project_last",
        compiler_params=pltpu.CompilerParams(vmem_limit_bytes=16 * 2**20),
        cost_estimate=pl.CostEstimate(flops=2**30, bytes_accessed=2**23, transcendentals=0),
    )(*[placed(a) for a in (x, begun, weight)])


def permute(x, axis, partner):
    return lax.ppermute(x, axis, list(enumerate(partner)))


def shift(x, axis, step, size):
    return permute(x, axis, [(i + step) % size for i in range(size)])


def add_kernel(axis, level, total, before, got, before_out, *more):
    upper = ((lax.axis_index(axis) >> level) & 1).astype(F32)
    term = got[...].astype(F32)
    earlier = before[...] + term * upper
    before_out[...] = earlier.astype(before_out.dtype)
    if more:
        total_out, sent = more
        summed = total[...] + term
        total_out[...] = summed
        sent[...] = summed.astype(BF16)


def earlier_memory(total, sent):
    before = jnp.zeros_like(total)
    shape = total.shape
    steps = (
        ("sz", 0, [i ^ 1 for i in range(8)], "z1"),
        ("sz", 1, [i ^ 2 for i in range(8)], "z2"),
        ("sz", 2, [7 - i for i in range(8)], "z3"),
        ("sx", 0, [i ^ 1 for i in range(4)], "x1"),
        ("sx", 1, [i ^ 2 for i in range(4)], "x2"),
    )
    for axis, level, partner, name in steps:
        last = name == "x2"
        got = permute(sent, axis, partner)
        outs = [(shape, BF16)] if last else [(shape, F32), (shape, F32), (shape, BF16)]
        result = kernel_call(
            functools.partial(add_kernel, axis, level), outs, (total, before, got),
            4, 2**17, 2**18,
        )
        if last:
            return result[0]
        before, total, sent = result


def layer(queries, keys, values, gain_mem, gain_dot, out_weight):
    k_recv = permute(keys, "c", (1, 0))
    v_recv = permute(values, "c", (1, 0))
    q_recv = permute(queries, "c", (1, 0))
    kv_own, q_own = prep(keys, values, queries)
    kv, total, sent = part(kv_own, k_recv, v_recv)
    left = shift(kv, "y", 1, 4)
    right = shift(kv, "y", 3, 4)
    half = kv.shape[0] // 2
    far = shift(left[:half], "y", 1, 4), shift(right[half:], "y", 3, 4)
    mine = earlier_memory(total, sent)
    memory = [mine] + [shift(mine, "y", step, 4) for step in (1, 2, 3)]
    ext, top = attend_first(q_own, q_recv, kv)
    ext, top = attend_next(1, q_own, q_recv, left, ext, top)
    ext, top = attend_next(3, q_own, q_recv, right, ext, top)
    gain_dot = gain_dot.reshape(2 * HEADS, HEAD)
    gain_mem = gain_mem.reshape(2 * HEADS, HEAD)
    dot = attend_last(q_own, q_recv, far, ext, top, gain_dot)
    shape = (2, *q_own.shape)
    sig = kernel_call(sig_kernel, [(shape, BF16)], (q_own, q_recv), 8, 2**21, 2**22)[0]
    mixed_send = mix(1, sig, dot, memory, gain_mem)
    mixed_keep = mix(0, sig, dot, memory, gain_mem)
    begun = project_first(mixed_keep, out_weight)
    mixed_recv = permute(mixed_send, "c", (1, 0))
    return project_last(mixed_recv, begun, out_weight)


def solution(mesh):
    finer = Mesh(mesh.devices.reshape(4, 8, 4, 2), AXES)
    in_specs = (P(AXES, None), P(AXES, None), P(AXES, None), P(), P(), P())
    return jax.shard_map(
        layer, mesh=finer, in_specs=in_specs, out_specs=P(AXES, None), check_vma=False
    )
```

time: 65.3 us -> 61.7 us (0.945)
  the two profiles are of different devices: /device:TPU:25 before, /device:TPU:29 now
where the time goes in v2:
time: 61.7 us; the launch traced here: 61.5 us
  starting transfers between devices  27.2 us (44%)
  Pallas kernels  19.7 us (32%)
  waiting for transfers between devices  14.1 us (23%)
    ppermute x16, starting transfers between devices, permute(): return lax.ppermute(x, axis, list(enumerate(partner)))  27.2 us
    pallas_call x15, Pallas kernels, kernel_call(): pl.pallas_call(body, out_shape=[pltpu.VMEM(shape, dtype) for shape, dtype...  17.6 us
    ppermute x16, waiting for transfers between devices, permute(): return lax.ppermute(x, axis, list(enumerate(partner)))  14.1 us
    pallas_call x1, Pallas kernels, project_last(): pl.pallas_call(project_last_kernel, out_shape=pltpu.HBM(shape, BF16), in_...  2.12 us
  transfers between devices with their start and end apart: 16, of which 7 were waited for; matrix products, arithmetic and copies ran while one was open for 0% of the time, Pallas kernels for 28%

profile of v2, /device:TPU:29, one launch (start us, length us, event | category | flops | bytes accessed | tf_op | source)
XLA Modules:
  0.0 61.5 jit_solution(7358463405664369046)
XLA Ops:
  0.0 0.7 %collective-permute-start = (bf16[256,2048]{1,0:T(8,128)(2,1)}, bf16[256,2048]{1,0:T(8,128)(2,1)S(1)}, u32[]{:S(2)}, u32[]{:S(2)}) collective-permute-start(bf16[256,2048]{1,0:T(8,128)(2,1)} %q.1), channel_id=1, source_target_pairs={{0,1},{1,0},{2,3},{3,2},{4,5},{5,4},{6,7},{7,6},{8,9},{9,8},{10,11... | collective-permute-start | bytes 3145736 | tf_op jit(solution)/shard_map/ppermute | solution.py:292
  0.7 0.0 collective-permute-start.1
  0.7 0.5 collective-permute-start.2
  1.2 1.2 %shard_map.64 = (bf16[256,512]{1,0:T(8,128)(2,1)S(1)}, bf16[256,1024]{1,0:T(8,128)(2,1)S(1)}) custom-call(bf16[256,512]{1,0:T(8,128)(2,1)} %k.1, bf16[256,512]{1,0:T(8,128)(2,1)} %v.1, bf16[256,2048]{1,0:T(8,128)(2,1)} %q.1), custom_call_target="tpu_custom_call" | custom-call | bytes 2097152 | tf_op jit(solution)/shard_map/pallas_call | solution.py:32
  2.4 1.2 %collective-permute-done.1.k_recv = bf16[256,512]{1,0:T(8,128)(2,1)S(1)} collective-permute-done((bf16[256,512]{1,0:T(8,128)(2,1)}, bf16[256,512]{1,0:T(8,128)(2,1)S(1)}, u32[]{:S(2)}, u32[]{:S(2)}) %collective-permute-start.1) | collective-permute-done | bytes 262176 | tf_op jit(solution)/shard_map/ppermute | solution.py:292
  3.5 0.4 collective-permute-done.2.v_recv
  3.9 0.4 shard_map.66
  4.4 0.1 collective-permute-start.3
  4.4 1.5 %collective-permute-start.5 = (bf16[512,512]{1,0:T(8,128)(2,1)S(1)}, bf16[512,512]{1,0:T(8,128)(2,1)S(1)}, u32[]{:S(2)}, u32[]{:S(2)}) collective-permute-start(bf16[512,512]{1,0:T(8,128)(2,1)S(1)} %get-tuple-element.30.kv), channel_id=1, source_target_pairs={{0,6},{2,0},{4,2},{6,4},{1,7},{3,1},{5,3},{7,5},{8,14},{10,8},{12,... | collective-permute-start | bytes 1572872 | tf_op jit(solution)/shard_map/ppermute | solution.py:292
  5.9 1.6 %collective-permute-start.7 = (bf16[256,128]{1,0:T(8,128)(2,1)S(1)}, bf16[256,128]{1,0:T(8,128)(2,1)S(1)}, u32[]{:S(2)}, u32[]{:S(2)}) collective-permute-start(bf16[256,128]{1,0:T(8,128)(2,1)S(1)} %get-tuple-element.38), channel_id=1, source_target_pairs={{0,8},{8,0},{16,24},{24,16},{32,40},{40,32},{48,56},{56,48},{1,9},... | collective-permute-start | bytes 196616 | tf_op jit(solution)/shard_map/ppermute | solution.py:292
  7.5 1.9 %collective-permute-done.7.got = bf16[256,128]{1,0:T(8,128)(2,1)S(1)} collective-permute-done((bf16[256,128]{1,0:T(8,128)(2,1)S(1)}, bf16[256,128]{1,0:T(8,128)(2,1)S(1)}, u32[]{:S(2)}, u32[]{:S(2)}) %collective-permute-start.7) | collective-permute-done | bytes 65568 | tf_op jit(solution)/shard_map/ppermute | solution.py:292
  9.5 3.1 %collective-permute-start.8 = (bf16[256,128]{1,0:T(8,128)(2,1)S(1)}, bf16[256,128]{1,0:T(8,128)(2,1)S(1)}, u32[]{:S(2)}, u32[]{:S(2)}) collective-permute-start(bf16[256,128]{1,0:T(8,128)(2,1)S(1)} %get-tuple-element.41), channel_id=1, source_target_pairs={{0,16},{8,24},{16,0},{24,8},{32,48},{40,56},{48,32},{56,40},{1,17}... | collective-permute-start | bytes 196616 | tf_op jit(solution)/shard_map/ppermute | solution.py:292
  12.6 2.0 %collective-permute-done.8.got = bf16[256,128]{1,0:T(8,128)(2,1)S(1)} collective-permute-done((bf16[256,128]{1,0:T(8,128)(2,1)S(1)}, bf16[256,128]{1,0:T(8,128)(2,1)S(1)}, u32[]{:S(2)}, u32[]{:S(2)}) %collective-permute-start.8) | collective-permute-done | bytes 65568 | tf_op jit(solution)/shard_map/ppermute | solution.py:292
  14.6 5.6 %collective-permute-start.9 = (bf16[256,128]{1,0:T(8,128)(2,1)S(1)}, bf16[256,128]{1,0:T(8,128)(2,1)S(1)}, u32[]{:S(2)}, u32[]{:S(2)}) collective-permute-start(bf16[256,128]{1,0:T(8,128)(2,1)S(1)} %get-tuple-element.44), channel_id=1, source_target_pairs={{0,56},{8,48},{16,40},{24,32},{32,24},{40,16},{48,8},{56,0},{1,57}... | collective-permute-start | bytes 196616 | tf_op jit(solution)/shard_map/ppermute | solution.py:292
  20.2 2.1 %collective-permute-done.9.got = bf16[256,128]{1,0:T(8,128)(2,1)S(1)} collective-permute-done((bf16[256,128]{1,0:T(8,128)(2,1)S(1)}, bf16[256,128]{1,0:T(8,128)(2,1)S(1)}, u32[]{:S(2)}, u32[]{:S(2)}) %collective-permute-start.9) | collective-permute-done | bytes 65568 | tf_op jit(solution)/shard_map/ppermute | solution.py:292
  22.3 1.0 %collective-permute-start.10 = (bf16[256,128]{1,0:T(8,128)(2,1)S(1)}, bf16[256,128]{1,0:T(8,128)(2,1)S(1)}, u32[]{:S(2)}, u32[]{:S(2)}) collective-permute-start(bf16[256,128]{1,0:T(8,128)(2,1)S(1)} %get-tuple-element.47), channel_id=1, source_target_pairs={{0,64},{64,0},{128,192},{192,128},{1,65},{65,1},{129,193},{193,129... | collective-permute-start | bytes 196616 | tf_op jit(solution)/shard_map/ppermute | solution.py:292
  23.3 2.2 %collective-permute-done.10.got = bf16[256,128]{1,0:T(8,128)(2,1)S(1)} collective-permute-done((bf16[256,128]{1,0:T(8,128)(2,1)S(1)}, bf16[256,128]{1,0:T(8,128)(2,1)S(1)}, u32[]{:S(2)}, u32[]{:S(2)}) %collective-permute-start.10) | collective-permute-done | bytes 65568 | tf_op jit(solution)/shard_map/ppermute | solution.py:292
  25.5 0.3 collective-permute-start.11
  25.9 4.4 %collective-permute-done.11.got = bf16[256,128]{1,0:T(8,128)(2,1)S(1)} collective-permute-done((bf16[256,128]{1,0:T(8,128)(2,1)S(1)}, bf16[256,128]{1,0:T(8,128)(2,1)S(1)}, u32[]{:S(2)}, u32[]{:S(2)}) %collective-permute-start.11) | collective-permute-done | bytes 65568 | tf_op jit(solution)/shard_map/ppermute | solution.py:292
  30.3 1.4 %collective-permute-start.12 = (bf16[256,128]{1,0:T(8,128)(2,1)S(1)}, bf16[256,128]{1,0:T(8,128)(2,1)S(1)}, u32[]{:S(2)}, u32[]{:S(2)}) collective-permute-start(bf16[256,128]{1,0:T(8,128)(2,1)S(1)} %shard_map.75.m0), channel_id=1, source_target_pairs={{0,2},{2,4},{4,6},{6,0},{1,3},{3,5},{5,7},{7,1},{8,10},{10,12},{12... | collective-permute-start | bytes 196616 | tf_op jit(solution)/shard_map/ppermute | solution.py:292
  31.6 1.0 %collective-permute-start.13 = (bf16[256,128]{1,0:T(8,128)(2,1)S(1)}, bf16[256,128]{1,0:T(8,128)(2,1)S(1)}, u32[]{:S(2)}, u32[]{:S(2)}) collective-permute-start(bf16[256,128]{1,0:T(8,128)(2,1)S(1)} %shard_map.75.m0), channel_id=1, source_target_pairs={{0,4},{2,6},{4,0},{6,2},{1,5},{3,7},{5,1},{7,3},{8,12},{10,14},{12... | collective-permute-start | bytes 196616 | tf_op jit(solution)/shard_map/ppermute | solution.py:292
  32.6 0.0 collective-permute-done.3.kv
  32.6 0.0 collective-permute-start.14
  32.6 0.0 collective-permute-done.5.kv
  32.6 2.8 %collective-permute-start.4 = (bf16[256,512]{1,0:T(8,128)(2,1)S(1)}, bf16[256,512]{1,0:T(8,128)(2,1)S(1)}, u32[]{:S(2)}, u32[]{:S(2)}) collective-permute-start(bf16[256,512]{1,0:T(8,128)(2,1)S(1)} %slice.8), channel_id=1, source_target_pairs={{0,2},{2,4},{4,6},{6,0},{1,3},{3,5},{5,7},{7,1},{8,10},{10,12},{12... | collective-permute-start | bytes 786440 | tf_op jit(solution)/shard_map/ppermute | solution.py:292
  35.4 0.0 collective-permute-done.q_recv
  35.4 0.3 collective-permute-start.6
  35.7 0.5 shard_map.65.sig
  36.2 2.9 %shard_map.67 = (f32[2,256,2048]{2,1,0:T(8,128)S(1)}, f32[2,256,1024]{2,1,0:T(8,128)S(1)}) custom-call(bf16[256,1024]{1,0:T(8,128)(2,1)S(1)} %get-tuple-element.28.q_keep, bf16[256,2048]{1,0:T(8,128)(2,1)S(1)} %collective-permute-done.q_recv, bf16[512,512]{1,0:T(8,128)(2,1)S(1)} %get-tuple-element.30.kv), custom_call_target="tpu_custom_call" | custom-call | flops 1073741824 | bytes 4194304 | tf_op jit(solution)/shard_map/pallas_call | solution.py:32
  39.1 3.0 %shard_map.68 = (f32[2,256,2048]{2,1,0:T(8,128)S(1)}, f32[2,256,1024]{2,1,0:T(8,128)S(1)}) custom-call(bf16[256,1024]{1,0:T(8,128)(2,1)S(1)} %get-tuple-element.28.q_keep, bf16[256,2048]{1,0:T(8,128)(2,1)S(1)} %collective-permute-done.q_recv, bf16[512,512]{1,0:T(8,128)(2,1)S(1)} %collective-permute-done.3.kv, ...), custom_call_target="tpu_custom_call", output_to_operand_aliasing={{0}: (3, {}), {1}: (4, {})} | custom-call | flops 1073741824 | bytes 4194304 | tf_op jit(solution)/shard_map/pallas_call | solution.py:32
  42.2 0.0 copy-start.1
  42.2 0.0 slice-start
  42.2 3.0 %shard_map.69 = (f32[2,256,2048]{2,1,0:T(8,128)S(1)}, f32[2,256,1024]{2,1,0:T(8,128)S(1)}) custom-call(bf16[256,1024]{1,0:T(8,128)(2,1)S(1)} %get-tuple-element.28.q_keep, bf16[256,2048]{1,0:T(8,128)(2,1)S(1)} %collective-permute-done.q_recv, bf16[512,512]{1,0:T(8,128)(2,1)S(1)} %collective-permute-done.5.kv, ...), custom_call_target="tpu_custom_call", output_to_operand_aliasing={{0}: (3, {}), {1}: (4, {})} | custom-call | flops 1073741824 | bytes 4194304 | tf_op jit(solution)/shard_map/pallas_call | solution.py:32
  45.2 0.0 collective-permute-done.4.kv_a
  45.2 0.0 collective-permute-done.6.kv_b
  45.2 0.0 copy-done.1
  45.3 0.0 copy-start
  45.3 0.0 slice-start.1
  45.3 3.9 %shard_map.70.dot = f32[2,256,1024]{2,1,0:T(8,128)S(1)} custom-call(bf16[256,1024]{1,0:T(8,128)(2,1)S(1)} %get-tuple-element.28.q_keep, bf16[256,2048]{1,0:T(8,128)(2,1)S(1)} %collective-permute-done.q_recv, bf16[256,512]{1,0:T(8,128)(2,1)S(1)} %collective-permute-done.4.kv_a, bf16[256,512]{1,0:T(8,128)(2,1)S(1)} %collective-permute-done.6.kv_b, ...), custom_call_target="tpu_custom_call" | custom-call | flops 1073741824 | bytes 4194304 | tf_op jit(solution)/shard_map/pallas_call | solution.py:32
  49.2 0.0 collective-permute-done.12.m1
  49.2 0.0 collective-permute-done.13.m2
  49.2 0.0 collective-permute-done.14.m3
  49.2 0.0 copy-done
  49.3 0.6 shard_map.76
  49.8 7.5 %collective-permute-start.15 = (bf16[256,1024]{1,0:T(8,128)(2,1)S(1)}, bf16[256,1024]{1,0:T(8,128)(2,1)S(1)}, u32[]{:S(2)}, u32[]{:S(2)}) collective-permute-start(bf16[256,1024]{1,0:T(8,128)(2,1)S(1)} %shard_map.76), channel_id=1, source_target_pairs={{0,1},{1,0},{2,3},{3,2},{4,5},{5,4},{6,7},{7,6},{8,9},{9,8},{10,11... | collective-permute-start | bytes 1572872 | tf_op jit(solution)/shard_map/ppermute | solution.py:292
  57.4 0.6 shard_map.77.x
  57.9 0.0 slice-done
  57.9 0.0 slice-done.1
  58.0 1.3 %shard_map.78.begun = f32[256,2048]{1,0:T(8,128)S(1)} custom-call(bf16[256,1024]{1,0:T(8,128)(2,1)S(1)} %shard_map.77.x, bf16[2048,2048]{1,0:T(8,128)(2,1)S(1)} %bitcast.3), custom_call_target="tpu_custom_call" | custom-call | flops 1073741824 | bytes 8388608 | tf_op jit(solution)/shard_map/pallas_call | solution.py:32
  59.2 0.0 collective-permute-done.15.x
  59.2 2.1 %project_last.1 = bf16[256,2048]{1,0:T(8,128)(2,1)} custom-call(bf16[256,1024]{1,0:T(8,128)(2,1)S(1)} %collective-permute-done.15.x, f32[256,2048]{1,0:T(8,128)S(1)} %shard_map.78.begun, bf16[2048,2048]{1,0:T(8,128)(2,1)S(1)} %bitcast.3), custom_call_target="tpu_custom_call" | custom-call | flops 1073741824 | bytes 8388608 | tf_op jit(solution)/shard_map/project_last/pallas_call | solution.py:279
  (9 shorter events, 0.2 us)
Async XLA Ops:
  0.0 35.4 %collective-permute-start = (bf16[256,2048]{1,0:T(8,128)(2,1)}, bf16[256,2048]{1,0:T(8,128)(2,1)S(1)}, u32[]{:S(2)}, u32[]{:S(2)}) collective-permute-start(bf16[256,2048]{1,0:T(8,128)(2,1)} %q.1), channel_id=1, source_target_pairs={{0,1},{1,0},{2,3},{3,2},{4,5},{5,4},{6,7},{7,6},{8,9},{9,8},{10,11... | collective-permute-start | bytes 3145736 | tf_op jit(solution)/shard_map/ppermute | solution.py:292
  0.7 2.9 %collective-permute-start.1 = (bf16[256,512]{1,0:T(8,128)(2,1)}, bf16[256,512]{1,0:T(8,128)(2,1)S(1)}, u32[]{:S(2)}, u32[]{:S(2)}) collective-permute-start(bf16[256,512]{1,0:T(8,128)(2,1)} %k.1), channel_id=1, source_target_pairs={{0,1},{1,0},{2,3},{3,2},{4,5},{5,4},{6,7},{7,6},{8,9},{9,8},{10,11... | collective-permute-start | bytes 786440 | tf_op jit(solution)/shard_map/ppermute | solution.py:292
  0.7 3.2 %collective-permute-start.2 = (bf16[256,512]{1,0:T(8,128)(2,1)}, bf16[256,512]{1,0:T(8,128)(2,1)S(1)}, u32[]{:S(2)}, u32[]{:S(2)}) collective-permute-start(bf16[256,512]{1,0:T(8,128)(2,1)} %v.1), channel_id=1, source_target_pairs={{0,1},{1,0},{2,3},{3,2},{4,5},{5,4},{6,7},{7,6},{8,9},{9,8},{10,11... | collective-permute-start | bytes 786440 | tf_op jit(solution)/shard_map/ppermute | solution.py:292
  4.4 28.2 %collective-permute-start.3 = (bf16[512,512]{1,0:T(8,128)(2,1)S(1)}, bf16[512,512]{1,0:T(8,128)(2,1)S(1)}, u32[]{:S(2)}, u32[]{:S(2)}) collective-permute-start(bf16[512,512]{1,0:T(8,128)(2,1)S(1)} %get-tuple-element.30.kv), channel_id=1, source_target_pairs={{0,2},{2,4},{4,6},{6,0},{1,3},{3,5},{5,7},{7,1},{8,10},{10,12},{12... | collective-permute-start | bytes 1572872 | tf_op jit(solution)/shard_map/ppermute | solution.py:292
  4.4 28.2 %collective-permute-start.5 = (bf16[512,512]{1,0:T(8,128)(2,1)S(1)}, bf16[512,512]{1,0:T(8,128)(2,1)S(1)}, u32[]{:S(2)}, u32[]{:S(2)}) collective-permute-start(bf16[512,512]{1,0:T(8,128)(2,1)S(1)} %get-tuple-element.30.kv), channel_id=1, source_target_pairs={{0,6},{2,0},{4,2},{6,4},{1,7},{3,1},{5,3},{7,5},{8,14},{10,8},{12,... | collective-permute-start | bytes 1572872 | tf_op jit(solution)/shard_map/ppermute | solution.py:292
  5.9 3.6 %collective-permute-start.7 = (bf16[256,128]{1,0:T(8,128)(2,1)S(1)}, bf16[256,128]{1,0:T(8,128)(2,1)S(1)}, u32[]{:S(2)}, u32[]{:S(2)}) collective-permute-start(bf16[256,128]{1,0:T(8,128)(2,1)S(1)} %get-tuple-element.38), channel_id=1, source_target_pairs={{0,8},{8,0},{16,24},{24,16},{32,40},{40,32},{48,56},{56,48},{1,9},... | collective-permute-start | bytes 196616 | tf_op jit(solution)/shard_map/ppermute | solution.py:292
  9.5 5.0 %collective-permute-start.8 = (bf16[256,128]{1,0:T(8,128)(2,1)S(1)}, bf16[256,128]{1,0:T(8,128)(2,1)S(1)}, u32[]{:S(2)}, u32[]{:S(2)}) collective-permute-start(bf16[256,128]{1,0:T(8,128)(2,1)S(1)} %get-tuple-element.41), channel_id=1, source_target_pairs={{0,16},{8,24},{16,0},{24,8},{32,48},{40,56},{48,32},{56,40},{1,17}... | collective-permute-start | bytes 196616 | tf_op jit(solution)/shard_map/ppermute | solution.py:292
  14.6 7.7 %collective-permute-start.9 = (bf16[256,128]{1,0:T(8,128)(2,1)S(1)}, bf16[256,128]{1,0:T(8,128)(2,1)S(1)}, u32[]{:S(2)}, u32[]{:S(2)}) collective-permute-start(bf16[256,128]{1,0:T(8,128)(2,1)S(1)} %get-tuple-element.44), channel_id=1, source_target_pairs={{0,56},{8,48},{16,40},{24,32},{32,24},{40,16},{48,8},{56,0},{1,57}... | collective-permute-start | bytes 196616 | tf_op jit(solution)/shard_map/ppermute | solution.py:292
  22.3 3.2 %collective-permute-start.10 = (bf16[256,128]{1,0:T(8,128)(2,1)S(1)}, bf16[256,128]{1,0:T(8,128)(2,1)S(1)}, u32[]{:S(2)}, u32[]{:S(2)}) collective-permute-start(bf16[256,128]{1,0:T(8,128)(2,1)S(1)} %get-tuple-element.47), channel_id=1, source_target_pairs={{0,64},{64,0},{128,192},{192,128},{1,65},{65,1},{129,193},{193,129... | collective-permute-start | bytes 196616 | tf_op jit(solution)/shard_map/ppermute | solution.py:292
  25.5 4.7 %collective-permute-start.11 = (bf16[256,128]{1,0:T(8,128)(2,1)S(1)}, bf16[256,128]{1,0:T(8,128)(2,1)S(1)}, u32[]{:S(2)}, u32[]{:S(2)}) collective-permute-start(bf16[256,128]{1,0:T(8,128)(2,1)S(1)} %get-tuple-element.50), channel_id=1, source_target_pairs={{0,128},{64,192},{128,0},{192,64},{1,129},{65,193},{129,1},{193,65... | collective-permute-start | bytes 196616 | tf_op jit(solution)/shard_map/ppermute | solution.py:292
  30.3 18.9 %collective-permute-start.12 = (bf16[256,128]{1,0:T(8,128)(2,1)S(1)}, bf16[256,128]{1,0:T(8,128)(2,1)S(1)}, u32[]{:S(2)}, u32[]{:S(2)}) collective-permute-start(bf16[256,128]{1,0:T(8,128)(2,1)S(1)} %shard_map.75.m0), channel_id=1, source_target_pairs={{0,2},{2,4},{4,6},{6,0},{1,3},{3,5},{5,7},{7,1},{8,10},{10,12},{12... | collective-permute-start | bytes 196616 | tf_op jit(solution)/shard_map/ppermute | solution.py:292
  31.6 17.6 %collective-permute-start.13 = (bf16[256,128]{1,0:T(8,128)(2,1)S(1)}, bf16[256,128]{1,0:T(8,128)(2,1)S(1)}, u32[]{:S(2)}, u32[]{:S(2)}) collective-permute-start(bf16[256,128]{1,0:T(8,128)(2,1)S(1)} %shard_map.75.m0), channel_id=1, source_target_pairs={{0,4},{2,6},{4,0},{6,2},{1,5},{3,7},{5,1},{7,3},{8,12},{10,14},{12... | collective-permute-start | bytes 196616 | tf_op jit(solution)/shard_map/ppermute | solution.py:292
  32.6 16.6 %collective-permute-start.14 = (bf16[256,128]{1,0:T(8,128)(2,1)S(1)}, bf16[256,128]{1,0:T(8,128)(2,1)S(1)}, u32[]{:S(2)}, u32[]{:S(2)}) collective-permute-start(bf16[256,128]{1,0:T(8,128)(2,1)S(1)} %shard_map.75.m0), channel_id=1, source_target_pairs={{0,6},{2,0},{4,2},{6,4},{1,7},{3,1},{5,3},{7,5},{8,14},{10,8},{12,... | collective-permute-start | bytes 196616 | tf_op jit(solution)/shard_map/ppermute | solution.py:292
  32.6 12.6 %collective-permute-start.4 = (bf16[256,512]{1,0:T(8,128)(2,1)S(1)}, bf16[256,512]{1,0:T(8,128)(2,1)S(1)}, u32[]{:S(2)}, u32[]{:S(2)}) collective-permute-start(bf16[256,512]{1,0:T(8,128)(2,1)S(1)} %slice.8), channel_id=1, source_target_pairs={{0,2},{2,4},{4,6},{6,0},{1,3},{3,5},{5,7},{7,1},{8,10},{10,12},{12... | collective-permute-start | bytes 786440 | tf_op jit(solution)/shard_map/ppermute | solution.py:292
  35.4 9.8 %collective-permute-start.6 = (bf16[256,512]{1,0:T(8,128)(2,1)S(1)}, bf16[256,512]{1,0:T(8,128)(2,1)S(1)}, u32[]{:S(2)}, u32[]{:S(2)}) collective-permute-start(bf16[256,512]{1,0:T(8,128)(2,1)S(1)} %slice.9), channel_id=1, source_target_pairs={{0,6},{2,0},{4,2},{6,4},{1,7},{3,1},{5,3},{7,5},{8,14},{10,8},{12,... | collective-permute-start | bytes 786440 | tf_op jit(solution)/shard_map/ppermute | solution.py:292
  42.2 3.1 %copy-start.1 = (f32[2048]{0:T(1024)S(1)}, f32[2048]{0:T(1024)}, u32[]{:S(2)}) copy-start(f32[2048]{0:T(1024)} %param.10) | copy-start | bytes 24580
  42.2 15.8 %slice-start = ((s8[8388608]{0:T(1024)(128)(4,1)}), s8[4194304]{0:T(1024)(128)(4,1)S(1)}, s32[]{:S(2)}) async-start(s8[8388608]{0:T(1024)(128)(4,1)} %bitcast.2), calls=%async_computation | async-start | bytes 8388608
  45.3 4.0 %copy-start = (f32[2048]{0:T(1024)S(1)}, f32[2048]{0:T(1024)}, u32[]{:S(2)}) copy-start(f32[2048]{0:T(1024)} %param.9) | copy-start | bytes 24580
  45.3 12.7 %slice-start.1 = ((s8[8388608]{0:T(1024)(128)(4,1)}), s8[4194304]{0:T(1024)(128)(4,1)S(1)}, s32[]{:S(2)}) async-start(s8[8388608]{0:T(1024)(128)(4,1)} %bitcast.2), calls=%async_computation.1 | async-start | bytes 8388608
  49.8 9.4 %collective-permute-start.15 = (bf16[256,1024]{1,0:T(8,128)(2,1)S(1)}, bf16[256,1024]{1,0:T(8,128)(2,1)S(1)}, u32[]{:S(2)}, u32[]{:S(2)}) collective-permute-start(bf16[256,1024]{1,0:T(8,128)(2,1)S(1)} %shard_map.76), channel_id=1, source_target_pairs={{0,1},{1,0},{2,3},{3,2},{4,5},{5,4},{6,7},{7,6},{8,9},{9,8},{10,11... | collective-permute-start | bytes 1572872 | tf_op jit(solution)/shard_map/ppermute | solution.py:292

commit v3 on v2

--- a/solution.py
+++ b/solution.py
@@ -186,7 +186,7 @@
     return x * (0.5 * lax.rsqrt(jnp.mean(x * x, axis=-1, keepdims=True) + 1e-06)) * gain
 
 
-def last_kernel(q_keep, q_recv, kv_a, kv_b, ext, top, gain, out, kv, v_ones):
+def last_kernel(q_keep, q_recv, kv, ext, top, gain, out, v_ones):
     y, c = lax.axis_index("y"), lax.axis_index("c")
     own = pl.multiple_of(c * HEADS, HEADS)
 
@@ -197,9 +197,6 @@
 
     @pl.when(y >= 2)
     def _():
-        half = kv_a.shape[0]
-        kv[:half, :] = kv_a[...]
-        kv[half:, :] = kv_b[...]
         for b, h, r, cols, wide, new, total in fold_chunk((q_keep, q_recv), kv, v_ones, ext, top):
             put(b, h, r, cols, total)
 
@@ -210,13 +207,13 @@
 
 
 def attend_last(q_keep, q_recv, far, ext, top, gain):
-    rows, keys, width = q_keep.shape[0], 2 * far[0].shape[0], far[0].shape[1]
+    rows, keys = q_keep.shape[0], far.shape[0]
     count = 2 * HEADS * rows * keys
     outs = [((2, rows, HEADS * HEAD), F32)]
     return kernel_call(
-        last_kernel, outs, (q_keep, q_recv, *far, ext, top, gain), 20,
+        last_kernel, outs, (q_keep, q_recv, far, ext, top, gain), 20,
         4 * count * HEAD, 2**22, count,
-        scratch_shapes=[pltpu.VMEM((keys, width), BF16), pltpu.VMEM((2, keys, 2 * HEAD), BF16)],
+        scratch_shapes=[pltpu.VMEM((2, keys, 2 * HEAD), BF16)],
     )[0]
 
 
@@ -316,7 +313,7 @@
         ("sz", 1, [i ^ 2 for i in range(8)], "z2"),
         ("sz", 2, [7 - i for i in range(8)], "z3"),
         ("sx", 0, [i ^ 1 for i in range(4)], "x1"),
-        ("sx", 1, [i ^ 2 for i in range(4)], "x2"),
+        ("sx", 1, [3 - i for i in range(4)], "x2"),
     )
     for axis, level, partner, name in steps:
         last = name == "x2"
@@ -339,10 +336,9 @@
     kv, total, sent = part(kv_own, k_recv, v_recv)
     left = shift(kv, "y", 1, 4)
     right = shift(kv, "y", 3, 4)
-    half = kv.shape[0] // 2
-    far = shift(left[:half], "y", 1, 4), shift(right[half:], "y", 3, 4)
+    far = permute(kv, "y", [i ^ 2 for i in range(4)])
     mine = earlier_memory(total, sent)
-    memory = [mine] + [shift(mine, "y", step, 4) for step in (1, 2, 3)]
+    memory = [mine] + [permute(mine, "y", [i ^ n for i in range(4)]) for n in (1, 2, 3)]
     ext, top = attend_first(q_own, q_recv, kv)
     ext, top = attend_next(1, q_own, q_recv, left, ext, top)
     ext, top = attend_next(3, q_own, q_recv, right, ext, top)

time: 61.7 us -> 57.4 us (0.930)
  the two profiles are of different devices: /device:TPU:29 before, /device:TPU:31 now
where the time goes in v3:
time: 57.4 us; the launch traced here: 57.3 us
  starting transfers between devices  25.5 us (44%)
  Pallas kernels  19.4 us (34%)
  waiting for transfers between devices  11.8 us (21%)
    ppermute x15, starting transfers between devices, permute(): return lax.ppermute(x, axis, list(enumerate(partner)))  25.5 us
    pallas_call x15, Pallas kernels, kernel_call(): pl.pallas_call(body, out_shape=[pltpu.VMEM(shape, dtype) for shape, dtype...  17.3 us
    ppermute x15, waiting for transfers between devices, permute(): return lax.ppermute(x, axis, list(enumerate(partner)))  11.8 us
    pallas_call x1, Pallas kernels, project_last(): pl.pallas_call(project_last_kernel, out_shape=pltpu.HBM(shape, BF16), in_...  2.12 us
  transfers between devices with their start and end apart: 15, of which 6 were waited for; matrix products, arithmetic and copies ran while one was open for 0% of the time, Pallas kernels for 29%

profile of v3, /device:TPU:31, one launch (start us, length us, event | category | flops | bytes accessed | tf_op | source)
XLA Modules:
  0.0 57.3 jit_solution(3791911088041279088)
XLA Ops:
  0.0 0.7 %collective-permute-start = (bf16[256,2048]{1,0:T(8,128)(2,1)}, bf16[256,2048]{1,0:T(8,128)(2,1)S(1)}, u32[]{:S(2)}, u32[]{:S(2)}) collective-permute-start(bf16[256,2048]{1,0:T(8,128)(2,1)} %q.1), channel_id=1, source_target_pairs={{0,1},{1,0},{2,3},{3,2},{4,5},{5,4},{6,7},{7,6},{8,9},{9,8},{10,11... | collective-permute-start | bytes 3145736 | tf_op jit(solution)/shard_map/ppermute | solution.py:289
  0.7 0.0 collective-permute-start.1
  0.7 0.5 collective-permute-start.2
  1.2 1.2 %shard_map.64 = (bf16[256,512]{1,0:T(8,128)(2,1)S(1)}, bf16[256,1024]{1,0:T(8,128)(2,1)S(1)}) custom-call(bf16[256,512]{1,0:T(8,128)(2,1)} %k.1, bf16[256,512]{1,0:T(8,128)(2,1)} %v.1, bf16[256,2048]{1,0:T(8,128)(2,1)} %q.1), custom_call_target="tpu_custom_call" | custom-call | bytes 2097152 | tf_op jit(solution)/shard_map/pallas_call | solution.py:32
  2.4 1.2 %collective-permute-done.1.k_recv = bf16[256,512]{1,0:T(8,128)(2,1)S(1)} collective-permute-done((bf16[256,512]{1,0:T(8,128)(2,1)}, bf16[256,512]{1,0:T(8,128)(2,1)S(1)}, u32[]{:S(2)}, u32[]{:S(2)}) %collective-permute-start.1) | collective-permute-done | bytes 262176 | tf_op jit(solution)/shard_map/ppermute | solution.py:289
  3.5 0.4 collective-permute-done.2.v_recv
  3.9 0.4 shard_map.66
  4.4 0.1 collective-permute-start.5
  4.4 1.7 %collective-permute-start.6 = (bf16[256,128]{1,0:T(8,128)(2,1)S(1)}, bf16[256,128]{1,0:T(8,128)(2,1)S(1)}, u32[]{:S(2)}, u32[]{:S(2)}) collective-permute-start(bf16[256,128]{1,0:T(8,128)(2,1)S(1)} %get-tuple-element.38), channel_id=1, source_target_pairs={{0,8},{8,0},{16,24},{24,16},{32,40},{40,32},{48,56},{56,48},{1,9},... | collective-permute-start | bytes 196616 | tf_op jit(solution)/shard_map/ppermute | solution.py:289
  6.2 1.4 %collective-permute-start.4 = (bf16[512,512]{1,0:T(8,128)(2,1)S(1)}, bf16[512,512]{1,0:T(8,128)(2,1)S(1)}, u32[]{:S(2)}, u32[]{:S(2)}) collective-permute-start(bf16[512,512]{1,0:T(8,128)(2,1)S(1)} %get-tuple-element.30.kv), channel_id=1, source_target_pairs={{0,6},{2,0},{4,2},{6,4},{1,7},{3,1},{5,3},{7,5},{8,14},{10,8},{12,... | collective-permute-start | bytes 1572872 | tf_op jit(solution)/shard_map/ppermute | solution.py:289
  7.5 0.6 %collective-permute-done.6.got = bf16[256,128]{1,0:T(8,128)(2,1)S(1)} collective-permute-done((bf16[256,128]{1,0:T(8,128)(2,1)S(1)}, bf16[256,128]{1,0:T(8,128)(2,1)S(1)}, u32[]{:S(2)}, u32[]{:S(2)}) %collective-permute-start.6) | collective-permute-done | bytes 65568 | tf_op jit(solution)/shard_map/ppermute | solution.py:289
  8.2 3.1 %collective-permute-start.7 = (bf16[256,128]{1,0:T(8,128)(2,1)S(1)}, bf16[256,128]{1,0:T(8,128)(2,1)S(1)}, u32[]{:S(2)}, u32[]{:S(2)}) collective-permute-start(bf16[256,128]{1,0:T(8,128)(2,1)S(1)} %get-tuple-element.41), channel_id=1, source_target_pairs={{0,16},{8,24},{16,0},{24,8},{32,48},{40,56},{48,32},{56,40},{1,17}... | collective-permute-start | bytes 196616 | tf_op jit(solution)/shard_map/ppermute | solution.py:289
  11.3 2.1 %collective-permute-start.3 = (bf16[512,512]{1,0:T(8,128)(2,1)S(1)}, bf16[512,512]{1,0:T(8,128)(2,1)S(1)}, u32[]{:S(2)}, u32[]{:S(2)}) collective-permute-start(bf16[512,512]{1,0:T(8,128)(2,1)S(1)} %get-tuple-element.30.kv), channel_id=1, source_target_pairs={{0,4},{2,6},{4,0},{6,2},{1,5},{3,7},{5,1},{7,3},{8,12},{10,14},{12... | collective-permute-start | bytes 1572872 | tf_op jit(solution)/shard_map/ppermute | solution.py:289
  13.4 0.0 collective-permute-done.7.got
  13.4 5.1 %collective-permute-start.8 = (bf16[256,128]{1,0:T(8,128)(2,1)S(1)}, bf16[256,128]{1,0:T(8,128)(2,1)S(1)}, u32[]{:S(2)}, u32[]{:S(2)}) collective-permute-start(bf16[256,128]{1,0:T(8,128)(2,1)S(1)} %get-tuple-element.44), channel_id=1, source_target_pairs={{0,56},{8,48},{16,40},{24,32},{32,24},{40,16},{48,8},{56,0},{1,57}... | collective-permute-start | bytes 196616 | tf_op jit(solution)/shard_map/ppermute | solution.py:289
  18.5 2.4 %collective-permute-done.8.got = bf16[256,128]{1,0:T(8,128)(2,1)S(1)} collective-permute-done((bf16[256,128]{1,0:T(8,128)(2,1)S(1)}, bf16[256,128]{1,0:T(8,128)(2,1)S(1)}, u32[]{:S(2)}, u32[]{:S(2)}) %collective-permute-start.8) | collective-permute-done | bytes 65568 | tf_op jit(solution)/shard_map/ppermute | solution.py:289
  21.0 0.6 %collective-permute-start.9 = (bf16[256,128]{1,0:T(8,128)(2,1)S(1)}, bf16[256,128]{1,0:T(8,128)(2,1)S(1)}, u32[]{:S(2)}, u32[]{:S(2)}) collective-permute-start(bf16[256,128]{1,0:T(8,128)(2,1)S(1)} %get-tuple-element.47), channel_id=1, source_target_pairs={{0,64},{64,0},{128,192},{192,128},{1,65},{65,1},{129,193},{193,129... | collective-permute-start | bytes 196616 | tf_op jit(solution)/shard_map/ppermute | solution.py:289
  21.6 2.9 %collective-permute-done.9.got = bf16[256,128]{1,0:T(8,128)(2,1)S(1)} collective-permute-done((bf16[256,128]{1,0:T(8,128)(2,1)S(1)}, bf16[256,128]{1,0:T(8,128)(2,1)S(1)}, u32[]{:S(2)}, u32[]{:S(2)}) %collective-permute-start.9) | collective-permute-done | bytes 65568 | tf_op jit(solution)/shard_map/ppermute | solution.py:289
  24.5 0.3 collective-permute-start.10
  24.8 4.4 %collective-permute-done.10.got = bf16[256,128]{1,0:T(8,128)(2,1)S(1)} collective-permute-done((bf16[256,128]{1,0:T(8,128)(2,1)S(1)}, bf16[256,128]{1,0:T(8,128)(2,1)S(1)}, u32[]{:S(2)}, u32[]{:S(2)}) %collective-permute-start.10) | collective-permute-done | bytes 65568 | tf_op jit(solution)/shard_map/ppermute | solution.py:289
  29.2 1.1 %collective-permute-start.11 = (bf16[256,128]{1,0:T(8,128)(2,1)S(1)}, bf16[256,128]{1,0:T(8,128)(2,1)S(1)}, u32[]{:S(2)}, u32[]{:S(2)}) collective-permute-start(bf16[256,128]{1,0:T(8,128)(2,1)S(1)} %shard_map.75.m0), channel_id=1, source_target_pairs={{0,2},{2,0},{4,6},{6,4},{1,3},{3,1},{5,7},{7,5},{8,10},{10,8},{12,... | collective-permute-start | bytes 196616 | tf_op jit(solution)/shard_map/ppermute | solution.py:289
  30.3 0.0 collective-permute-done.q_recv
  30.3 1.6 %collective-permute-start.12 = (bf16[256,128]{1,0:T(8,128)(2,1)S(1)}, bf16[256,128]{1,0:T(8,128)(2,1)S(1)}, u32[]{:S(2)}, u32[]{:S(2)}) collective-permute-start(bf16[256,128]{1,0:T(8,128)(2,1)S(1)} %shard_map.75.m0), channel_id=1, source_target_pairs={{0,4},{2,6},{4,0},{6,2},{1,5},{3,7},{5,1},{7,3},{8,12},{10,14},{12... | collective-permute-start | bytes 196616 | tf_op jit(solution)/shard_map/ppermute | solution.py:289
  31.9 0.5 shard_map.65.sig
  32.4 2.9 %shard_map.67 = (f32[2,256,2048]{2,1,0:T(8,128)S(1)}, f32[2,256,1024]{2,1,0:T(8,128)S(1)}) custom-call(bf16[256,1024]{1,0:T(8,128)(2,1)S(1)} %get-tuple-element.28.q_keep, bf16[256,2048]{1,0:T(8,128)(2,1)S(1)} %collective-permute-done.q_recv, bf16[512,512]{1,0:T(8,128)(2,1)S(1)} %get-tuple-element.30.kv), custom_call_target="tpu_custom_call" | custom-call | flops 1073741824 | bytes 4194304 | tf_op jit(solution)/shard_map/pallas_call | solution.py:32
  35.3 0.0 collective-permute-done.5.kv
  35.3 1.6 %collective-permute-start.13 = (bf16[256,128]{1,0:T(8,128)(2,1)S(1)}, bf16[256,128]{1,0:T(8,128)(2,1)S(1)}, u32[]{:S(2)}, u32[]{:S(2)}) collective-permute-start(bf16[256,128]{1,0:T(8,128)(2,1)S(1)} %shard_map.75.m0), channel_id=1, source_target_pairs={{0,6},{2,4},{4,2},{6,0},{1,7},{3,5},{5,3},{7,1},{8,14},{10,12},{12... | collective-permute-start | bytes 196616 | tf_op jit(solution)/shard_map/ppermute | solution.py:289
  36.9 3.0 %shard_map.68 = (f32[2,256,2048]{2,1,0:T(8,128)S(1)}, f32[2,256,1024]{2,1,0:T(8,128)S(1)}) custom-call(bf16[256,1024]{1,0:T(8,128)(2,1)S(1)} %get-tuple-element.28.q_keep, bf16[256,2048]{1,0:T(8,128)(2,1)S(1)} %collective-permute-done.q_recv, bf16[512,512]{1,0:T(8,128)(2,1)S(1)} %collective-permute-done.5.kv, ...), custom_call_target="tpu_custom_call", output_to_operand_aliasing={{0}: (3, {}), {1}: (4, {})} | custom-call | flops 1073741824 | bytes 4194304 | tf_op jit(solution)/shard_map/pallas_call | solution.py:32
  39.9 0.0 collective-permute-done.4.kv
  39.9 0.0 copy-start.1
  39.9 0.0 slice-start
  39.9 3.0 %shard_map.69 = (f32[2,256,2048]{2,1,0:T(8,128)S(1)}, f32[2,256,1024]{2,1,0:T(8,128)S(1)}) custom-call(bf16[256,1024]{1,0:T(8,128)(2,1)S(1)} %get-tuple-element.28.q_keep, bf16[256,2048]{1,0:T(8,128)(2,1)S(1)} %collective-permute-done.q_recv, bf16[512,512]{1,0:T(8,128)(2,1)S(1)} %collective-permute-done.4.kv, ...), custom_call_target="tpu_custom_call", output_to_operand_aliasing={{0}: (3, {}), {1}: (4, {})} | custom-call | flops 1073741824 | bytes 4194304 | tf_op jit(solution)/shard_map/pallas_call | solution.py:32
  43.0 0.0 collective-permute-done.3.kv
  43.0 0.0 copy-done.1
  43.0 0.0 copy-start
  43.0 0.0 slice-start.1
  43.0 3.7 %shard_map.70.dot = f32[2,256,1024]{2,1,0:T(8,128)S(1)} custom-call(bf16[256,1024]{1,0:T(8,128)(2,1)S(1)} %get-tuple-element.28.q_keep, bf16[256,2048]{1,0:T(8,128)(2,1)S(1)} %collective-permute-done.q_recv, bf16[512,512]{1,0:T(8,128)(2,1)S(1)} %collective-permute-done.3.kv, f32[2,256,2048]{2,1,0:T(8,128)S(1)} %get-tuple-element.35.ext, ...), custom_call_target="tpu_custom_call" | custom-call | flops 1073741824 | bytes 4194304 | tf_op jit(solution)/shard_map/pallas_call | solution.py:32
  46.7 0.0 collective-permute-done.11.m1
  46.7 0.0 collective-permute-done.12.m2
  46.7 0.0 collective-permute-done.13.m3
  46.8 0.0 copy-done
  46.8 0.6 %shard_map.76 = bf16[256,1024]{1,0:T(8,128)(2,1)S(1)} custom-call(bf16[2,256,1024]{2,1,0:T(8,128)(2,1)S(1)} %shard_map.65.sig, f32[2,256,1024]{2,1,0:T(8,128)S(1)} %shard_map.70.dot, bf16[256,128]{1,0:T(8,128)(2,1)S(1)} %shard_map.75.m0, bf16[256,128]{1,0:T(8,128)(2,1)S(1)} %collective-permute-done.11.m1, bf16[256,128]{1,0:T(8,128)(2,1)S(1)} %collective-permute-done.12.m2, ...), custom_call_target="tpu_custom_call" | custom-call | flops 67108864 | bytes 2097152 | tf_op jit(solution)/shard_map/pallas_call | solution.py:32
  47.3 5.8 %collective-permute-start.14 = (bf16[256,1024]{1,0:T(8,128)(2,1)S(1)}, bf16[256,1024]{1,0:T(8,128)(2,1)S(1)}, u32[]{:S(2)}, u32[]{:S(2)}) collective-permute-start(bf16[256,1024]{1,0:T(8,128)(2,1)S(1)} %shard_map.76), channel_id=1, source_target_pairs={{0,1},{1,0},{2,3},{3,2},{4,5},{5,4},{6,7},{7,6},{8,9},{9,8},{10,11... | collective-permute-start | bytes 1572872 | tf_op jit(solution)/shard_map/ppermute | solution.py:289
  53.1 0.6 shard_map.77.x
  53.7 0.0 slice-done
  53.7 0.0 slice-done.1
  53.7 1.3 %shard_map.78.begun = f32[256,2048]{1,0:T(8,128)S(1)} custom-call(bf16[256,1024]{1,0:T(8,128)(2,1)S(1)} %shard_map.77.x, bf16[2048,2048]{1,0:T(8,128)(2,1)S(1)} %bitcast.3), custom_call_target="tpu_custom_call" | custom-call | flops 1073741824 | bytes 8388608 | tf_op jit(solution)/shard_map/pallas_call | solution.py:32
  55.0 0.0 collective-permute-done.14.x
  55.0 2.1 %project_last.1 = bf16[256,2048]{1,0:T(8,128)(2,1)} custom-call(bf16[256,1024]{1,0:T(8,128)(2,1)S(1)} %collective-permute-done.14.x, f32[256,2048]{1,0:T(8,128)S(1)} %shard_map.78.begun, bf16[2048,2048]{1,0:T(8,128)(2,1)S(1)} %bitcast.3), custom_call_target="tpu_custom_call" | custom-call | flops 1073741824 | bytes 8388608 | tf_op jit(solution)/shard_map/project_last/pallas_call | solution.py:276
  (7 shorter events, 0.2 us)
Async XLA Ops:
  0.0 30.3 %collective-permute-start = (bf16[256,2048]{1,0:T(8,128)(2,1)}, bf16[256,2048]{1,0:T(8,128)(2,1)S(1)}, u32[]{:S(2)}, u32[]{:S(2)}) collective-permute-start(bf16[256,2048]{1,0:T(8,128)(2,1)} %q.1), channel_id=1, source_target_pairs={{0,1},{1,0},{2,3},{3,2},{4,5},{5,4},{6,7},{7,6},{8,9},{9,8},{10,11... | collective-permute-start | bytes 3145736 | tf_op jit(solution)/shard_map/ppermute | solution.py:289
  0.7 2.9 %collective-permute-start.1 = (bf16[256,512]{1,0:T(8,128)(2,1)}, bf16[256,512]{1,0:T(8,128)(2,1)S(1)}, u32[]{:S(2)}, u32[]{:S(2)}) collective-permute-start(bf16[256,512]{1,0:T(8,128)(2,1)} %k.1), channel_id=1, source_target_pairs={{0,1},{1,0},{2,3},{3,2},{4,5},{5,4},{6,7},{7,6},{8,9},{9,8},{10,11... | collective-permute-start | bytes 786440 | tf_op jit(solution)/shard_map/ppermute | solution.py:289
  0.7 3.2 %collective-permute-start.2 = (bf16[256,512]{1,0:T(8,128)(2,1)}, bf16[256,512]{1,0:T(8,128)(2,1)S(1)}, u32[]{:S(2)}, u32[]{:S(2)}) collective-permute-start(bf16[256,512]{1,0:T(8,128)(2,1)} %v.1), channel_id=1, source_target_pairs={{0,1},{1,0},{2,3},{3,2},{4,5},{5,4},{6,7},{7,6},{8,9},{9,8},{10,11... | collective-permute-start | bytes 786440 | tf_op jit(solution)/shard_map/ppermute | solution.py:289
  4.4 30.9 %collective-permute-start.5 = (bf16[512,512]{1,0:T(8,128)(2,1)S(1)}, bf16[512,512]{1,0:T(8,128)(2,1)S(1)}, u32[]{:S(2)}, u32[]{:S(2)}) collective-permute-start(bf16[512,512]{1,0:T(8,128)(2,1)S(1)} %get-tuple-element.30.kv), channel_id=1, source_target_pairs={{0,2},{2,4},{4,6},{6,0},{1,3},{3,5},{5,7},{7,1},{8,10},{10,12},{12... | collective-permute-start | bytes 1572872 | tf_op jit(solution)/shard_map/ppermute | solution.py:289
  4.4 3.7 %collective-permute-start.6 = (bf16[256,128]{1,0:T(8,128)(2,1)S(1)}, bf16[256,128]{1,0:T(8,128)(2,1)S(1)}, u32[]{:S(2)}, u32[]{:S(2)}) collective-permute-start(bf16[256,128]{1,0:T(8,128)(2,1)S(1)} %get-tuple-element.38), channel_id=1, source_target_pairs={{0,8},{8,0},{16,24},{24,16},{32,40},{40,32},{48,56},{56,48},{1,9},... | collective-permute-start | bytes 196616 | tf_op jit(solution)/shard_map/ppermute | solution.py:289
  6.2 33.7 %collective-permute-start.4 = (bf16[512,512]{1,0:T(8,128)(2,1)S(1)}, bf16[512,512]{1,0:T(8,128)(2,1)S(1)}, u32[]{:S(2)}, u32[]{:S(2)}) collective-permute-start(bf16[512,512]{1,0:T(8,128)(2,1)S(1)} %get-tuple-element.30.kv), channel_id=1, source_target_pairs={{0,6},{2,0},{4,2},{6,4},{1,7},{3,1},{5,3},{7,5},{8,14},{10,8},{12,... | collective-permute-start | bytes 1572872 | tf_op jit(solution)/shard_map/ppermute | solution.py:289
  8.2 5.2 %collective-permute-start.7 = (bf16[256,128]{1,0:T(8,128)(2,1)S(1)}, bf16[256,128]{1,0:T(8,128)(2,1)S(1)}, u32[]{:S(2)}, u32[]{:S(2)}) collective-permute-start(bf16[256,128]{1,0:T(8,128)(2,1)S(1)} %get-tuple-element.41), channel_id=1, source_target_pairs={{0,16},{8,24},{16,0},{24,8},{32,48},{40,56},{48,32},{56,40},{1,17}... | collective-permute-start | bytes 196616 | tf_op jit(solution)/shard_map/ppermute | solution.py:289
  11.3 31.7 %collective-permute-start.3 = (bf16[512,512]{1,0:T(8,128)(2,1)S(1)}, bf16[512,512]{1,0:T(8,128)(2,1)S(1)}, u32[]{:S(2)}, u32[]{:S(2)}) collective-permute-start(bf16[512,512]{1,0:T(8,128)(2,1)S(1)} %get-tuple-element.30.kv), channel_id=1, source_target_pairs={{0,4},{2,6},{4,0},{6,2},{1,5},{3,7},{5,1},{7,3},{8,12},{10,14},{12... | collective-permute-start | bytes 1572872 | tf_op jit(solution)/shard_map/ppermute | solution.py:289
  13.4 7.5 %collective-permute-start.8 = (bf16[256,128]{1,0:T(8,128)(2,1)S(1)}, bf16[256,128]{1,0:T(8,128)(2,1)S(1)}, u32[]{:S(2)}, u32[]{:S(2)}) collective-permute-start(bf16[256,128]{1,0:T(8,128)(2,1)S(1)} %get-tuple-element.44), channel_id=1, source_target_pairs={{0,56},{8,48},{16,40},{24,32},{32,24},{40,16},{48,8},{56,0},{1,57}... | collective-permute-start | bytes 196616 | tf_op jit(solution)/shard_map/ppermute | solution.py:289
  21.0 3.5 %collective-permute-start.9 = (bf16[256,128]{1,0:T(8,128)(2,1)S(1)}, bf16[256,128]{1,0:T(8,128)(2,1)S(1)}, u32[]{:S(2)}, u32[]{:S(2)}) collective-permute-start(bf16[256,128]{1,0:T(8,128)(2,1)S(1)} %get-tuple-element.47), channel_id=1, source_target_pairs={{0,64},{64,0},{128,192},{192,128},{1,65},{65,1},{129,193},{193,129... | collective-permute-start | bytes 196616 | tf_op jit(solution)/shard_map/ppermute | solution.py:289
  24.5 4.7 %collective-permute-start.10 = (bf16[256,128]{1,0:T(8,128)(2,1)S(1)}, bf16[256,128]{1,0:T(8,128)(2,1)S(1)}, u32[]{:S(2)}, u32[]{:S(2)}) collective-permute-start(bf16[256,128]{1,0:T(8,128)(2,1)S(1)} %get-tuple-element.50), channel_id=1, source_target_pairs={{0,192},{64,128},{128,64},{192,0},{1,193},{65,129},{129,65},{193,1... | collective-permute-start | bytes 196616 | tf_op jit(solution)/shard_map/ppermute | solution.py:289
  29.2 17.5 %collective-permute-start.11 = (bf16[256,128]{1,0:T(8,128)(2,1)S(1)}, bf16[256,128]{1,0:T(8,128)(2,1)S(1)}, u32[]{:S(2)}, u32[]{:S(2)}) collective-permute-start(bf16[256,128]{1,0:T(8,128)(2,1)S(1)} %shard_map.75.m0), channel_id=1, source_target_pairs={{0,2},{2,0},{4,6},{6,4},{1,3},{3,1},{5,7},{7,5},{8,10},{10,8},{12,... | collective-permute-start | bytes 196616 | tf_op jit(solution)/shard_map/ppermute | solution.py:289
  30.3 16.4 %collective-permute-start.12 = (bf16[256,128]{1,0:T(8,128)(2,1)S(1)}, bf16[256,128]{1,0:T(8,128)(2,1)S(1)}, u32[]{:S(2)}, u32[]{:S(2)}) collective-permute-start(bf16[256,128]{1,0:T(8,128)(2,1)S(1)} %shard_map.75.m0), channel_id=1, source_target_pairs={{0,4},{2,6},{4,0},{6,2},{1,5},{3,7},{5,1},{7,3},{8,12},{10,14},{12... | collective-permute-start | bytes 196616 | tf_op jit(solution)/shard_map/ppermute | solution.py:289
  35.3 11.5 %collective-permute-start.13 = (bf16[256,128]{1,0:T(8,128)(2,1)S(1)}, bf16[256,128]{1,0:T(8,128)(2,1)S(1)}, u32[]{:S(2)}, u32[]{:S(2)}) collective-permute-start(bf16[256,128]{1,0:T(8,128)(2,1)S(1)} %shard_map.75.m0), channel_id=1, source_target_pairs={{0,6},{2,4},{4,2},{6,0},{1,7},{3,5},{5,3},{7,1},{8,14},{10,12},{12... | collective-permute-start | bytes 196616 | tf_op jit(solution)/shard_map/ppermute | solution.py:289
  39.9 3.1 %copy-start.1 = (f32[2048]{0:T(1024)S(1)}, f32[2048]{0:T(1024)}, u32[]{:S(2)}) copy-start(f32[2048]{0:T(1024)} %param.10) | copy-start | bytes 24580
  39.9 13.8 %slice-start = ((s8[8388608]{0:T(1024)(128)(4,1)}), s8[4194304]{0:T(1024)(128)(4,1)S(1)}, s32[]{:S(2)}) async-start(s8[8388608]{0:T(1024)(128)(4,1)} %bitcast.2), calls=%async_computation | async-start | bytes 8388608
  43.0 3.8 %copy-start = (f32[2048]{0:T(1024)S(1)}, f32[2048]{0:T(1024)}, u32[]{:S(2)}) copy-start(f32[2048]{0:T(1024)} %param.9) | copy-start | bytes 24580
  43.0 10.7 %slice-start.1 = ((s8[8388608]{0:T(1024)(128)(4,1)}), s8[4194304]{0:T(1024)(128)(4,1)S(1)}, s32[]{:S(2)}) async-start(s8[8388608]{0:T(1024)(128)(4,1)} %bitcast.2), calls=%async_computation.1 | async-start | bytes 8388608
  47.3 7.6 %collective-permute-start.14 = (bf16[256,1024]{1,0:T(8,128)(2,1)S(1)}, bf16[256,1024]{1,0:T(8,128)(2,1)S(1)}, u32[]{:S(2)}, u32[]{:S(2)}) collective-permute-start(bf16[256,1024]{1,0:T(8,128)(2,1)S(1)} %shard_map.76), channel_id=1, source_target_pairs={{0,1},{1,0},{2,3},{3,2},{4,5},{5,4},{6,7},{7,6},{8,9},{9,8},{10,11... | collective-permute-start | bytes 1572872 | tf_op jit(solution)/shard_map/ppermute | solution.py:289

commit v4 on v3

--- a/solution.py
+++ b/solution.py
@@ -224,10 +224,10 @@
             sig[b, :, h * HEAD : (h + 1) * HEAD] = feature_map(x).astype(BF16)
 
 
-def mix_kernel(b, sig, dot, m0, m1, m2, m3, gain, out):
+def mix_rows(b, sig, dot, parts, gain, out):
     own = pl.multiple_of(lax.axis_index("c") * HEADS, HEADS)
-    memory = (m0[...].astype(F32) + m1[...].astype(F32)) + (m2[...].astype(F32) + m3[...].astype(F32))
-    memory = memory.astype(BF16)
+    terms = [ref[...].astype(F32) for ref in parts]
+    memory = ((terms[0] + terms[1]) + (terms[2] + terms[3])).astype(BF16)
     for h in range(HEADS):
         cols, g = slice(h * HEAD, (h + 1) * HEAD), h // GROUP
         read = jnp.dot(
@@ -237,24 +237,38 @@
         out[:, cols] = mixed.astype(BF16)
 
 
-def mix(b, sig, dot, memory, gain):
+def mix_send_kernel(sig, dot, m0, m1, m2, m3, gain, out):
+    mix_rows(1, sig, dot, (m0, m1, m2, m3), gain, out)
+
+
+def mix_send(sig, dot, memory, gain):
     outs = [(sig.shape[1:], BF16)]
-    body = functools.partial(mix_kernel, b)
-    return kernel_call(body, outs, (sig, dot, *memory, gain), 12, 2**26, 2**21)[0]
-
-
-def project_first_kernel(x, weight, out):
-    half = x.shape[1]
-    own = pl.multiple_of(lax.axis_index("c") * half, half)
-    for n in range(0, weight.shape[1], 512):
-        out[:, n : n + 512] = jnp.dot(
-            x[...], weight[pl.ds(own, half), n : n + 512], preferred_element_type=F32
-        )
-
-
-def project_first(x, weight):
-    outs = [((x.shape[0], weight.shape[1]), F32)]
-    return kernel_call(project_first_kernel, outs, (x, weight), 16, 2**30, 2**23)[0]
+    args = (sig, dot, *memory, gain)
+    return kernel_call(mix_send_kernel, outs, args, 12, 2**26, 2**21)[0]
+
+
+def project_own_kernel(core, sig, dot, m0, m1, m2, m3, gain, weight, *more):
+    out, keep = more[-2:]
+
+    @pl.when(lax.axis_index("c") == core)
+    def _():
+        mix_rows(0, sig, dot, (m0, m1, m2, m3), gain, keep)
+        half = keep.shape[1]
+        own = pl.multiple_of(core * half, half)
+        for n in range(0, weight.shape[1], 512):
+            out[:, n : n + 512] = jnp.dot(
+                keep[...], weight[pl.ds(own, half), n : n + 512], preferred_element_type=F32
+            )
+
+
+def project_own(core, sig, dot, memory, gain, weight, begun):
+    rows, width = sig.shape[1], weight.shape[1]
+    args = (sig, dot, *memory, gain, weight, *begun)
+    return kernel_call(
+        functools.partial(project_own_kernel, core), [((rows, width), F32)], args, 16,
+        2**30, 2**23, scratch_shapes=[pltpu.VMEM(sig.shape[1:], BF16)],
+        input_output_aliases={8: 0} if begun else {},
+    )
 
 
 def project_last_kernel(x, begun, weight, out, stage, sems):
@@ -347,9 +361,9 @@
     dot = attend_last(q_own, q_recv, far, ext, top, gain_dot)
     shape = (2, *q_own.shape)
     sig = kernel_call(sig_kernel, [(shape, BF16)], (q_own, q_recv), 8, 2**21, 2**22)[0]
-    mixed_send = mix(1, sig, dot, memory, gain_mem)
-    mixed_keep = mix(0, sig, dot, memory, gain_mem)
-    begun = project_first(mixed_keep, out_weight)
+    mixed_send = mix_send(sig, dot, memory, gain_mem)
+    begun = project_own(1, sig, dot, memory, gain_mem, out_weight, [])
+    begun = project_own(0, sig, dot, memory, gain_mem, out_weight, begun)[0]
     mixed_recv = permute(mixed_send, "c", (1, 0))
     return project_last(mixed_recv, begun, out_weight)
 

time: 57.4 us -> 57.2 us (level)
  no operation moved by 1% of the time
where the time goes in v4:
time: 57.2 us; the launch traced here: 57.1 us
  starting transfers between devices  25.6 us (45%)
  Pallas kernels  19.2 us (34%)
  waiting for transfers between devices  11.8 us (21%)
    ppermute x15, starting transfers between devices, permute(): return lax.ppermute(x, axis, list(enumerate(partner)))  25.6 us
    pallas_call x15, Pallas kernels, kernel_call(): pl.pallas_call(body, out_shape=[pltpu.VMEM(shape, dtype) for shape, dtype...  17.1 us
    ppermute x15, waiting for transfers between devices, permute(): return lax.ppermute(x, axis, list(enumerate(partner)))  11.8 us
    pallas_call x1, Pallas kernels, project_last(): pl.pallas_call(project_last_kernel, out_shape=pltpu.HBM(shape, BF16), in_...  2.12 us
  transfers between devices with their start and end apart: 15, of which 6 were waited for; matrix products, arithmetic and copies ran while one was open for 0% of the time, Pallas kernels for 29%

profile of v4, /device:TPU:31, one launch (start us, length us, event | category | flops | bytes accessed | tf_op | source)
XLA Modules:
  0.0 57.1 jit_solution(9894799798968885941)
XLA Ops:
  0.0 0.7 %collective-permute-start = (bf16[256,2048]{1,0:T(8,128)(2,1)}, bf16[256,2048]{1,0:T(8,128)(2,1)S(1)}, u32[]{:S(2)}, u32[]{:S(2)}) collective-permute-start(bf16[256,2048]{1,0:T(8,128)(2,1)} %q.1), channel_id=1, source_target_pairs={{0,1},{1,0},{2,3},{3,2},{4,5},{5,4},{6,7},{7,6},{8,9},{9,8},{10,11... | collective-permute-start | bytes 3145736 | tf_op jit(solution)/shard_map/ppermute | solution.py:303
  0.7 0.0 collective-permute-start.1
  0.7 0.5 collective-permute-start.2
  1.2 1.2 %shard_map.64 = (bf16[256,512]{1,0:T(8,128)(2,1)S(1)}, bf16[256,1024]{1,0:T(8,128)(2,1)S(1)}) custom-call(bf16[256,512]{1,0:T(8,128)(2,1)} %k.1, bf16[256,512]{1,0:T(8,128)(2,1)} %v.1, bf16[256,2048]{1,0:T(8,128)(2,1)} %q.1), custom_call_target="tpu_custom_call" | custom-call | bytes 2097152 | tf_op jit(solution)/shard_map/pallas_call | solution.py:32
  2.4 1.2 %collective-permute-done.1.k_recv = bf16[256,512]{1,0:T(8,128)(2,1)S(1)} collective-permute-done((bf16[256,512]{1,0:T(8,128)(2,1)}, bf16[256,512]{1,0:T(8,128)(2,1)S(1)}, u32[]{:S(2)}, u32[]{:S(2)}) %collective-permute-start.1) | collective-permute-done | bytes 262176 | tf_op jit(solution)/shard_map/ppermute | solution.py:303
  3.5 0.4 collective-permute-done.2.v_recv
  3.9 0.4 shard_map.66
  4.4 0.1 collective-permute-start.5
  4.4 1.7 %collective-permute-start.6 = (bf16[256,128]{1,0:T(8,128)(2,1)S(1)}, bf16[256,128]{1,0:T(8,128)(2,1)S(1)}, u32[]{:S(2)}, u32[]{:S(2)}) collective-permute-start(bf16[256,128]{1,0:T(8,128)(2,1)S(1)} %get-tuple-element.38), channel_id=1, source_target_pairs={{0,8},{8,0},{16,24},{24,16},{32,40},{40,32},{48,56},{56,48},{1,9},... | collective-permute-start | bytes 196616 | tf_op jit(solution)/shard_map/ppermute | solution.py:303
  6.2 1.4 %collective-permute-start.4 = (bf16[512,512]{1,0:T(8,128)(2,1)S(1)}, bf16[512,512]{1,0:T(8,128)(2,1)S(1)}, u32[]{:S(2)}, u32[]{:S(2)}) collective-permute-start(bf16[512,512]{1,0:T(8,128)(2,1)S(1)} %get-tuple-element.30.kv), channel_id=1, source_target_pairs={{0,6},{2,0},{4,2},{6,4},{1,7},{3,1},{5,3},{7,5},{8,14},{10,8},{12,... | collective-permute-start | bytes 1572872 | tf_op jit(solution)/shard_map/ppermute | solution.py:303
  7.5 0.6 %collective-permute-done.6.got = bf16[256,128]{1,0:T(8,128)(2,1)S(1)} collective-permute-done((bf16[256,128]{1,0:T(8,128)(2,1)S(1)}, bf16[256,128]{1,0:T(8,128)(2,1)S(1)}, u32[]{:S(2)}, u32[]{:S(2)}) %collective-permute-start.6) | collective-permute-done | bytes 65568 | tf_op jit(solution)/shard_map/ppermute | solution.py:303
  8.2 3.1 %collective-permute-start.7 = (bf16[256,128]{1,0:T(8,128)(2,1)S(1)}, bf16[256,128]{1,0:T(8,128)(2,1)S(1)}, u32[]{:S(2)}, u32[]{:S(2)}) collective-permute-start(bf16[256,128]{1,0:T(8,128)(2,1)S(1)} %get-tuple-element.41), channel_id=1, source_target_pairs={{0,16},{8,24},{16,0},{24,8},{32,48},{40,56},{48,32},{56,40},{1,17}... | collective-permute-start | bytes 196616 | tf_op jit(solution)/shard_map/ppermute | solution.py:303
  11.3 2.1 %collective-permute-start.3 = (bf16[512,512]{1,0:T(8,128)(2,1)S(1)}, bf16[512,512]{1,0:T(8,128)(2,1)S(1)}, u32[]{:S(2)}, u32[]{:S(2)}) collective-permute-start(bf16[512,512]{1,0:T(8,128)(2,1)S(1)} %get-tuple-element.30.kv), channel_id=1, source_target_pairs={{0,4},{2,6},{4,0},{6,2},{1,5},{3,7},{5,1},{7,3},{8,12},{10,14},{12... | collective-permute-start | bytes 1572872 | tf_op jit(solution)/shard_map/ppermute | solution.py:303
  13.4 0.0 collective-permute-done.7.got
  13.4 5.1 %collective-permute-start.8 = (bf16[256,128]{1,0:T(8,128)(2,1)S(1)}, bf16[256,128]{1,0:T(8,128)(2,1)S(1)}, u32[]{:S(2)}, u32[]{:S(2)}) collective-permute-start(bf16[256,128]{1,0:T(8,128)(2,1)S(1)} %get-tuple-element.44), channel_id=1, source_target_pairs={{0,56},{8,48},{16,40},{24,32},{32,24},{40,16},{48,8},{56,0},{1,57}... | collective-permute-start | bytes 196616 | tf_op jit(solution)/shard_map/ppermute | solution.py:303
  18.5 2.4 %collective-permute-done.8.got = bf16[256,128]{1,0:T(8,128)(2,1)S(1)} collective-permute-done((bf16[256,128]{1,0:T(8,128)(2,1)S(1)}, bf16[256,128]{1,0:T(8,128)(2,1)S(1)}, u32[]{:S(2)}, u32[]{:S(2)}) %collective-permute-start.8) | collective-permute-done | bytes 65568 | tf_op jit(solution)/shard_map/ppermute | solution.py:303
  21.0 0.6 %collective-permute-start.9 = (bf16[256,128]{1,0:T(8,128)(2,1)S(1)}, bf16[256,128]{1,0:T(8,128)(2,1)S(1)}, u32[]{:S(2)}, u32[]{:S(2)}) collective-permute-start(bf16[256,128]{1,0:T(8,128)(2,1)S(1)} %get-tuple-element.47), channel_id=1, source_target_pairs={{0,64},{64,0},{128,192},{192,128},{1,65},{65,1},{129,193},{193,129... | collective-permute-start | bytes 196616 | tf_op jit(solution)/shard_map/ppermute | solution.py:303
  21.6 2.9 %collective-permute-done.9.got = bf16[256,128]{1,0:T(8,128)(2,1)S(1)} collective-permute-done((bf16[256,128]{1,0:T(8,128)(2,1)S(1)}, bf16[256,128]{1,0:T(8,128)(2,1)S(1)}, u32[]{:S(2)}, u32[]{:S(2)}) %collective-permute-start.9) | collective-permute-done | bytes 65568 | tf_op jit(solution)/shard_map/ppermute | solution.py:303
  24.5 0.3 collective-permute-start.10
  24.8 4.4 %collective-permute-done.10.got = bf16[256,128]{1,0:T(8,128)(2,1)S(1)} collective-permute-done((bf16[256,128]{1,0:T(8,128)(2,1)S(1)}, bf16[256,128]{1,0:T(8,128)(2,1)S(1)}, u32[]{:S(2)}, u32[]{:S(2)}) %collective-permute-start.10) | collective-permute-done | bytes 65568 | tf_op jit(solution)/shard_map/ppermute | solution.py:303
  29.2 1.1 %collective-permute-start.11 = (bf16[256,128]{1,0:T(8,128)(2,1)S(1)}, bf16[256,128]{1,0:T(8,128)(2,1)S(1)}, u32[]{:S(2)}, u32[]{:S(2)}) collective-permute-start(bf16[256,128]{1,0:T(8,128)(2,1)S(1)} %shard_map.75.m0), channel_id=1, source_target_pairs={{0,2},{2,0},{4,6},{6,4},{1,3},{3,1},{5,7},{7,5},{8,10},{10,8},{12,... | collective-permute-start | bytes 196616 | tf_op jit(solution)/shard_map/ppermute | solution.py:303
  30.3 0.0 collective-permute-done.q_recv
  30.3 1.6 %collective-permute-start.12 = (bf16[256,128]{1,0:T(8,128)(2,1)S(1)}, bf16[256,128]{1,0:T(8,128)(2,1)S(1)}, u32[]{:S(2)}, u32[]{:S(2)}) collective-permute-start(bf16[256,128]{1,0:T(8,128)(2,1)S(1)} %shard_map.75.m0), channel_id=1, source_target_pairs={{0,4},{2,6},{4,0},{6,2},{1,5},{3,7},{5,1},{7,3},{8,12},{10,14},{12... | collective-permute-start | bytes 196616 | tf_op jit(solution)/shard_map/ppermute | solution.py:303
  31.9 0.5 shard_map.65.sig
  32.4 2.9 %shard_map.67 = (f32[2,256,2048]{2,1,0:T(8,128)S(1)}, f32[2,256,1024]{2,1,0:T(8,128)S(1)}) custom-call(bf16[256,1024]{1,0:T(8,128)(2,1)S(1)} %get-tuple-element.28.q_keep, bf16[256,2048]{1,0:T(8,128)(2,1)S(1)} %collective-permute-done.q_recv, bf16[512,512]{1,0:T(8,128)(2,1)S(1)} %get-tuple-element.30.kv), custom_call_target="tpu_custom_call" | custom-call | flops 1073741824 | bytes 4194304 | tf_op jit(solution)/shard_map/pallas_call | solution.py:32
  35.3 0.0 collective-permute-done.5.kv
  35.3 1.6 %collective-permute-start.13 = (bf16[256,128]{1,0:T(8,128)(2,1)S(1)}, bf16[256,128]{1,0:T(8,128)(2,1)S(1)}, u32[]{:S(2)}, u32[]{:S(2)}) collective-permute-start(bf16[256,128]{1,0:T(8,128)(2,1)S(1)} %shard_map.75.m0), channel_id=1, source_target_pairs={{0,6},{2,4},{4,2},{6,0},{1,7},{3,5},{5,3},{7,1},{8,14},{10,12},{12... | collective-permute-start | bytes 196616 | tf_op jit(solution)/shard_map/ppermute | solution.py:303
  36.9 3.0 %shard_map.68 = (f32[2,256,2048]{2,1,0:T(8,128)S(1)}, f32[2,256,1024]{2,1,0:T(8,128)S(1)}) custom-call(bf16[256,1024]{1,0:T(8,128)(2,1)S(1)} %get-tuple-element.28.q_keep, bf16[256,2048]{1,0:T(8,128)(2,1)S(1)} %collective-permute-done.q_recv, bf16[512,512]{1,0:T(8,128)(2,1)S(1)} %collective-permute-done.5.kv, ...), custom_call_target="tpu_custom_call", output_to_operand_aliasing={{0}: (3, {}), {1}: (4, {})} | custom-call | flops 1073741824 | bytes 4194304 | tf_op jit(solution)/shard_map/pallas_call | solution.py:32
  39.9 0.0 collective-permute-done.4.kv
  39.9 0.0 copy-start.1
  39.9 0.0 slice-start
  39.9 3.0 %shard_map.69 = (f32[2,256,2048]{2,1,0:T(8,128)S(1)}, f32[2,256,1024]{2,1,0:T(8,128)S(1)}) custom-call(bf16[256,1024]{1,0:T(8,128)(2,1)S(1)} %get-tuple-element.28.q_keep, bf16[256,2048]{1,0:T(8,128)(2,1)S(1)} %collective-permute-done.q_recv, bf16[512,512]{1,0:T(8,128)(2,1)S(1)} %collective-permute-done.4.kv, ...), custom_call_target="tpu_custom_call", output_to_operand_aliasing={{0}: (3, {}), {1}: (4, {})} | custom-call | flops 1073741824 | bytes 4194304 | tf_op jit(solution)/shard_map/pallas_call | solution.py:32
  43.0 0.0 collective-permute-done.3.kv
  43.0 0.0 copy-done.1
  43.0 0.0 copy-start
  43.0 0.0 slice-start.1
  43.0 3.7 %shard_map.70.dot = f32[2,256,1024]{2,1,0:T(8,128)S(1)} custom-call(bf16[256,1024]{1,0:T(8,128)(2,1)S(1)} %get-tuple-element.28.q_keep, bf16[256,2048]{1,0:T(8,128)(2,1)S(1)} %collective-permute-done.q_recv, bf16[512,512]{1,0:T(8,128)(2,1)S(1)} %collective-permute-done.3.kv, f32[2,256,2048]{2,1,0:T(8,128)S(1)} %get-tuple-element.35.ext, ...), custom_call_target="tpu_custom_call" | custom-call | flops 1073741824 | bytes 4194304 | tf_op jit(solution)/shard_map/pallas_call | solution.py:32
  46.7 0.0 collective-permute-done.11.m1
  46.7 0.0 collective-permute-done.12.m2
  46.8 0.0 collective-permute-done.13.m3
  46.8 0.0 copy-done
  46.8 0.5 shard_map.76
  47.3 5.8 %collective-permute-start.14 = (bf16[256,1024]{1,0:T(8,128)(2,1)S(1)}, bf16[256,1024]{1,0:T(8,128)(2,1)S(1)}, u32[]{:S(2)}, u32[]{:S(2)}) collective-permute-start(bf16[256,1024]{1,0:T(8,128)(2,1)S(1)} %shard_map.76), channel_id=1, source_target_pairs={{0,1},{1,0},{2,3},{3,2},{4,5},{5,4},{6,7},{7,6},{8,9},{9,8},{10,11... | collective-permute-start | bytes 1572872 | tf_op jit(solution)/shard_map/ppermute | solution.py:303
  53.1 0.0 slice-done
  53.1 0.0 slice-done.1
  53.1 1.6 %shard_map.77.more_0_ = f32[256,2048]{1,0:T(8,128)S(1)} custom-call(bf16[2,256,1024]{2,1,0:T(8,128)(2,1)S(1)} %shard_map.65.sig, f32[2,256,1024]{2,1,0:T(8,128)S(1)} %shard_map.70.dot, bf16[256,128]{1,0:T(8,128)(2,1)S(1)} %shard_map.75.m0, bf16[256,128]{1,0:T(8,128)(2,1)S(1)} %collective-permute-done.11.m1, bf16[256,128]{1,0:T(8,128)(2,1)S(1)} %collective-permute-done.12.m2, ...), custom_call_target="tpu_custom_call" | custom-call | flops 1073741824 | bytes 8388608 | tf_op jit(solution)/shard_map/pallas_call | solution.py:32
  54.7 0.0 collective-permute-done.14.x
  54.8 2.1 %project_last.1 = bf16[256,2048]{1,0:T(8,128)(2,1)} custom-call(bf16[256,1024]{1,0:T(8,128)(2,1)S(1)} %collective-permute-done.14.x, f32[256,2048]{1,0:T(8,128)S(1)} %shard_map.78.begun, bf16[2048,2048]{1,0:T(8,128)(2,1)S(1)} %bitcast.3), custom_call_target="tpu_custom_call" | custom-call | flops 1073741824 | bytes 8388608 | tf_op jit(solution)/shard_map/project_last/pallas_call | solution.py:290
  (8 shorter events, 0.2 us)
Async XLA Ops:
  0.0 30.3 %collective-permute-start = (bf16[256,2048]{1,0:T(8,128)(2,1)}, bf16[256,2048]{1,0:T(8,128)(2,1)S(1)}, u32[]{:S(2)}, u32[]{:S(2)}) collective-permute-start(bf16[256,2048]{1,0:T(8,128)(2,1)} %q.1), channel_id=1, source_target_pairs={{0,1},{1,0},{2,3},{3,2},{4,5},{5,4},{6,7},{7,6},{8,9},{9,8},{10,11... | collective-permute-start | bytes 3145736 | tf_op jit(solution)/shard_map/ppermute | solution.py:303
  0.7 2.9 %collective-permute-start.1 = (bf16[256,512]{1,0:T(8,128)(2,1)}, bf16[256,512]{1,0:T(8,128)(2,1)S(1)}, u32[]{:S(2)}, u32[]{:S(2)}) collective-permute-start(bf16[256,512]{1,0:T(8,128)(2,1)} %k.1), channel_id=1, source_target_pairs={{0,1},{1,0},{2,3},{3,2},{4,5},{5,4},{6,7},{7,6},{8,9},{9,8},{10,11... | collective-permute-start | bytes 786440 | tf_op jit(solution)/shard_map/ppermute | solution.py:303
  0.7 3.2 %collective-permute-start.2 = (bf16[256,512]{1,0:T(8,128)(2,1)}, bf16[256,512]{1,0:T(8,128)(2,1)S(1)}, u32[]{:S(2)}, u32[]{:S(2)}) collective-permute-start(bf16[256,512]{1,0:T(8,128)(2,1)} %v.1), channel_id=1, source_target_pairs={{0,1},{1,0},{2,3},{3,2},{4,5},{5,4},{6,7},{7,6},{8,9},{9,8},{10,11... | collective-permute-start | bytes 786440 | tf_op jit(solution)/shard_map/ppermute | solution.py:303
  4.4 30.9 %collective-permute-start.5 = (bf16[512,512]{1,0:T(8,128)(2,1)S(1)}, bf16[512,512]{1,0:T(8,128)(2,1)S(1)}, u32[]{:S(2)}, u32[]{:S(2)}) collective-permute-start(bf16[512,512]{1,0:T(8,128)(2,1)S(1)} %get-tuple-element.30.kv), channel_id=1, source_target_pairs={{0,2},{2,4},{4,6},{6,0},{1,3},{3,5},{5,7},{7,1},{8,10},{10,12},{12... | collective-permute-start | bytes 1572872 | tf_op jit(solution)/shard_map/ppermute | solution.py:303
  4.4 3.7 %collective-permute-start.6 = (bf16[256,128]{1,0:T(8,128)(2,1)S(1)}, bf16[256,128]{1,0:T(8,128)(2,1)S(1)}, u32[]{:S(2)}, u32[]{:S(2)}) collective-permute-start(bf16[256,128]{1,0:T(8,128)(2,1)S(1)} %get-tuple-element.38), channel_id=1, source_target_pairs={{0,8},{8,0},{16,24},{24,16},{32,40},{40,32},{48,56},{56,48},{1,9},... | collective-permute-start | bytes 196616 | tf_op jit(solution)/shard_map/ppermute | solution.py:303
  6.2 33.7 %collective-permute-start.4 = (bf16[512,512]{1,0:T(8,128)(2,1)S(1)}, bf16[512,512]{1,0:T(8,128)(2,1)S(1)}, u32[]{:S(2)}, u32[]{:S(2)}) collective-permute-start(bf16[512,512]{1,0:T(8,128)(2,1)S(1)} %get-tuple-element.30.kv), channel_id=1, source_target_pairs={{0,6},{2,0},{4,2},{6,4},{1,7},{3,1},{5,3},{7,5},{8,14},{10,8},{12,... | collective-permute-start | bytes 1572872 | tf_op jit(solution)/shard_map/ppermute | solution.py:303
  8.2 5.2 %collective-permute-start.7 = (bf16[256,128]{1,0:T(8,128)(2,1)S(1)}, bf16[256,128]{1,0:T(8,128)(2,1)S(1)}, u32[]{:S(2)}, u32[]{:S(2)}) collective-permute-start(bf16[256,128]{1,0:T(8,128)(2,1)S(1)} %get-tuple-element.41), channel_id=1, source_target_pairs={{0,16},{8,24},{16,0},{24,8},{32,48},{40,56},{48,32},{56,40},{1,17}... | collective-permute-start | bytes 196616 | tf_op jit(solution)/shard_map/ppermute | solution.py:303
  11.3 31.7 %collective-permute-start.3 = (bf16[512,512]{1,0:T(8,128)(2,1)S(1)}, bf16[512,512]{1,0:T(8,128)(2,1)S(1)}, u32[]{:S(2)}, u32[]{:S(2)}) collective-permute-start(bf16[512,512]{1,0:T(8,128)(2,1)S(1)} %get-tuple-element.30.kv), channel_id=1, source_target_pairs={{0,4},{2,6},{4,0},{6,2},{1,5},{3,7},{5,1},{7,3},{8,12},{10,14},{12... | collective-permute-start | bytes 1572872 | tf_op jit(solution)/shard_map/ppermute | solution.py:303
  13.4 7.5 %collective-permute-start.8 = (bf16[256,128]{1,0:T(8,128)(2,1)S(1)}, bf16[256,128]{1,0:T(8,128)(2,1)S(1)}, u32[]{:S(2)}, u32[]{:S(2)}) collective-permute-start(bf16[256,128]{1,0:T(8,128)(2,1)S(1)} %get-tuple-element.44), channel_id=1, source_target_pairs={{0,56},{8,48},{16,40},{24,32},{32,24},{40,16},{48,8},{56,0},{1,57}... | collective-permute-start | bytes 196616 | tf_op jit(solution)/shard_map/ppermute | solution.py:303
  21.0 3.5 %collective-permute-start.9 = (bf16[256,128]{1,0:T(8,128)(2,1)S(1)}, bf16[256,128]{1,0:T(8,128)(2,1)S(1)}, u32[]{:S(2)}, u32[]{:S(2)}) collective-permute-start(bf16[256,128]{1,0:T(8,128)(2,1)S(1)} %get-tuple-element.47), channel_id=1, source_target_pairs={{0,64},{64,0},{128,192},{192,128},{1,65},{65,1},{129,193},{193,129... | collective-permute-start | bytes 196616 | tf_op jit(solution)/shard_map/ppermute | solution.py:303
  24.5 4.7 %collective-permute-start.10 = (bf16[256,128]{1,0:T(8,128)(2,1)S(1)}, bf16[256,128]{1,0:T(8,128)(2,1)S(1)}, u32[]{:S(2)}, u32[]{:S(2)}) collective-permute-start(bf16[256,128]{1,0:T(8,128)(2,1)S(1)} %get-tuple-element.50), channel_id=1, source_target_pairs={{0,192},{64,128},{128,64},{192,0},{1,193},{65,129},{129,65},{193,1... | collective-permute-start | bytes 196616 | tf_op jit(solution)/shard_map/ppermute | solution.py:303
  29.2 17.5 %collective-permute-start.11 = (bf16[256,128]{1,0:T(8,128)(2,1)S(1)}, bf16[256,128]{1,0:T(8,128)(2,1)S(1)}, u32[]{:S(2)}, u32[]{:S(2)}) collective-permute-start(bf16[256,128]{1,0:T(8,128)(2,1)S(1)} %shard_map.75.m0), channel_id=1, source_target_pairs={{0,2},{2,0},{4,6},{6,4},{1,3},{3,1},{5,7},{7,5},{8,10},{10,8},{12,... | collective-permute-start | bytes 196616 | tf_op jit(solution)/shard_map/ppermute | solution.py:303
  30.3 16.4 %collective-permute-start.12 = (bf16[256,128]{1,0:T(8,128)(2,1)S(1)}, bf16[256,128]{1,0:T(8,128)(2,1)S(1)}, u32[]{:S(2)}, u32[]{:S(2)}) collective-permute-start(bf16[256,128]{1,0:T(8,128)(2,1)S(1)} %shard_map.75.m0), channel_id=1, source_target_pairs={{0,4},{2,6},{4,0},{6,2},{1,5},{3,7},{5,1},{7,3},{8,12},{10,14},{12... | collective-permute-start | bytes 196616 | tf_op jit(solution)/shard_map/ppermute | solution.py:303
  35.3 11.5 %collective-permute-start.13 = (bf16[256,128]{1,0:T(8,128)(2,1)S(1)}, bf16[256,128]{1,0:T(8,128)(2,1)S(1)}, u32[]{:S(2)}, u32[]{:S(2)}) collective-permute-start(bf16[256,128]{1,0:T(8,128)(2,1)S(1)} %shard_map.75.m0), channel_id=1, source_target_pairs={{0,6},{2,4},{4,2},{6,0},{1,7},{3,5},{5,3},{7,1},{8,14},{10,12},{12... | collective-permute-start | bytes 196616 | tf_op jit(solution)/shard_map/ppermute | solution.py:303
  39.9 3.1 %copy-start.1 = (f32[2048]{0:T(1024)S(1)}, f32[2048]{0:T(1024)}, u32[]{:S(2)}) copy-start(f32[2048]{0:T(1024)} %param.10) | copy-start | bytes 24580
  39.9 13.2 %slice-start = ((s8[8388608]{0:T(1024)(128)(4,1)}), s8[4194304]{0:T(1024)(128)(4,1)S(1)}, s32[]{:S(2)}) async-start(s8[8388608]{0:T(1024)(128)(4,1)} %bitcast.2), calls=%async_computation | async-start | bytes 8388608
  43.0 3.8 %copy-start = (f32[2048]{0:T(1024)S(1)}, f32[2048]{0:T(1024)}, u32[]{:S(2)}) copy-start(f32[2048]{0:T(1024)} %param.9) | copy-start | bytes 24580
  43.0 10.1 %slice-start.1 = ((s8[8388608]{0:T(1024)(128)(4,1)}), s8[4194304]{0:T(1024)(128)(4,1)S(1)}, s32[]{:S(2)}) async-start(s8[8388608]{0:T(1024)(128)(4,1)} %bitcast.2), calls=%async_computation.1 | async-start | bytes 8388608
  47.3 7.4 %collective-permute-start.14 = (bf16[256,1024]{1,0:T(8,128)(2,1)S(1)}, bf16[256,1024]{1,0:T(8,128)(2,1)S(1)}, u32[]{:S(2)}, u32[]{:S(2)}) collective-permute-start(bf16[256,1024]{1,0:T(8,128)(2,1)S(1)} %shard_map.76), channel_id=1, source_target_pairs={{0,1},{1,0},{2,3},{3,2},{4,5},{5,4},{6,7},{7,6},{8,9},{9,8},{10,11... | collective-permute-start | bytes 1572872 | tf_op jit(solution)/shard_map/ppermute | solution.py:303

commit v5 on v4

--- a/solution.py
+++ b/solution.py
@@ -224,27 +224,35 @@
             sig[b, :, h * HEAD : (h + 1) * HEAD] = feature_map(x).astype(BF16)
 
 
-def mix_rows(b, sig, dot, parts, gain, out):
+def mix_rows(b, r, sig, dot, parts, gain, out):
     own = pl.multiple_of(lax.axis_index("c") * HEADS, HEADS)
     terms = [ref[...].astype(F32) for ref in parts]
     memory = ((terms[0] + terms[1]) + (terms[2] + terms[3])).astype(BF16)
     for h in range(HEADS):
         cols, g = slice(h * HEAD, (h + 1) * HEAD), h // GROUP
         read = jnp.dot(
-            sig[b, :, cols], memory[g * HEAD : (g + 1) * HEAD], preferred_element_type=F32
+            sig[b, r, cols], memory[g * HEAD : (g + 1) * HEAD], preferred_element_type=F32
         )
-        mixed = head_norm(read, gain[pl.ds(own + h, 1), :]) + dot[b, :, cols]
+        mixed = head_norm(read, gain[pl.ds(own + h, 1), :]) + dot[b, r, cols]
         out[:, cols] = mixed.astype(BF16)
 
 
-def mix_send_kernel(sig, dot, m0, m1, m2, m3, gain, out):
-    mix_rows(1, sig, dot, (m0, m1, m2, m3), gain, out)
-
-
-def mix_send(sig, dot, memory, gain):
-    outs = [(sig.shape[1:], BF16)]
-    args = (sig, dot, *memory, gain)
-    return kernel_call(mix_send_kernel, outs, args, 12, 2**26, 2**21)[0]
+def mix_send_kernel(r, core, sig, dot, m0, m1, m2, m3, gain, *more):
+    here = True if core is None else lax.axis_index("c") == core
+
+    @pl.when(here)
+    def _():
+        mix_rows(1, r, sig, dot, (m0, m1, m2, m3), gain, more[-1])
+
+
+def mix_send(part, core, sig, dot, memory, gain, begun):
+    half = sig.shape[1] // 2
+    outs = [((half, sig.shape[2]), BF16)]
+    body = functools.partial(mix_send_kernel, slice(part * half, (part + 1) * half), core)
+    return kernel_call(
+        body, outs, (sig, dot, *memory, gain, *begun), 12, 2**25, 2**20,
+        input_output_aliases={7: 0} if begun else {},
+    )
 
 
 def project_own_kernel(core, sig, dot, m0, m1, m2, m3, gain, weight, *more):
@@ -252,7 +260,7 @@
 
     @pl.when(lax.axis_index("c") == core)
     def _():
-        mix_rows(0, sig, dot, (m0, m1, m2, m3), gain, keep)
+        mix_rows(0, slice(None), sig, dot, (m0, m1, m2, m3), gain, keep)
         half = keep.shape[1]
         own = pl.multiple_of(core * half, half)
         for n in range(0, weight.shape[1], 512):
@@ -271,32 +279,52 @@
     )
 
 
-def project_last_kernel(x, begun, weight, out, stage, sems):
-    half, width = x.shape[1], 256
+def project_rows(part, x, begun, weight):
+    rows, half = x.shape
     other = pl.multiple_of(half - lax.axis_index("c") * half, half)
-    copies = []
-    for i in range(out.shape[1] // width):
-        n = slice(i * width, (i + 1) * width)
+    for first in range(0, weight.shape[1], 256):
+        n = slice(first, first + 256)
         total = jnp.dot(x[...], weight[pl.ds(other, half), n], preferred_element_type=F32)
-        stage[:, n] = (begun[:, n] + total).astype(BF16)
-        copies.append(pltpu.make_async_copy(stage.at[:, n], out.at[:, n], sems.at[i]))
-        copies[-1].start()
+        yield n, (begun[part * rows : (part + 1) * rows, n] + total).astype(BF16)
+
+
+def project_a_kernel(x, begun, weight, out):
+    for n, total in project_rows(0, x, begun, weight):
+        out[:, n] = total
+
+
+def project_b_kernel(x, begun, weight, done, out, stage, sems):
+    rows = x.shape[0]
+    copies = [pltpu.make_async_copy(done, out.at[:rows, :], sems.at[0])]
+    copies[0].start()
+    for i, (n, total) in enumerate(project_rows(1, x, begun, weight)):
+        stage[:, n] = total
+        if i % 2:
+            pair = slice(n.stop - 512, n.stop)
+            dst = out.at[rows:, pair]
+            copies.append(pltpu.make_async_copy(stage.at[:, pair], dst, sems.at[1 + i // 2]))
+            copies[-1].start()
     for copy in copies:
         copy.wait()
 
 
-def project_last(x, begun, weight):
-    shape = begun.shape
+def project_last(x_a, x_b, begun, weight):
+    shape, rows = begun.shape, x_a.shape[0]
+    outs = [((rows, shape[1]), BF16)]
+    done = kernel_call(project_a_kernel, outs, (x_a, begun, weight), 16, 2**29, 2**22)
     return pl.pallas_call(
-        project_last_kernel,
+        project_b_kernel,
         out_shape=pltpu.HBM(shape, BF16),
-        in_specs=[VM] * 3,
+        in_specs=[VM] * 4,
         out_specs=HBM,
-        scratch_shapes=[pltpu.VMEM(shape, BF16), pltpu.SemaphoreType.DMA((shape[1] // 256,))],
-        name="project_last",
+        scratch_shapes=[
+            pltpu.VMEM((rows, shape[1]), BF16),
+            pltpu.SemaphoreType.DMA((1 + shape[1] // 512,)),
+        ],
+        name="project_b",
         compiler_params=pltpu.CompilerParams(vmem_limit_bytes=16 * 2**20),
-        cost_estimate=pl.CostEstimate(flops=2**30, bytes_accessed=2**23, transcendentals=0),
-    )(*[placed(a) for a in (x, begun, weight)])
+        cost_estimate=pl.CostEstimate(flops=2**29, bytes_accessed=2**22, transcendentals=0),
+    )(*[placed(a) for a in (x_b, begun, weight, done[0])])
 
 
 def permute(x, axis, partner):
@@ -361,11 +389,14 @@
     dot = attend_last(q_own, q_recv, far, ext, top, gain_dot)
     shape = (2, *q_own.shape)
     sig = kernel_call(sig_kernel, [(shape, BF16)], (q_own, q_recv), 8, 2**21, 2**22)[0]
-    mixed_send = mix_send(sig, dot, memory, gain_mem)
+    mixed_a = mix_send(0, None, sig, dot, memory, gain_mem, [])[0]
+    mixed_b = mix_send(1, 1, sig, dot, memory, gain_mem, [])
+    mixed_b = mix_send(1, 0, sig, dot, memory, gain_mem, mixed_b)[0]
     begun = project_own(1, sig, dot, memory, gain_mem, out_weight, [])
     begun = project_own(0, sig, dot, memory, gain_mem, out_weight, begun)[0]
-    mixed_recv = permute(mixed_send, "c", (1, 0))
-    return project_last(mixed_recv, begun, out_weight)
+    mixed_a = permute(mixed_a, "c", (1, 0))
+    mixed_b = permute(mixed_b, "c", (1, 0))
+    return project_last(mixed_a, mixed_b, begun, out_weight)
 
 
 def solution(mesh):

time: 57.2 us -> 58.2 us (1.017)
  the two profiles are of different devices: /device:TPU:31 before, /device:TPU:30 now
where the time goes in v5:
time: 58.2 us; the launch traced here: 58 us
  starting transfers between devices  23.7 us (41%)
  Pallas kernels  19.6 us (34%)
  waiting for transfers between devices  13.6 us (23%)
  local copies, waits for them, and re-layouts  0.7 us (1%)
    ppermute x16, starting transfers between devices, permute(): return lax.ppermute(x, axis, list(enumerate(partner)))  23.7 us
    pallas_call x18, Pallas kernels, kernel_call(): pl.pallas_call(body, out_shape=[pltpu.VMEM(shape, dtype) for shape, dtype...  18.1 us
    ppermute x16, waiting for transfers between devices, permute(): return lax.ppermute(x, axis, list(enumerate(partner)))  13.6 us
    pallas_call x1, Pallas kernels, project_last(): pl.pallas_call(project_b_kernel, out_shape=pltpu.HBM(shape, BF16), in_spe...  1.47 us
  transfers between devices with their start and end apart: 16, of which 6 were waited for; matrix products, arithmetic and copies ran while one was open for 0% of the time, Pallas kernels for 31%

profile of v5, /device:TPU:30, one launch (start us, length us, event | category | flops | bytes accessed | tf_op | source)
XLA Modules:
  0.0 58.0 jit_solution(3119727643254657988)
XLA Ops:
  0.0 0.0 collective-permute-start
  0.0 0.5 collective-permute-start.1
  0.5 0.0 collective-permute-start.2
  0.5 1.2 %shard_map.64 = (bf16[256,512]{1,0:T(8,128)(2,1)S(1)}, bf16[256,1024]{1,0:T(8,128)(2,1)S(1)}) custom-call(bf16[256,512]{1,0:T(8,128)(2,1)} %k.1, bf16[256,512]{1,0:T(8,128)(2,1)} %v.1, bf16[256,2048]{1,0:T(8,128)(2,1)} %q.1), custom_call_target="tpu_custom_call" | custom-call | bytes 2097152 | tf_op jit(solution)/shard_map/pallas_call | solution.py:32
  1.7 1.5 %collective-permute-done.1.k_recv = bf16[256,512]{1,0:T(8,128)(2,1)S(1)} collective-permute-done((bf16[256,512]{1,0:T(8,128)(2,1)}, bf16[256,512]{1,0:T(8,128)(2,1)S(1)}, u32[]{:S(2)}, u32[]{:S(2)}) %collective-permute-start.1) | collective-permute-done | bytes 262176 | tf_op jit(solution)/shard_map/ppermute | solution.py:331
  3.2 0.4 collective-permute-done.2.v_recv
  3.6 0.4 shard_map.66
  4.1 0.3 collective-permute-start.5
  4.4 1.9 %collective-permute-start.6 = (bf16[256,128]{1,0:T(8,128)(2,1)S(1)}, bf16[256,128]{1,0:T(8,128)(2,1)S(1)}, u32[]{:S(2)}, u32[]{:S(2)}) collective-permute-start(bf16[256,128]{1,0:T(8,128)(2,1)S(1)} %get-tuple-element.38), channel_id=1, source_target_pairs={{0,8},{8,0},{16,24},{24,16},{32,40},{40,32},{48,56},{56,48},{1,9},... | collective-permute-start | bytes 196616 | tf_op jit(solution)/shard_map/ppermute | solution.py:331
  6.3 1.8 %collective-permute-start.4 = (bf16[512,512]{1,0:T(8,128)(2,1)S(1)}, bf16[512,512]{1,0:T(8,128)(2,1)S(1)}, u32[]{:S(2)}, u32[]{:S(2)}) collective-permute-start(bf16[512,512]{1,0:T(8,128)(2,1)S(1)} %get-tuple-element.30.kv), channel_id=1, source_target_pairs={{0,6},{2,0},{4,2},{6,4},{1,7},{3,1},{5,3},{7,5},{8,14},{10,8},{12,... | collective-permute-start | bytes 1572872 | tf_op jit(solution)/shard_map/ppermute | solution.py:331
  8.1 0.5 collective-permute-done.6.got
  8.7 3.4 %collective-permute-start.7 = (bf16[256,128]{1,0:T(8,128)(2,1)S(1)}, bf16[256,128]{1,0:T(8,128)(2,1)S(1)}, u32[]{:S(2)}, u32[]{:S(2)}) collective-permute-start(bf16[256,128]{1,0:T(8,128)(2,1)S(1)} %get-tuple-element.41), channel_id=1, source_target_pairs={{0,16},{8,24},{16,0},{24,8},{32,48},{40,56},{48,32},{56,40},{1,17}... | collective-permute-start | bytes 196616 | tf_op jit(solution)/shard_map/ppermute | solution.py:331
  12.0 2.6 %collective-permute-start.3 = (bf16[512,512]{1,0:T(8,128)(2,1)S(1)}, bf16[512,512]{1,0:T(8,128)(2,1)S(1)}, u32[]{:S(2)}, u32[]{:S(2)}) collective-permute-start(bf16[512,512]{1,0:T(8,128)(2,1)S(1)} %get-tuple-element.30.kv), channel_id=1, source_target_pairs={{0,4},{2,6},{4,0},{6,2},{1,5},{3,7},{5,1},{7,3},{8,12},{10,14},{12... | collective-permute-start | bytes 1572872 | tf_op jit(solution)/shard_map/ppermute | solution.py:331
  14.6 0.0 collective-permute-done.7.got
  14.7 6.0 %collective-permute-start.8 = (bf16[256,128]{1,0:T(8,128)(2,1)S(1)}, bf16[256,128]{1,0:T(8,128)(2,1)S(1)}, u32[]{:S(2)}, u32[]{:S(2)}) collective-permute-start(bf16[256,128]{1,0:T(8,128)(2,1)S(1)} %get-tuple-element.44), channel_id=1, source_target_pairs={{0,56},{8,48},{16,40},{24,32},{32,24},{40,16},{48,8},{56,0},{1,57}... | collective-permute-start | bytes 196616 | tf_op jit(solution)/shard_map/ppermute | solution.py:331
  20.7 2.7 %collective-permute-done.8.got = bf16[256,128]{1,0:T(8,128)(2,1)S(1)} collective-permute-done((bf16[256,128]{1,0:T(8,128)(2,1)S(1)}, bf16[256,128]{1,0:T(8,128)(2,1)S(1)}, u32[]{:S(2)}, u32[]{:S(2)}) %collective-permute-start.8) | collective-permute-done | bytes 65568 | tf_op jit(solution)/shard_map/ppermute | solution.py:331
  23.4 0.9 %collective-permute-start.9 = (bf16[256,128]{1,0:T(8,128)(2,1)S(1)}, bf16[256,128]{1,0:T(8,128)(2,1)S(1)}, u32[]{:S(2)}, u32[]{:S(2)}) collective-permute-start(bf16[256,128]{1,0:T(8,128)(2,1)S(1)} %get-tuple-element.47), channel_id=1, source_target_pairs={{0,64},{64,0},{128,192},{192,128},{1,65},{65,1},{129,193},{193,129... | collective-permute-start | bytes 196616 | tf_op jit(solution)/shard_map/ppermute | solution.py:331
  24.3 3.4 %collective-permute-done.9.got = bf16[256,128]{1,0:T(8,128)(2,1)S(1)} collective-permute-done((bf16[256,128]{1,0:T(8,128)(2,1)S(1)}, bf16[256,128]{1,0:T(8,128)(2,1)S(1)}, u32[]{:S(2)}, u32[]{:S(2)}) %collective-permute-start.9) | collective-permute-done | bytes 65568 | tf_op jit(solution)/shard_map/ppermute | solution.py:331
  27.8 0.6 collective-permute-start.10
  28.4 5.0 %collective-permute-done.10.got = bf16[256,128]{1,0:T(8,128)(2,1)S(1)} collective-permute-done((bf16[256,128]{1,0:T(8,128)(2,1)S(1)}, bf16[256,128]{1,0:T(8,128)(2,1)S(1)}, u32[]{:S(2)}, u32[]{:S(2)}) %collective-permute-start.10) | collective-permute-done | bytes 65568 | tf_op jit(solution)/shard_map/ppermute | solution.py:331
  33.4 1.9 %collective-permute-start.11 = (bf16[256,128]{1,0:T(8,128)(2,1)S(1)}, bf16[256,128]{1,0:T(8,128)(2,1)S(1)}, u32[]{:S(2)}, u32[]{:S(2)}) collective-permute-start(bf16[256,128]{1,0:T(8,128)(2,1)S(1)} %shard_map.75.m0), channel_id=1, source_target_pairs={{0,2},{2,0},{4,6},{6,4},{1,3},{3,1},{5,7},{7,5},{8,10},{10,8},{12,... | collective-permute-start | bytes 196616 | tf_op jit(solution)/shard_map/ppermute | solution.py:331
  35.3 0.0 collective-permute-done.q_recv
  35.3 1.3 %collective-permute-start.12 = (bf16[256,128]{1,0:T(8,128)(2,1)S(1)}, bf16[256,128]{1,0:T(8,128)(2,1)S(1)}, u32[]{:S(2)}, u32[]{:S(2)}) collective-permute-start(bf16[256,128]{1,0:T(8,128)(2,1)S(1)} %shard_map.75.m0), channel_id=1, source_target_pairs={{0,4},{2,6},{4,0},{6,2},{1,5},{3,7},{5,1},{7,3},{8,12},{10,14},{12... | collective-permute-start | bytes 196616 | tf_op jit(solution)/shard_map/ppermute | solution.py:331
  36.6 0.5 shard_map.65.sig
  37.2 2.9 %shard_map.67 = (f32[2,256,2048]{2,1,0:T(8,128)S(1)}, f32[2,256,1024]{2,1,0:T(8,128)S(1)}) custom-call(bf16[256,1024]{1,0:T(8,128)(2,1)S(1)} %get-tuple-element.28.q_keep, bf16[256,2048]{1,0:T(8,128)(2,1)S(1)} %collective-permute-done.q_recv, bf16[512,512]{1,0:T(8,128)(2,1)S(1)} %get-tuple-element.30.kv), custom_call_target="tpu_custom_call" | custom-call | flops 1073741824 | bytes 4194304 | tf_op jit(solution)/shard_map/pallas_call | solution.py:32
  40.0 0.0 collective-permute-done.5.kv
  40.0 1.8 %collective-permute-start.13 = (bf16[256,128]{1,0:T(8,128)(2,1)S(1)}, bf16[256,128]{1,0:T(8,128)(2,1)S(1)}, u32[]{:S(2)}, u32[]{:S(2)}) collective-permute-start(bf16[256,128]{1,0:T(8,128)(2,1)S(1)} %shard_map.75.m0), channel_id=1, source_target_pairs={{0,6},{2,4},{4,2},{6,0},{1,7},{3,5},{5,3},{7,1},{8,14},{10,12},{12... | collective-permute-start | bytes 196616 | tf_op jit(solution)/shard_map/ppermute | solution.py:331
  41.9 3.0 %shard_map.68 = (f32[2,256,2048]{2,1,0:T(8,128)S(1)}, f32[2,256,1024]{2,1,0:T(8,128)S(1)}) custom-call(bf16[256,1024]{1,0:T(8,128)(2,1)S(1)} %get-tuple-element.28.q_keep, bf16[256,2048]{1,0:T(8,128)(2,1)S(1)} %collective-permute-done.q_recv, bf16[512,512]{1,0:T(8,128)(2,1)S(1)} %collective-permute-done.5.kv, ...), custom_call_target="tpu_custom_call", output_to_operand_aliasing={{0}: (3, {}), {1}: (4, {})} | custom-call | flops 1073741824 | bytes 4194304 | tf_op jit(solution)/shard_map/pallas_call | solution.py:32
  44.9 0.0 collective-permute-done.4.kv
  44.9 0.0 copy-start.1
  44.9 3.0 %shard_map.69 = (f32[2,256,2048]{2,1,0:T(8,128)S(1)}, f32[2,256,1024]{2,1,0:T(8,128)S(1)}) custom-call(bf16[256,1024]{1,0:T(8,128)(2,1)S(1)} %get-tuple-element.28.q_keep, bf16[256,2048]{1,0:T(8,128)(2,1)S(1)} %collective-permute-done.q_recv, bf16[512,512]{1,0:T(8,128)(2,1)S(1)} %collective-permute-done.4.kv, ...), custom_call_target="tpu_custom_call", output_to_operand_aliasing={{0}: (3, {}), {1}: (4, {})} | custom-call | flops 1073741824 | bytes 4194304 | tf_op jit(solution)/shard_map/pallas_call | solution.py:32
  48.0 0.0 collective-permute-done.3.kv
  48.0 0.0 copy-done.1
  48.0 0.0 copy-start
  48.0 0.0 slice-start
  48.0 3.7 %shard_map.70.dot = f32[2,256,1024]{2,1,0:T(8,128)S(1)} custom-call(bf16[256,1024]{1,0:T(8,128)(2,1)S(1)} %get-tuple-element.28.q_keep, bf16[256,2048]{1,0:T(8,128)(2,1)S(1)} %collective-permute-done.q_recv, bf16[512,512]{1,0:T(8,128)(2,1)S(1)} %collective-permute-done.3.kv, f32[2,256,2048]{2,1,0:T(8,128)S(1)} %get-tuple-element.35.ext, ...), custom_call_target="tpu_custom_call" | custom-call | flops 1073741824 | bytes 4194304 | tf_op jit(solution)/shard_map/pallas_call | solution.py:32
  51.7 0.0 collective-permute-done.11.m1
  51.7 0.0 collective-permute-done.12.m2
  51.8 0.0 collective-permute-done.13.m3
  51.8 0.0 copy-done
  51.8 0.0 slice-start.1
  51.8 0.4 shard_map.80
  52.2 0.1 collective-permute-start.15
  52.3 0.4 shard_map.77
  52.7 0.6 collective-permute-start.14
  53.3 0.0 slice-done
  53.3 0.7 %slice-done.1 = s8[4194304]{0:T(1024)(128)(4,1)S(1)} async-done(((s8[8388608]{0:T(1024)(128)(4,1)}), s8[4194304]{0:T(1024)(128)(4,1)S(1)}, s32[]{:S(2)}) %slice-start.1) | async-done | bytes 4194328
  54.0 1.6 %shard_map.79.begun = f32[256,2048]{1,0:T(8,128)S(1)} custom-call(bf16[2,256,1024]{2,1,0:T(8,128)(2,1)S(1)} %shard_map.65.sig, f32[2,256,1024]{2,1,0:T(8,128)S(1)} %shard_map.70.dot, bf16[256,128]{1,0:T(8,128)(2,1)S(1)} %shard_map.75.m0, bf16[256,128]{1,0:T(8,128)(2,1)S(1)} %collective-permute-done.11.m1, ...), custom_call_target="tpu_custom_call", output_to_operand_aliasing={{}: (8, {})} | custom-call | flops 1073741824 | bytes 8388608 | tf_op jit(solution)/shard_map/pallas_call | solution.py:32
  55.6 0.0 collective-permute-done.15.x
  55.6 0.8 %shard_map.81.done = bf16[128,2048]{1,0:T(8,128)(2,1)S(1)} custom-call(bf16[128,1024]{1,0:T(8,128)(2,1)S(1)} %collective-permute-done.15.x, f32[256,2048]{1,0:T(8,128)S(1)} %shard_map.79.begun, bf16[2048,2048]{1,0:T(8,128)(2,1)S(1)} %bitcast.3), custom_call_target="tpu_custom_call" | custom-call | flops 536870912 | bytes 4194304 | tf_op jit(solution)/shard_map/pallas_call | solution.py:32
  56.4 0.0 collective-permute-done.14.x
  56.4 1.5 %project_b.1 = bf16[256,2048]{1,0:T(8,128)(2,1)} custom-call(bf16[128,1024]{1,0:T(8,128)(2,1)S(1)} %collective-permute-done.14.x, f32[256,2048]{1,0:T(8,128)S(1)} %shard_map.79.begun, bf16[2048,2048]{1,0:T(8,128)(2,1)S(1)} %bitcast.3, bf16[128,2048]{1,0:T(8,128)(2,1)S(1)} %shard_map.81.done), custom_call_target="tpu_custom_call" | custom-call | flops 536870912 | bytes 4194304 | tf_op jit(solution)/shard_map/project_b/pallas_call | solution.py:315
  (9 shorter events, 0.2 us)
Async XLA Ops:
  0.0 35.3 %collective-permute-start = (bf16[256,2048]{1,0:T(8,128)(2,1)}, bf16[256,2048]{1,0:T(8,128)(2,1)S(1)}, u32[]{:S(2)}, u32[]{:S(2)}) collective-permute-start(bf16[256,2048]{1,0:T(8,128)(2,1)} %q.1), channel_id=1, source_target_pairs={{0,1},{1,0},{2,3},{3,2},{4,5},{5,4},{6,7},{7,6},{8,9},{9,8},{10,11... | collective-permute-start | bytes 3145736 | tf_op jit(solution)/shard_map/ppermute | solution.py:331
  0.0 3.2 %collective-permute-start.1 = (bf16[256,512]{1,0:T(8,128)(2,1)}, bf16[256,512]{1,0:T(8,128)(2,1)S(1)}, u32[]{:S(2)}, u32[]{:S(2)}) collective-permute-start(bf16[256,512]{1,0:T(8,128)(2,1)} %k.1), channel_id=1, source_target_pairs={{0,1},{1,0},{2,3},{3,2},{4,5},{5,4},{6,7},{7,6},{8,9},{9,8},{10,11... | collective-permute-start | bytes 786440 | tf_op jit(solution)/shard_map/ppermute | solution.py:331
  0.5 3.1 %collective-permute-start.2 = (bf16[256,512]{1,0:T(8,128)(2,1)}, bf16[256,512]{1,0:T(8,128)(2,1)S(1)}, u32[]{:S(2)}, u32[]{:S(2)}) collective-permute-start(bf16[256,512]{1,0:T(8,128)(2,1)} %v.1), channel_id=1, source_target_pairs={{0,1},{1,0},{2,3},{3,2},{4,5},{5,4},{6,7},{7,6},{8,9},{9,8},{10,11... | collective-permute-start | bytes 786440 | tf_op jit(solution)/shard_map/ppermute | solution.py:331
  4.1 36.0 %collective-permute-start.5 = (bf16[512,512]{1,0:T(8,128)(2,1)S(1)}, bf16[512,512]{1,0:T(8,128)(2,1)S(1)}, u32[]{:S(2)}, u32[]{:S(2)}) collective-permute-start(bf16[512,512]{1,0:T(8,128)(2,1)S(1)} %get-tuple-element.30.kv), channel_id=1, source_target_pairs={{0,2},{2,4},{4,6},{6,0},{1,3},{3,5},{5,7},{7,1},{8,10},{10,12},{12... | collective-permute-start | bytes 1572872 | tf_op jit(solution)/shard_map/ppermute | solution.py:331
  4.4 4.3 %collective-permute-start.6 = (bf16[256,128]{1,0:T(8,128)(2,1)S(1)}, bf16[256,128]{1,0:T(8,128)(2,1)S(1)}, u32[]{:S(2)}, u32[]{:S(2)}) collective-permute-start(bf16[256,128]{1,0:T(8,128)(2,1)S(1)} %get-tuple-element.38), channel_id=1, source_target_pairs={{0,8},{8,0},{16,24},{24,16},{32,40},{40,32},{48,56},{56,48},{1,9},... | collective-permute-start | bytes 196616 | tf_op jit(solution)/shard_map/ppermute | solution.py:331
  6.3 38.6 %collective-permute-start.4 = (bf16[512,512]{1,0:T(8,128)(2,1)S(1)}, bf16[512,512]{1,0:T(8,128)(2,1)S(1)}, u32[]{:S(2)}, u32[]{:S(2)}) collective-permute-start(bf16[512,512]{1,0:T(8,128)(2,1)S(1)} %get-tuple-element.30.kv), channel_id=1, source_target_pairs={{0,6},{2,0},{4,2},{6,4},{1,7},{3,1},{5,3},{7,5},{8,14},{10,8},{12,... | collective-permute-start | bytes 1572872 | tf_op jit(solution)/shard_map/ppermute | solution.py:331
  8.7 5.9 %collective-permute-start.7 = (bf16[256,128]{1,0:T(8,128)(2,1)S(1)}, bf16[256,128]{1,0:T(8,128)(2,1)S(1)}, u32[]{:S(2)}, u32[]{:S(2)}) collective-permute-start(bf16[256,128]{1,0:T(8,128)(2,1)S(1)} %get-tuple-element.41), channel_id=1, source_target_pairs={{0,16},{8,24},{16,0},{24,8},{32,48},{40,56},{48,32},{56,40},{1,17}... | collective-permute-start | bytes 196616 | tf_op jit(solution)/shard_map/ppermute | solution.py:331
  12.0 36.0 %collective-permute-start.3 = (bf16[512,512]{1,0:T(8,128)(2,1)S(1)}, bf16[512,512]{1,0:T(8,128)(2,1)S(1)}, u32[]{:S(2)}, u32[]{:S(2)}) collective-permute-start(bf16[512,512]{1,0:T(8,128)(2,1)S(1)} %get-tuple-element.30.kv), channel_id=1, source_target_pairs={{0,4},{2,6},{4,0},{6,2},{1,5},{3,7},{5,1},{7,3},{8,12},{10,14},{12... | collective-permute-start | bytes 1572872 | tf_op jit(solution)/shard_map/ppermute | solution.py:331
  14.7 8.7 %collective-permute-start.8 = (bf16[256,128]{1,0:T(8,128)(2,1)S(1)}, bf16[256,128]{1,0:T(8,128)(2,1)S(1)}, u32[]{:S(2)}, u32[]{:S(2)}) collective-permute-start(bf16[256,128]{1,0:T(8,128)(2,1)S(1)} %get-tuple-element.44), channel_id=1, source_target_pairs={{0,56},{8,48},{16,40},{24,32},{32,24},{40,16},{48,8},{56,0},{1,57}... | collective-permute-start | bytes 196616 | tf_op jit(solution)/shard_map/ppermute | solution.py:331
  23.4 4.4 %collective-permute-start.9 = (bf16[256,128]{1,0:T(8,128)(2,1)S(1)}, bf16[256,128]{1,0:T(8,128)(2,1)S(1)}, u32[]{:S(2)}, u32[]{:S(2)}) collective-permute-start(bf16[256,128]{1,0:T(8,128)(2,1)S(1)} %get-tuple-element.47), channel_id=1, source_target_pairs={{0,64},{64,0},{128,192},{192,128},{1,65},{65,1},{129,193},{193,129... | collective-permute-start | bytes 196616 | tf_op jit(solution)/shard_map/ppermute | solution.py:331
  27.8 5.6 %collective-permute-start.10 = (bf16[256,128]{1,0:T(8,128)(2,1)S(1)}, bf16[256,128]{1,0:T(8,128)(2,1)S(1)}, u32[]{:S(2)}, u32[]{:S(2)}) collective-permute-start(bf16[256,128]{1,0:T(8,128)(2,1)S(1)} %get-tuple-element.50), channel_id=1, source_target_pairs={{0,192},{64,128},{128,64},{192,0},{1,193},{65,129},{129,65},{193,1... | collective-permute-start | bytes 196616 | tf_op jit(solution)/shard_map/ppermute | solution.py:331
  33.4 18.3 %collective-permute-start.11 = (bf16[256,128]{1,0:T(8,128)(2,1)S(1)}, bf16[256,128]{1,0:T(8,128)(2,1)S(1)}, u32[]{:S(2)}, u32[]{:S(2)}) collective-permute-start(bf16[256,128]{1,0:T(8,128)(2,1)S(1)} %shard_map.75.m0), channel_id=1, source_target_pairs={{0,2},{2,0},{4,6},{6,4},{1,3},{3,1},{5,7},{7,5},{8,10},{10,8},{12,... | collective-permute-start | bytes 196616 | tf_op jit(solution)/shard_map/ppermute | solution.py:331
  35.3 16.4 %collective-permute-start.12 = (bf16[256,128]{1,0:T(8,128)(2,1)S(1)}, bf16[256,128]{1,0:T(8,128)(2,1)S(1)}, u32[]{:S(2)}, u32[]{:S(2)}) collective-permute-start(bf16[256,128]{1,0:T(8,128)(2,1)S(1)} %shard_map.75.m0), channel_id=1, source_target_pairs={{0,4},{2,6},{4,0},{6,2},{1,5},{3,7},{5,1},{7,3},{8,12},{10,14},{12... | collective-permute-start | bytes 196616 | tf_op jit(solution)/shard_map/ppermute | solution.py:331
  40.0 11.7 %collective-permute-start.13 = (bf16[256,128]{1,0:T(8,128)(2,1)S(1)}, bf16[256,128]{1,0:T(8,128)(2,1)S(1)}, u32[]{:S(2)}, u32[]{:S(2)}) collective-permute-start(bf16[256,128]{1,0:T(8,128)(2,1)S(1)} %shard_map.75.m0), channel_id=1, source_target_pairs={{0,6},{2,4},{4,2},{6,0},{1,7},{3,5},{5,3},{7,1},{8,14},{10,12},{12... | collective-permute-start | bytes 196616 | tf_op jit(solution)/shard_map/ppermute | solution.py:331
  44.9 3.1 %copy-start.1 = (f32[2048]{0:T(1024)S(1)}, f32[2048]{0:T(1024)}, u32[]{:S(2)}) copy-start(f32[2048]{0:T(1024)} %param.10) | copy-start | bytes 24580
  48.0 3.8 %copy-start = (f32[2048]{0:T(1024)S(1)}, f32[2048]{0:T(1024)}, u32[]{:S(2)}) copy-start(f32[2048]{0:T(1024)} %param.9) | copy-start | bytes 24580
  48.0 5.3 %slice-start = ((s8[8388608]{0:T(1024)(128)(4,1)}), s8[4194304]{0:T(1024)(128)(4,1)S(1)}, s32[]{:S(2)}) async-start(s8[8388608]{0:T(1024)(128)(4,1)} %bitcast.2), calls=%async_computation | async-start | bytes 8388608
  51.8 2.2 %slice-start.1 = ((s8[8388608]{0:T(1024)(128)(4,1)}), s8[4194304]{0:T(1024)(128)(4,1)S(1)}, s32[]{:S(2)}) async-start(s8[8388608]{0:T(1024)(128)(4,1)} %bitcast.2), calls=%async_computation.1 | async-start | bytes 8388608
  52.2 3.4 %collective-permute-start.15 = (bf16[128,1024]{1,0:T(8,128)(2,1)S(1)}, bf16[128,1024]{1,0:T(8,128)(2,1)S(1)}, u32[]{:S(2)}, u32[]{:S(2)}) collective-permute-start(bf16[128,1024]{1,0:T(8,128)(2,1)S(1)} %shard_map.80), channel_id=1, source_target_pairs={{0,1},{1,0},{2,3},{3,2},{4,5},{5,4},{6,7},{7,6},{8,9},{9,8},{10,11... | collective-permute-start | bytes 786440 | tf_op jit(solution)/shard_map/ppermute | solution.py:331
  52.7 3.6 %collective-permute-start.14 = (bf16[128,1024]{1,0:T(8,128)(2,1)S(1)}, bf16[128,1024]{1,0:T(8,128)(2,1)S(1)}, u32[]{:S(2)}, u32[]{:S(2)}) collective-permute-start(bf16[128,1024]{1,0:T(8,128)(2,1)S(1)} %shard_map.77), channel_id=1, source_target_pairs={{0,1},{1,0},{2,3},{3,2},{4,5},{5,4},{6,7},{7,6},{8,9},{9,8},{10,11... | collective-permute-start | bytes 786440 | tf_op jit(solution)/shard_map/ppermute | solution.py:331
